TPU v7x, 256 devices: a whole 4x4x8 slice. The times are simulated.
256 devices in a mesh: segment: 32 (over y_hi, z, core), dp: 8 (over y_lo, x).
Axes of the slice: x: 4, y: 4 (y_hi: 2, y_lo: 2; y = y_hi * 2 + y_lo), z: 8, core: 2. Of those that a mesh axis runs over, the one named last changes fastest.
Arguments:
- incoming: bfloat16 [32, 4, 32, 16, 16, 128], P('segment', None, 'dp'), may hold values from -6 to 6
- fresh: bfloat16 [3, 4, 32, 16, 16, 128], P(None, None, 'dp'), may hold values from -6 to 6
- weights: bfloat16 [32, 2, 1152, 128], P('segment'), may hold values from -0.1875 to 0.1875
- momentum: float32 [32, 2, 1152, 128], P('segment', None, 'dp'), may hold values from -6 to 6
Outputs:
- outgoing: bfloat16 [32, 4, 32, 16, 16, 128], P('segment', None, 'dp')
- new_momentum: float32 [32, 2, 1152, 128], P('segment', None, 'dp')
All inputs are finite; a program needn't handle non-finite values.
Results may differ from a plain program's by a relative error of at most 0.023.
Values may be sent and summed in bfloat16 or wider, within the bound.
No kernel may reach another device: no remote copies, remote signals or barrier semaphores. Data moves between devices by JAX's collectives and lax.ppermute only.
A program may use at most 64 MiB of HBM per device.

v0:
```python
import jax
import jax.numpy as jnp
from jax import lax
from jax.sharding import PartitionSpec as P

FRAMES = 4
TICKS = 4


def passed_along(value, axis, steps):
    count = lax.axis_size(axis)
    first, last = (max(0, -steps), min(count, count - steps))
    return lax.ppermute(value, axis, [(source, source + steps) for source in range(first, last)])


def patches(field):
    hgt, wid = (field.shape[1], field.shape[2])
    padded = jnp.pad(field, ((0, 0), (1, 1), (1, 1), (0, 0)))
    return jnp.concatenate(
        [padded[:, a : a + hgt, b : b + wid, :] for a in range(3) for b in range(3)], axis=-1
    )


def convolve(field, filters):
    cols = patches(field).reshape(-1, filters.shape[0])
    out = jnp.dot(cols, filters, preferred_element_type=jnp.float32)
    return out.reshape(field.shape[:3] + (filters.shape[1],))


def flipped(filters):
    chans = filters.shape[1]
    four = filters.reshape(3, 3, chans, chans)
    return jnp.transpose(four[::-1, ::-1], (0, 1, 3, 2)).reshape(9 * chans, chans)


def filter_grad(field, slope):
    cols = patches(field).reshape(-1, 9 * field.shape[3])
    flat = slope.reshape(-1, slope.shape[3])
    return lax.dot_general(cols, flat, (((0,), (0,)), ((), ())), preferred_element_type=jnp.float32)


def silu_slope(value):
    sig = jax.nn.sigmoid(value)
    return sig * (1.0 + value * (1.0 - sig))


def branch_g(state, w_g, flip_g):
    y_one, y_two, dy_one, dy_two = (state[0], state[1], state[2], state[3])
    act_g = convolve(y_one, w_g)
    x_two = (y_two.astype(jnp.float32) - jax.nn.silu(act_g)).astype(jnp.bfloat16)
    z_g = (dy_two.astype(jnp.float32) * silu_slope(act_g)).astype(jnp.bfloat16)
    dx_one = (dy_one.astype(jnp.float32) + convolve(z_g, flip_g)).astype(jnp.bfloat16)
    return (x_two, dx_one, filter_grad(y_one, z_g))


def branch_f(state, x_two, dx_one, w_f, flip_f):
    y_one, dy_two = (state[0], state[3])
    act_f = convolve(x_two, w_f)
    x_one = (y_one.astype(jnp.float32) - jax.nn.silu(act_f)).astype(jnp.bfloat16)
    z_f = (dx_one.astype(jnp.float32) * silu_slope(act_f)).astype(jnp.bfloat16)
    dx_two = (dy_two.astype(jnp.float32) + convolve(z_f, flip_f)).astype(jnp.bfloat16)
    return (x_one, dx_two, filter_grad(x_two, z_f))


def shards(incoming, fresh, weights, momentum):
    w_f, w_g = (weights[0, 0], weights[0, 1])
    flip_f, flip_g = (flipped(w_f), flipped(w_g))
    is_last = lax.axis_index("segment") == lax.axis_size("segment") - 1
    replicas = lax.axis_size("dp")
    state = incoming[0]
    total = jnp.zeros(weights.shape[1:], jnp.float32)
    outs = state
    for tick in range(TICKS):
        x_two, dx_one, grad_g = branch_g(state, w_g, flip_g)
        x_one, dx_two, grad_f = branch_f(state, x_two, dx_one, w_f, flip_f)
        outs = jnp.stack([x_one, x_two, dx_one, dx_two])
        if tick < TICKS - 1:
            moved = passed_along(outs, "segment", -1)
            state = jnp.where(is_last, fresh[tick], moved)
        grads = jnp.stack([grad_f, grad_g])
        total = total + grads
    shares = lax.psum_scatter(
        total.astype(jnp.bfloat16), "dp", scatter_dimension=1, tiled=True
    ).astype(jnp.float32)
    new_momentum = 0.9 * momentum[0] + shares / (TICKS * FRAMES * replicas)
    return (outs[None], new_momentum[None])


def solution(mesh):
    return jax.shard_map(
        shards,
        mesh=mesh,
        in_specs=(
            P("segment", None, "dp", None, None, None),
            P(None, None, "dp", None, None, None),
            P("segment", None, None, None),
            P("segment", None, "dp", None),
        ),
        out_specs=(P("segment", None, "dp", None, None, None), P("segment", None, "dp", None)),
        check_vma=False,
    )
```

profile of v0, /device:TPU:16, one launch (start us, length us, event | category | flops | bytes accessed | tf_op | source)
XLA Modules:
  0.0 150.2 jit_solution(2102000327594900233)
XLA Ops:
  7.2 1.0 slice_bitcast_fusion.12
  8.2 1.1 fusion.55
  11.1 1.0 fusion.12
  15.3 0.9 fusion.39
  18.1 7.2 %collective-permute-start = (bf16[4,4,16,16,128]{4,3,2,1,0:T(8,128)(2,1)S(1)}, bf16[4,4,16,16,128]{4,3,2,1,0:T(8,128)(2,1)S(1)}, u32[]{:S(2)}, u32[]{:S(2)}) collective-permute-start(bf16[4,4,16,16,128]{4,3,2,1,0:T(8,128)(2,1)S(1)} %pad_maximum_fusion), channel_id=1, source_target_pairs={{8,0},{16,8},{24,16},{32,24},{40,32},{48,40},{56,48},{64,56},{72,6... | collective-permute-start | bytes 3145736 | tf_op jit(solution)/shard_map/ppermute | solution.py:13
  25.2 2.6 %convolution_bitcast_fusion.6 = f32[1,1152,128]{2,1,0:T(8,128)S(1)} fusion(bf16[4,16,16,1152]{3,2,1,0:T(8,128)(2,1)} %copy-done.7, bf16[4,16,16,128]{3,2,1,0:T(8,128)(2,1)S(1)} %get-tuple-element.17), kind=kOutput, calls=%fused_computation.6 | convolution fusion | flops 301989888 | bytes 3211264 | tf_op jit(solution)/shard_map/dot_general | solution.py:39
  28.7 8.6 %collective-permute-done = bf16[4,4,16,16,128]{4,3,2,1,0:T(8,128)(2,1)S(1)} collective-permute-done((bf16[4,4,16,16,128]{4,3,2,1,0:T(8,128)(2,1)S(1)}, bf16[4,4,16,16,128]{4,3,2,1,0:T(8,128)(2,1)S(1)}, u32[]{:S(2)}, u32[]{:S(2)}) %collective-permute-start) | collective-permute-done | bytes 1048608 | tf_op jit(solution)/shard_map/ppermute | solution.py:13
  38.4 1.0 fusion.13
  41.9 1.0 fusion.40
  44.8 7.6 %collective-permute-start.1 = (bf16[4,4,16,16,128]{4,3,2,1,0:T(8,128)(2,1)S(1)}, bf16[4,4,16,16,128]{4,3,2,1,0:T(8,128)(2,1)S(1)}, u32[]{:S(2)}, u32[]{:S(2)}) collective-permute-start(bf16[4,4,16,16,128]{4,3,2,1,0:T(8,128)(2,1)S(1)} %pad_maximum_fusion.1), channel_id=1, source_target_pairs={{8,0},{16,8},{24,16},{32,24},{40,32},{48,40},{56,48},{64,56},{72,6... | collective-permute-start | bytes 3145736 | tf_op jit(solution)/shard_map/ppermute | solution.py:13
  53.3 0.8 convolution_bitcast_fusion.5
  54.1 10.4 %collective-permute-done.1 = bf16[4,4,16,16,128]{4,3,2,1,0:T(8,128)(2,1)S(1)} collective-permute-done((bf16[4,4,16,16,128]{4,3,2,1,0:T(8,128)(2,1)S(1)}, bf16[4,4,16,16,128]{4,3,2,1,0:T(8,128)(2,1)S(1)}, u32[]{:S(2)}, u32[]{:S(2)}) %collective-permute-start.1) | collective-permute-done | bytes 1048608 | tf_op jit(solution)/shard_map/ppermute | solution.py:13
  65.5 1.0 fusion.14
  69.0 1.0 fusion.41
  71.8 7.7 %collective-permute-start.2 = (bf16[4,4,16,16,128]{4,3,2,1,0:T(8,128)(2,1)S(1)}, bf16[4,4,16,16,128]{4,3,2,1,0:T(8,128)(2,1)S(1)}, u32[]{:S(2)}, u32[]{:S(2)}) collective-permute-start(bf16[4,4,16,16,128]{4,3,2,1,0:T(8,128)(2,1)S(1)} %pad_maximum_fusion.2), channel_id=1, source_target_pairs={{8,0},{16,8},{24,16},{32,24},{40,32},{48,40},{56,48},{64,56},{72,6... | collective-permute-start | bytes 3145736 | tf_op jit(solution)/shard_map/ppermute | solution.py:13
  81.2 10.4 %collective-permute-done.2 = bf16[4,4,16,16,128]{4,3,2,1,0:T(8,128)(2,1)S(1)} collective-permute-done((bf16[4,4,16,16,128]{4,3,2,1,0:T(8,128)(2,1)S(1)}, bf16[4,4,16,16,128]{4,3,2,1,0:T(8,128)(2,1)S(1)}, u32[]{:S(2)}, u32[]{:S(2)}) %collective-permute-start.2) | collective-permute-done | bytes 1048608 | tf_op jit(solution)/shard_map/ppermute | solution.py:13
  92.6 1.0 fusion.15
  96.9 1.7 %fusion.42 = (bf16[1,4,16,16,128]{4,3,2,1,0:T(8,128)(2,1)S(1)}, bf16[4,16,16,128]{3,2,1,0:T(8,128)(2,1)S(1)}, bf16[1,4,16,16,128]{4,3,2,1,0:T(8,128)(2,1)}) fusion(bf16[4,4,16,16,128]{4,3,2,1,0:T(8,128)(2,1)S(1)} %bitcast_select_fusion.2, f32[4,16,16,128]{3,2,1,0:T(8,128)S(1)} %fusion.66, ...), kind=kOutput, calls=%fused_computation.377 | convolution fusion | flops 304218112 | bytes 4489216 | tf_op jit(solution)/shard_map/dot_general | solution.py:26
  100.1 1.1 fusion.7
  105.2 0.8 constant_dynamic-update-slice_fusion.137
  107.6 2.5 %fusion.8 = bf16[1,4,16,16,128]{4,3,2,1,0:T(8,128)(2,1)S(1)} fusion(bf16[4,16,16,1152]{3,2,1,0:T(8,128)(2,1)} %constant_dynamic-update-slice_fusion.135, bf16[1152,128,1,1]{1,0,3,2:T(8,128)(2,1)S(1)} %bitcast.297, bf16[4,4,16,16,128]{4,3,2,1,0:T(8,128)(2,1)S(1)} %bitcast_select_fusion.2), kind=kOutput, calls=%fused_computation.22 | convolution fusion | flops 302383104 | bytes 3178496 | tf_op jit(solution)/shard_map/dot_general | solution.py:26
  110.1 1.1 maximum_bitcast_fusion
  111.2 30.5 %reduce-scatter.2.cloned.1.call-done = bf16[2,144,128]{2,1,0:T(8,128)(2,1)} async-done(((bf16[2,1152,128]{2,1,0:T(8,128)(2,1)}), bf16[2,144,128]{2,1,0:T(8,128)(2,1)}) %reduce-scatter.2.cloned.1.call-update) | async-done | bytes 73744 | tf_op jit(solution)/shard_map/reduce_scatter | solution.py:82
  141.8 1.6 %fusion.43 = f32[1,2,144,128]{3,2,1,0:T(8,128)} fusion(bf16[2,144,128]{2,1,0:T(8,128)(2,1)} %reduce-scatter.2.cloned.1.call-done, f32[1,2,144,128]{3,2,1,0:T(8,128)S(1)} %copy-done.6), kind=kLoop, calls=%fused_computation.379 | loop fusion | flops 147456 | bytes 368640 | tf_op jit(solution)/shard_map/broadcast_in_dim | solution.py:86
  (190 shorter events, 31.4 us)
Async XLA Ops:
  7.2 134.6 %reduce-scatter.2.cloned.1.call-start = ((), (), s32[]{:S(2)}) async-start(), calls=%async_computation.1 | async-start | bytes 663552 | tf_op jit(solution)/shard_map/reduce_scatter | solution.py:82
  9.3 1.3 copy-start.4
  9.5 7.6 %copy-start.2 = (bf16[3,3,128,128]{3,2,1,0:T(8,128)(2,1)}, bf16[3,3,128,128]{3,2,1,0:T(8,128)(2,1)S(1)}, u32[]{:S(2)}) copy-start(bf16[3,3,128,128]{3,2,1,0:T(8,128)(2,1)S(1)} %copy.7) | copy-start | bytes 884740
  9.8 1.3 copy-start.1
  11.1 2.4 %copy-start.7 = (bf16[4,16,16,1152]{3,2,1,0:T(8,128)(2,1)}, bf16[4,16,16,1152]{3,2,1,0:T(8,128)(2,1)S(1)}, u32[]{:S(2)}) copy-start(bf16[4,16,16,1152]{3,2,1,0:T(8,128)(2,1)S(1)} %constant_dynamic-update-slice_fusion) | copy-start | bytes 7077892
  13.8 1.4 copy-start.8
  18.1 19.3 %collective-permute-start = (bf16[4,4,16,16,128]{4,3,2,1,0:T(8,128)(2,1)S(1)}, bf16[4,4,16,16,128]{4,3,2,1,0:T(8,128)(2,1)S(1)}, u32[]{:S(2)}, u32[]{:S(2)}) collective-permute-start(bf16[4,4,16,16,128]{4,3,2,1,0:T(8,128)(2,1)S(1)} %pad_maximum_fusion), channel_id=1, source_target_pairs={{8,0},{16,8},{24,16},{32,24},{40,32},{48,40},{56,48},{64,56},{72,6... | collective-permute-start | bytes 3145736 | tf_op jit(solution)/shard_map/ppermute | solution.py:13
  25.2 2.6 %copy-start.9 = (bf16[4,16,16,1152]{3,2,1,0:T(8,128)(2,1)S(1)}, bf16[4,16,16,1152]{3,2,1,0:T(8,128)(2,1)}, u32[]{:S(2)}) copy-start(bf16[4,16,16,1152]{3,2,1,0:T(8,128)(2,1)} %copy-done.8) | copy-start | bytes 7077892
  27.9 9.5 %copy-start = (bf16[3,4,4,16,16,128]{5,4,3,2,1,0:T(8,128)(2,1)S(1)}, bf16[3,4,4,16,16,128]{5,4,3,2,1,0:T(8,128)(2,1)}, u32[]{:S(2)}) copy-start(bf16[3,4,4,16,16,128]{5,4,3,2,1,0:T(8,128)(2,1)} %param.5) | copy-start | bytes 9437188
  42.9 1.0 copy-start.3
  44.8 19.7 %collective-permute-start.1 = (bf16[4,4,16,16,128]{4,3,2,1,0:T(8,128)(2,1)S(1)}, bf16[4,4,16,16,128]{4,3,2,1,0:T(8,128)(2,1)S(1)}, u32[]{:S(2)}, u32[]{:S(2)}) collective-permute-start(bf16[4,4,16,16,128]{4,3,2,1,0:T(8,128)(2,1)S(1)} %pad_maximum_fusion.1), channel_id=1, source_target_pairs={{8,0},{16,8},{24,16},{32,24},{40,32},{48,40},{56,48},{64,56},{72,6... | collective-permute-start | bytes 3145736 | tf_op jit(solution)/shard_map/ppermute | solution.py:13
  71.8 19.7 %collective-permute-start.2 = (bf16[4,4,16,16,128]{4,3,2,1,0:T(8,128)(2,1)S(1)}, bf16[4,4,16,16,128]{4,3,2,1,0:T(8,128)(2,1)S(1)}, u32[]{:S(2)}, u32[]{:S(2)}) collective-permute-start(bf16[4,4,16,16,128]{4,3,2,1,0:T(8,128)(2,1)S(1)} %pad_maximum_fusion.2), channel_id=1, source_target_pairs={{8,0},{16,8},{24,16},{32,24},{40,32},{48,40},{56,48},{64,56},{72,6... | collective-permute-start | bytes 3145736 | tf_op jit(solution)/shard_map/ppermute | solution.py:13
  107.6 2.5 %copy-start.5 = (bf16[1,4,16,16,128]{4,3,2,1,0:T(8,128)(2,1)S(1)}, bf16[1,4,16,16,128]{4,3,2,1,0:T(8,128)(2,1)}, u32[]{:S(2)}) copy-start(bf16[1,4,16,16,128]{4,3,2,1,0:T(8,128)(2,1)} %get-tuple-element.4) | copy-start | bytes 786436
  107.6 34.2 %copy-start.6 = (f32[1,2,144,128]{3,2,1,0:T(8,128)S(1)}, f32[1,2,144,128]{3,2,1,0:T(8,128)}, u32[]{:S(2)}) copy-start(f32[1,2,144,128]{3,2,1,0:T(8,128)} %param.7) | copy-start | bytes 442372
Sparse Core Ops, SparseCore 0:
  101.4 40.3 reduce-scatter.1
where the time goes:
time: 151 us; the launch traced here: 150 us
  waiting for transfers between devices  60 us (40%)
  matrix products  24.7 us (16%)
  local copies, waits for them, and re-layouts  23.2 us (15%)
  starting transfers between devices  22.5 us (15%)
  between operations  15.2 us (10%)
  other arithmetic  4.53 us (3%)
    reduce_scatter x1, waiting for transfers between devices, shards(): lax.psum_scatter(total.astype(jnp.bfloat16), 'dp', scatter_dimension=1, t...  30.5 us
    ppermute x3, waiting for transfers between devices, passed_along(): lax.ppermute(value, axis, [(source, source + steps) for source in range(f...  29.4 us
    ppermute x3, starting transfers between devices, passed_along(): lax.ppermute(value, axis, [(source, source + steps) for source in range(f...  22.5 us
    unnamed x148, local copies, waits for them, and re-layouts  18.1 us
    dot_general x16, matrix products, convolve(): out = jnp.dot(cols, filters, preferred_element_type=jnp.float32)  16.4 us
    dot_general x8, matrix products, filter_grad(): lax.dot_general(cols, flat, (((0,), (0,)), ((), ())), preferred_element_t...  8.35 us
  transfers between devices with their start and end apart: 4, of which 4 were waited for; matrix products, arithmetic and copies ran while one was open for 11% of the time, Pallas kernels for 0%

commit v1 on v0

v1 whole, which is shorter than its diff:
```python
import functools

import jax
import jax.numpy as jnp
from jax import lax
from jax.experimental import pallas as pl
from jax.experimental.pallas import tpu as pltpu
from jax.sharding import PartitionSpec as P

TICKS = 4
TAPS = 3
CHUNKS = ((0, 2), (2, 2))
F32, BF16 = jnp.float32, jnp.bfloat16


def passed_along(value, axis):
    count = lax.axis_size(axis)
    return lax.ppermute(value, axis, [(source, source - 1) for source in range(1, count)])


def tap(w, a, b):
    chans = w.shape[1]
    first = (TAPS * a + b) * chans
    return w[first : first + chans, :]


def sides(value, wid):
    rows = value.shape[0]
    col = lax.broadcasted_iota(jnp.int32, value.shape, 0) % wid
    before = jnp.where(col == 0, 0.0, pltpu.roll(value, 1, 0))
    after = jnp.where(col == wid - 1, 0.0, pltpu.roll(value, rows - 1, 0))
    return before, after


def windows(pad, count, hgt):
    return pad[:, count : count + hgt].reshape(-1, pad.shape[-1])


def conv(pad_ref, w, wid):
    hgt, chans = pad_ref.shape[1] - 2, pad_ref.shape[-1]
    field = pad_ref[...]
    lhs = jnp.concatenate([windows(field, a, hgt) for a in range(TAPS)], axis=1)
    rhs = jnp.concatenate(
        [jnp.concatenate([tap(w, a, b) for b in range(TAPS)], axis=1) for a in range(TAPS)], axis=0
    )
    out = jnp.dot(lhs, rhs, preferred_element_type=F32)
    left, mid, right = (out[:, b * chans : (b + 1) * chans] for b in range(TAPS))
    return sides(left, wid)[0] + mid + sides(right, wid)[1]


def conv_back(pads_ref, w):
    hgt = pads_ref.shape[2] - 2
    lhs = jnp.concatenate(
        [windows(pads_ref[b], a, hgt) for a in range(TAPS) for b in range(TAPS)], axis=1
    )
    rhs = jnp.concatenate(
        [tap(w, TAPS - 1 - a, TAPS - 1 - b) for a in range(TAPS) for b in range(TAPS)], axis=1
    )
    return lax.dot_general(lhs, rhs, (((1,), (1,)), ((), ())), preferred_element_type=F32)


def grad_of(field, pads_ref):
    hgt = pads_ref.shape[2] - 2
    cols = jnp.concatenate(
        [
            windows(pads_ref[TAPS - 1 - b], TAPS - 1 - a, hgt)
            for a in range(TAPS)
            for b in range(TAPS)
        ],
        axis=1,
    )
    return lax.dot_general(field, cols, (((0,), (0,)), ((), ())), preferred_element_type=F32)


def put_field(pad_ref, value):
    frames, tall, wid, chans = pad_ref.shape
    pad_ref[:, 1 : tall - 1] = value.reshape(frames, tall - 2, wid, chans)


def put_slope(pads_ref, slope, wid):
    before, after = sides(slope, wid)
    put_field(pads_ref.at[0], before.astype(BF16))
    put_field(pads_ref.at[1], slope.astype(BF16))
    put_field(pads_ref.at[2], after.astype(BF16))


def clear_edges(pads_ref):
    tall = pads_ref.shape[-3]
    lead = pads_ref.shape[:-3]
    zero = jnp.zeros(lead + (1,) + pads_ref.shape[-2:], BF16)
    at = (slice(None),) * len(lead)
    pads_ref[at + (slice(0, 1),)] = zero
    pads_ref[at + (slice(tall - 1, tall),)] = zero


def slopes(act):
    sig = jax.nn.sigmoid(act)
    return act * sig, sig * (1.0 + act * (1.0 - sig))


def block_kernel(cfg, *refs):
    first, frames, begin, tick, last = cfg
    refs = list(refs)
    st_ref, w_ref = refs[:2]
    del refs[:2]
    fresh_ref = None if tick == 0 else refs.pop(0)
    acc_ref = None if begin else refs.pop(0)
    out_ref, sum_ref, xpad, xpad2, zpads, zpads2 = refs[:6]
    hgt, wid, chans = out_ref.shape[2:]
    if tick:
        fbuf, sem = refs[6:]
        is_last = lax.axis_index("segment") == lax.axis_size("segment") - 1

        @pl.when(is_last)
        def _():
            copy = pltpu.make_async_copy(
                fresh_ref.at[tick - 1, :, pl.ds(first, frames)], fbuf, sem
            )
            copy.start()
            copy.wait()

        def part(i):
            return jnp.where(is_last, fbuf[i], st_ref[i]).reshape(-1, chans)
    else:

        def part(i):
            return st_ref[0, i, first : first + frames].reshape(-1, chans)

    clear_edges(xpad)
    clear_edges(xpad2)
    clear_edges(zpads)
    clear_edges(zpads2)
    w_f, w_g = w_ref[0, 0], w_ref[0, 1]

    y_one = part(0)
    put_field(xpad, y_one)
    act, slope = slopes(conv(xpad, w_g, wid))
    x_two = (part(1).astype(F32) - act).astype(BF16)
    put_field(xpad2, x_two)
    put_slope(zpads, part(3).astype(F32) * slope, wid)
    out_ref[1] = x_two.reshape(frames, hgt, wid, chans)
    dx_one = (part(2).astype(F32) + conv_back(zpads, w_g)).astype(BF16)
    out_ref[2] = dx_one.reshape(frames, hgt, wid, chans)

    act, slope = slopes(conv(xpad2, w_f, wid))
    out_ref[0] = (y_one.astype(F32) - act).astype(BF16).reshape(frames, hgt, wid, chans)
    put_slope(zpads2, dx_one.astype(F32) * slope, wid)
    dx_two = part(3).astype(F32) + conv_back(zpads2, w_f)
    out_ref[3] = dx_two.astype(BF16).reshape(frames, hgt, wid, chans)

    grad_g = grad_of(y_one, zpads)
    grad_f = grad_of(x_two, zpads2)
    if not begin:
        grad_f = grad_f + acc_ref[0]
        grad_g = grad_g + acc_ref[1]
    if not last:
        sum_ref[0] = grad_f
        sum_ref[1] = grad_g
    else:
        for b in range(TAPS * TAPS):
            sum_ref[0, pl.ds(b * chans, chans)] = grad_f[:, b * chans : (b + 1) * chans]
            sum_ref[1, pl.ds(b * chans, chans)] = grad_g[:, b * chans : (b + 1) * chans]


def block(state, weights, fresh, acc, first, frames, tick, last):
    hgt, wid, chans = state.shape[-3:]
    vmem = pl.BlockSpec(memory_space=pltpu.VMEM)
    hbm = pl.BlockSpec(memory_space=pl.ANY)
    rows = weights.shape[2]
    args, specs = [state, weights], [vmem, vmem]
    if tick:
        args.append(fresh)
        specs.append(hbm)
    begin = acc is None
    if not begin:
        args.append(acc)
        specs.append(vmem)
    tall = hgt + 2
    scratch = [
        pltpu.VMEM((frames, tall, wid, chans), BF16),
        pltpu.VMEM((frames, tall, wid, chans), BF16),
        pltpu.VMEM((TAPS, frames, tall, wid, chans), BF16),
        pltpu.VMEM((TAPS, frames, tall, wid, chans), BF16),
    ]
    if tick:
        scratch += [pltpu.VMEM((4, frames, hgt, wid, chans), BF16), pltpu.SemaphoreType.DMA]
    sums = (2, rows, chans) if last else (2, chans, rows)
    cells = frames * hgt * wid
    return pl.pallas_call(
        functools.partial(block_kernel, (first, frames, begin, tick, last)),
        out_shape=(
            jax.ShapeDtypeStruct((4, frames, hgt, wid, chans), BF16),
            jax.ShapeDtypeStruct(sums, F32),
        ),
        in_specs=specs,
        out_specs=(vmem, vmem),
        scratch_shapes=scratch,
        compiler_params=pltpu.CompilerParams(vmem_limit_bytes=32 << 20),
        cost_estimate=pl.CostEstimate(
            flops=12 * cells * rows * chans, bytes_accessed=8 * cells * chans * 2, transcendentals=0
        ),
        name=f"block_{tick}_{first}",
    )(*args)


def shards(incoming, fresh, weights, momentum):
    replicas = lax.axis_size("dp")
    states = [incoming for _ in CHUNKS]
    acc = None
    outs = [None] * len(CHUNKS)
    for tick in range(TICKS):
        for i, (first, frames) in enumerate(CHUNKS):
            last = tick == TICKS - 1 and i == len(CHUNKS) - 1
            outs[i], acc = block(states[i], weights, fresh, acc, first, frames, tick, last)
            if tick < TICKS - 1:
                states[i] = passed_along(outs[i], "segment")
    rows = weights.shape[2] // replicas
    me = lax.axis_index("dp")
    parts = acc.reshape(2, replicas, rows, weights.shape[3])

    def piece(k):
        return lax.dynamic_slice_in_dim(parts, me ^ k, 1, 1)[:, 0]

    total = piece(0)
    for k in range(1, replicas):
        got = lax.ppermute(piece(k).astype(BF16), "dp", [(d, d ^ k) for d in range(replicas)])
        total = total + got.astype(F32)
    new_momentum = 0.9 * momentum[0] + total / (TICKS * incoming.shape[2] * replicas)
    return (jnp.concatenate(outs, axis=1)[None], new_momentum[None])


def solution(mesh):
    return jax.shard_map(
        shards,
        mesh=mesh,
        in_specs=(
            P("segment", None, "dp", None, None, None),
            P(None, None, "dp", None, None, None),
            P("segment", None, None, None),
            P("segment", None, "dp", None),
        ),
        out_specs=(P("segment", None, "dp", None, None, None), P("segment", None, "dp", None)),
        check_vma=False,
    )
```

time: 151 us -> 84.2 us (0.56)
  waiting for transfers between devices: 60 us -> 8.02 us
  matrix products: 24.7 us -> 0 us
  Pallas kernels: 0 us -> 21.9 us
  starting transfers between devices: 22.5 us -> 42.6 us
  local copies, waits for them, and re-layouts: 23.2 us -> 7.56 us
  between operations: 15.2 us -> 0.88 us
  other arithmetic: 4.53 us -> 2.73 us
    reduce_scatter x1 -> x0, waiting for transfers between devices: 30.5 us -> none  [shards(): lax.psum_scatter(total.astype(jnp.bfloat16), 'dp', scatter_dimension=1, t...]
    dot_general x24 -> x0, matrix products: 24.7 us -> none  [the longest x16 16.4 us: convolve(): out = jnp.dot(cols, filters, preferred_element_type=jnp.float32)]
    pallas_call x0 -> x8, Pallas kernels: none -> 21.9 us  [block(): pl.pallas_call(functools.partial(block_kernel, (first, frames, begin, tic...]
    ppermute x3 -> x13, waiting for transfers between devices: 29.4 us -> 8.02 us  [the longest x6 4.14 us: passed_along(): lax.ppermute(value, axis, [(source, source - 1) for source in range(1, co...]
    ppermute x3 -> x13, starting transfers between devices: 22.5 us -> 42.6 us  [the longest x6 30.1 us: passed_along(): lax.ppermute(value, axis, [(source, source - 1) for source in range(1, co...]
    unnamed x148 -> x26, local copies, waits for them, and re-layouts: 18.1 us -> 7.49 us
    concatenate x15 -> x0, local copies, waits for them, and re-layouts: 2.45 us -> none  [patches(): jnp.concatenate([padded[:, a:a + hgt, b:b + wid, :] for a in range(3) for...]
  transfers between devices with their start and end apart: 4 -> 13, of which waited for: 4 -> 6; matrix products, arithmetic and copies ran while one was open for 11% -> 1% of each run, Pallas kernels for 0% -> 20%
where the time goes in v1:
time: 84.2 us; the launch traced here: 83.7 us
  starting transfers between devices  42.6 us (51%)
  Pallas kernels  21.9 us (26%)
  waiting for transfers between devices  8.02 us (10%)
  local copies, waits for them, and re-layouts  7.56 us (9%)
  other arithmetic  2.73 us (3%)
  between operations  0.88 us (1%)
    ppermute x6, starting transfers between devices, passed_along(): lax.ppermute(value, axis, [(source, source - 1) for source in range(1, co...  30.1 us
    pallas_call x8, Pallas kernels, block(): pl.pallas_call(functools.partial(block_kernel, (first, frames, begin, tic...  21.9 us
    ppermute x7, starting transfers between devices, shards(): lax.ppermute(piece(k).astype(BF16), 'dp', [(d, d ^ k) for d in range(repl...  12.5 us
    unnamed x26, local copies, waits for them, and re-layouts  7.49 us
    ppermute x6, waiting for transfers between devices, passed_along(): lax.ppermute(value, axis, [(source, source - 1) for source in range(1, co...  4.14 us
    ppermute x7, waiting for transfers between devices, shards(): lax.ppermute(piece(k).astype(BF16), 'dp', [(d, d ^ k) for d in range(repl...  3.88 us
    broadcast_in_dim x2, other arithmetic, shards(): return (jnp.concatenate(outs, axis=1)[None], new_momentum[None])  2.73 us
  transfers between devices with their start and end apart: 13, of which 6 were waited for; matrix products, arithmetic and copies ran while one was open for 1% of the time, Pallas kernels for 20%

profile of v1, /device:TPU:16, one launch (start us, length us, event | category | flops | bytes accessed | tf_op | source)
XLA Modules:
  0.0 83.7 jit_solution(681909903500763021)
XLA Ops:
  1.7 1.2 %copy-done.11 = bf16[1,4,4,16,16,128]{5,4,3,2,1,0:T(8,128)(2,1)S(1)} copy-done((bf16[1,4,4,16,16,128]{5,4,3,2,1,0:T(8,128)(2,1)S(1)}, bf16[1,4,4,16,16,128]{5,4,3,2,1,0:T(8,128)(2,1)}, u32[]{:S(2)}) %copy-start.11) | copy-done | bytes 1048600
  2.9 2.3 %block_0_0.1 = (bf16[4,2,16,16,128]{4,3,2,1,0:T(8,128)(2,1)S(1)}, f32[2,128,1152]{2,1,0:T(8,128)S(1)}) custom-call(bf16[1,4,4,16,16,128]{5,4,3,2,1,0:T(8,128)(2,1)S(1)} %copy-done.11, bf16[1,2,1152,128]{3,2,1,0:T(8,128)(2,1)S(1)} %copy-done.1), custom_call_target="tpu_custom_call" | custom-call | flops 905969664 | bytes 1048576 | tf_op jit(solution)/shard_map/block_0_0/pallas_call | solution.py:189
  5.2 7.0 %collective-permute-start = (bf16[4,2,16,16,128]{4,3,2,1,0:T(8,128)(2,1)S(1)}, bf16[4,2,16,16,128]{4,3,2,1,0:T(8,128)(2,1)S(1)}, u32[]{:S(2)}, u32[]{:S(2)}) collective-permute-start(bf16[4,2,16,16,128]{4,3,2,1,0:T(8,128)(2,1)S(1)} %get-tuple-element.18), channel_id=1, source_target_pairs={{8,0},{16,8},{24,16},{32,24},{40,32},{48,40},{56,48},{64,56},{72,6... | collective-permute-start | bytes 1572872 | tf_op jit(solution)/shard_map/ppermute | solution.py:18
  12.2 2.3 %block_0_2.1 = (bf16[4,2,16,16,128]{4,3,2,1,0:T(8,128)(2,1)S(1)}, f32[2,128,1152]{2,1,0:T(8,128)S(1)}) custom-call(bf16[1,4,4,16,16,128]{5,4,3,2,1,0:T(8,128)(2,1)S(1)} %copy-done.11, bf16[1,2,1152,128]{3,2,1,0:T(8,128)(2,1)S(1)} %copy-done.1, f32[2,128,1152]{2,1,0:T(8,128)S(1)} %get-tuple-element.19.refs_2_), custom_call_target="tpu_custom_call" | custom-call | flops 905969664 | bytes 1048576 | tf_op jit(solution)/shard_map/block_0_2/pallas_call | solution.py:189
  14.4 2.6 %collective-permute-start.2 = (bf16[4,2,16,16,128]{4,3,2,1,0:T(8,128)(2,1)S(1)}, bf16[4,2,16,16,128]{4,3,2,1,0:T(8,128)(2,1)S(1)}, u32[]{:S(2)}, u32[]{:S(2)}) collective-permute-start(bf16[4,2,16,16,128]{4,3,2,1,0:T(8,128)(2,1)S(1)} %get-tuple-element.22), channel_id=1, source_target_pairs={{8,0},{16,8},{24,16},{32,24},{40,32},{48,40},{56,48},{64,56},{72,6... | collective-permute-start | bytes 1572872 | tf_op jit(solution)/shard_map/ppermute | solution.py:18
  17.0 1.8 %collective-permute-done.refs_0_ = bf16[4,2,16,16,128]{4,3,2,1,0:T(8,128)(2,1)S(1)} collective-permute-done((bf16[4,2,16,16,128]{4,3,2,1,0:T(8,128)(2,1)S(1)}, bf16[4,2,16,16,128]{4,3,2,1,0:T(8,128)(2,1)S(1)}, u32[]{:S(2)}, u32[]{:S(2)}) %collective-permute-start) | collective-permute-done | bytes 524320 | tf_op jit(solution)/shard_map/ppermute | solution.py:18
  18.9 2.3 %block_1_0.1 = (bf16[4,2,16,16,128]{4,3,2,1,0:T(8,128)(2,1)S(1)}, f32[2,128,1152]{2,1,0:T(8,128)S(1)}) custom-call(bf16[4,2,16,16,128]{4,3,2,1,0:T(8,128)(2,1)S(1)} %collective-permute-done.refs_0_, bf16[1,2,1152,128]{3,2,1,0:T(8,128)(2,1)S(1)} %copy-done.2, bf16[3,4,4,16,16,128]{5,4,3,2,1,0:T(8,128)(2,1)S(1)} %copy-done, ...), custom_call_target="tpu_custom_call" | custom-call | flops 905969664 | bytes 1048576 | tf_op jit(solution)/shard_map/block_1_0/pallas_call | solution.py:189
  21.2 7.4 %collective-permute-start.1 = (bf16[4,2,16,16,128]{4,3,2,1,0:T(8,128)(2,1)S(1)}, bf16[4,2,16,16,128]{4,3,2,1,0:T(8,128)(2,1)S(1)}, u32[]{:S(2)}, u32[]{:S(2)}) collective-permute-start(bf16[4,2,16,16,128]{4,3,2,1,0:T(8,128)(2,1)S(1)} %get-tuple-element.21), channel_id=1, source_target_pairs={{8,0},{16,8},{24,16},{32,24},{40,32},{48,40},{56,48},{64,56},{72,6... | collective-permute-start | bytes 1572872 | tf_op jit(solution)/shard_map/ppermute | solution.py:18
  28.6 2.3 %block_1_2.1 = (bf16[4,2,16,16,128]{4,3,2,1,0:T(8,128)(2,1)S(1)}, f32[2,128,1152]{2,1,0:T(8,128)S(1)}) custom-call(bf16[4,2,16,16,128]{4,3,2,1,0:T(8,128)(2,1)S(1)} %collective-permute-done.2.refs_0_, bf16[1,2,1152,128]{3,2,1,0:T(8,128)(2,1)S(1)} %copy-done.2, bf16[3,4,4,16,16,128]{5,4,3,2,1,0:T(8,128)(2,1)S(1)} %copy-done, ...), custom_call_target="tpu_custom_call" | custom-call | flops 905969664 | bytes 1048576 | tf_op jit(solution)/shard_map/block_1_2/pallas_call | solution.py:189
  30.9 3.3 %collective-permute-start.4 = (bf16[4,2,16,16,128]{4,3,2,1,0:T(8,128)(2,1)S(1)}, bf16[4,2,16,16,128]{4,3,2,1,0:T(8,128)(2,1)S(1)}, u32[]{:S(2)}, u32[]{:S(2)}) collective-permute-start(bf16[4,2,16,16,128]{4,3,2,1,0:T(8,128)(2,1)S(1)} %get-tuple-element.26), channel_id=1, source_target_pairs={{8,0},{16,8},{24,16},{32,24},{40,32},{48,40},{56,48},{64,56},{72,6... | collective-permute-start | bytes 1572872 | tf_op jit(solution)/shard_map/ppermute | solution.py:18
  35.3 3.0 %block_2_0.1 = (bf16[4,2,16,16,128]{4,3,2,1,0:T(8,128)(2,1)}, f32[2,128,1152]{2,1,0:T(8,128)S(1)}) custom-call(bf16[4,2,16,16,128]{4,3,2,1,0:T(8,128)(2,1)S(1)} %collective-permute-done.1.refs_0_, bf16[1,2,1152,128]{3,2,1,0:T(8,128)(2,1)S(1)} %copy-done.2, bf16[3,4,4,16,16,128]{5,4,3,2,1,0:T(8,128)(2,1)S(1)} %copy-done, ...), custom_call_target="tpu_custom_call" | custom-call | flops 905969664 | bytes 1048576 | tf_op jit(solution)/shard_map/block_2_0/pallas_call | solution.py:189
  38.2 7.4 %collective-permute-start.3 = (bf16[4,2,16,16,128]{4,3,2,1,0:T(8,128)(2,1)}, bf16[4,2,16,16,128]{4,3,2,1,0:T(8,128)(2,1)}, u32[]{:S(2)}, u32[]{:S(2)}) collective-permute-start(bf16[4,2,16,16,128]{4,3,2,1,0:T(8,128)(2,1)} %get-tuple-element.25), channel_id=1, source_target_pairs={{8,0},{16,8},{24,16},{32,24},{40,32},{48,40},{56,48},{64,56},{72,6... | collective-permute-start | bytes 1572872 | tf_op jit(solution)/shard_map/ppermute | solution.py:18
  45.7 3.2 %block_2_2.1 = (bf16[4,2,16,16,128]{4,3,2,1,0:T(8,128)(2,1)}, f32[2,128,1152]{2,1,0:T(8,128)S(1)}) custom-call(bf16[4,2,16,16,128]{4,3,2,1,0:T(8,128)(2,1)S(1)} %collective-permute-done.4.refs_0_, bf16[1,2,1152,128]{3,2,1,0:T(8,128)(2,1)S(1)} %copy-done.2, bf16[3,4,4,16,16,128]{5,4,3,2,1,0:T(8,128)(2,1)S(1)} %copy-done, ...), custom_call_target="tpu_custom_call" | custom-call | flops 905969664 | bytes 1048576 | tf_op jit(solution)/shard_map/block_2_2/pallas_call | solution.py:189
  49.9 2.4 %collective-permute-start.5 = (bf16[4,2,16,16,128]{4,3,2,1,0:T(8,128)(2,1)}, bf16[4,2,16,16,128]{4,3,2,1,0:T(8,128)(2,1)}, u32[]{:S(2)}, u32[]{:S(2)}) collective-permute-start(bf16[4,2,16,16,128]{4,3,2,1,0:T(8,128)(2,1)} %get-tuple-element.30), channel_id=1, source_target_pairs={{8,0},{16,8},{24,16},{32,24},{40,32},{48,40},{56,48},{64,56},{72,6... | collective-permute-start | bytes 1572872 | tf_op jit(solution)/shard_map/ppermute | solution.py:18
  53.7 1.3 %copy-done.5 = f32[2,128,1152]{2,1,0:T(8,128)S(1)} copy-done((f32[2,128,1152]{2,1,0:T(8,128)S(1)}, f32[2,128,1152]{2,1,0:T(8,128)}, u32[]{:S(2)}) %copy-start.5) | copy-done | bytes 1179672
  55.0 3.3 %block_3_0.1 = (bf16[4,2,16,16,128]{4,3,2,1,0:T(8,128)(2,1)S(1)}, f32[2,128,1152]{2,1,0:T(8,128)S(1)}) custom-call(bf16[4,2,16,16,128]{4,3,2,1,0:T(8,128)(2,1)} %collective-permute-done.3.refs_0_, bf16[1,2,1152,128]{3,2,1,0:T(8,128)(2,1)S(1)} %copy-done.3, bf16[3,4,4,16,16,128]{5,4,3,2,1,0:T(8,128)(2,1)S(1)} %copy-done, f32[2,128,1152]{2,1,0:T(8,128)S(1)} %copy-done.5), custom_call_target="tpu_custom_call" | custom-call | flops 905969664 | bytes 1048576 | tf_op jit(solution)/shard_map/block_3_0/pallas_call | solution.py:189
  59.3 3.3 %block_3_2.1 = (bf16[4,2,16,16,128]{4,3,2,1,0:T(8,128)(2,1)S(1)}, f32[2,1152,128]{2,1,0:T(8,128)S(1)}) custom-call(bf16[4,2,16,16,128]{4,3,2,1,0:T(8,128)(2,1)} %collective-permute-done.5.refs_0_, bf16[1,2,1152,128]{3,2,1,0:T(8,128)(2,1)S(1)} %copy-done.3, bf16[3,4,4,16,16,128]{5,4,3,2,1,0:T(8,128)(2,1)S(1)} %copy-done, ...), custom_call_target="tpu_custom_call" | custom-call | flops 905969664 | bytes 1048576 | tf_op jit(solution)/shard_map/block_3_2/pallas_call | solution.py:189
  64.6 3.6 %collective-permute-start.10 = (bf16[2,144,128]{2,1,0:T(8,128)(2,1)S(1)}, bf16[2,144,128]{2,1,0:T(8,128)(2,1)S(1)}, u32[]{:S(2)}, u32[]{:S(2)}) collective-permute-start(bf16[2,144,128]{2,1,0:T(8,128)(2,1)S(1)} %get-tuple-element.36), channel_id=1, source_target_pairs={{0,5},{1,4},{2,7},{3,6},{4,1},{5,0},{6,3},{7,2},{8,13},{9,12},{10,... | collective-permute-start | bytes 221192 | tf_op jit(solution)/shard_map/ppermute | solution.py:226
  68.1 1.6 %collective-permute-start.11 = (bf16[2,144,128]{2,1,0:T(8,128)(2,1)S(1)}, bf16[2,144,128]{2,1,0:T(8,128)(2,1)S(1)}, u32[]{:S(2)}, u32[]{:S(2)}) collective-permute-start(bf16[2,144,128]{2,1,0:T(8,128)(2,1)S(1)} %get-tuple-element.35), channel_id=1, source_target_pairs={{0,6},{1,7},{2,4},{3,5},{4,2},{5,3},{6,0},{7,1},{8,14},{9,15},{10,... | collective-permute-start | bytes 221192 | tf_op jit(solution)/shard_map/ppermute | solution.py:226
  69.8 2.5 %collective-permute-start.12 = (bf16[2,144,128]{2,1,0:T(8,128)(2,1)S(1)}, bf16[2,144,128]{2,1,0:T(8,128)(2,1)S(1)}, u32[]{:S(2)}, u32[]{:S(2)}) collective-permute-start(bf16[2,144,128]{2,1,0:T(8,128)(2,1)S(1)} %get-tuple-element.40), channel_id=1, source_target_pairs={{0,7},{1,6},{2,5},{3,4},{4,3},{5,2},{6,1},{7,0},{8,15},{9,14},{10,... | collective-permute-start | bytes 221192 | tf_op jit(solution)/shard_map/ppermute | solution.py:226
  72.5 3.9 %collective-permute-start.7 = (bf16[2,144,128]{2,1,0:T(8,128)(2,1)S(1)}, bf16[2,144,128]{2,1,0:T(8,128)(2,1)S(1)}, u32[]{:S(2)}, u32[]{:S(2)}) collective-permute-start(bf16[2,144,128]{2,1,0:T(8,128)(2,1)S(1)} %get-tuple-element.39), channel_id=1, source_target_pairs={{0,2},{1,3},{2,0},{3,1},{4,6},{5,7},{6,4},{7,5},{8,10},{9,11},{10,... | collective-permute-start | bytes 221192 | tf_op jit(solution)/shard_map/ppermute | solution.py:226
  78.2 1.4 %collective-permute-done.7 = bf16[2,144,128]{2,1,0:T(8,128)(2,1)S(1)} collective-permute-done((bf16[2,144,128]{2,1,0:T(8,128)(2,1)S(1)}, bf16[2,144,128]{2,1,0:T(8,128)(2,1)S(1)}, u32[]{:S(2)}, u32[]{:S(2)}) %collective-permute-start.7) | collective-permute-done | bytes 73760 | tf_op jit(solution)/shard_map/ppermute | solution.py:226
  79.6 2.5 %collective-permute-done.8 = bf16[2,144,128]{2,1,0:T(8,128)(2,1)S(1)} collective-permute-done((bf16[2,144,128]{2,1,0:T(8,128)(2,1)S(1)}, bf16[2,144,128]{2,1,0:T(8,128)(2,1)S(1)}, u32[]{:S(2)}, u32[]{:S(2)}) %collective-permute-start.8) | collective-permute-done | bytes 73760 | tf_op jit(solution)/shard_map/ppermute | solution.py:226
  82.0 1.7 %fusion.8 = f32[1,2,144,128]{3,2,1,0:T(8,128)} fusion(bf16[2,144,128]{2,1,0:T(8,128)(2,1)S(1)} %collective-permute-done.12, bf16[2,144,128]{2,1,0:T(8,128)(2,1)S(1)} %collective-permute-done.11, bf16[2,144,128]{2,1,0:T(8,128)(2,1)S(1)} %collective-permute-done.10, bf16[2,144,128]{2,1,0:T(8,128)(2,1)S(1)} %collective-permute-done.9, ...), kind=kLoop, calls=%fused_computation.17 | loop fusion | flops 626688 | bytes 958468 | tf_op jit(solution)/shard_map/broadcast_in_dim | solution.py:229
  (39 shorter events, 9.4 us)
Async XLA Ops:
  0.6 1.1 %copy-start.1 = (bf16[1,2,1152,128]{3,2,1,0:T(8,128)(2,1)S(1)}, bf16[1,2,1152,128]{3,2,1,0:T(8,128)(2,1)}, u32[]{:S(2)}) copy-start(bf16[1,2,1152,128]{3,2,1,0:T(8,128)(2,1)} %refs_1_.15) | copy-start | bytes 1769476
  1.7 1.2 %copy-start.11 = (bf16[1,4,4,16,16,128]{5,4,3,2,1,0:T(8,128)(2,1)S(1)}, bf16[1,4,4,16,16,128]{5,4,3,2,1,0:T(8,128)(2,1)}, u32[]{:S(2)}) copy-start(bf16[1,4,4,16,16,128]{5,4,3,2,1,0:T(8,128)(2,1)} %refs_0_.3) | copy-start | bytes 3145732
  2.9 15.9 %copy-start.2 = (bf16[1,2,1152,128]{3,2,1,0:T(8,128)(2,1)S(1)}, bf16[1,2,1152,128]{3,2,1,0:T(8,128)(2,1)}, u32[]{:S(2)}) copy-start(bf16[1,2,1152,128]{3,2,1,0:T(8,128)(2,1)} %refs_1_.15) | copy-start | bytes 1769476
  5.2 13.7 %collective-permute-start = (bf16[4,2,16,16,128]{4,3,2,1,0:T(8,128)(2,1)S(1)}, bf16[4,2,16,16,128]{4,3,2,1,0:T(8,128)(2,1)S(1)}, u32[]{:S(2)}, u32[]{:S(2)}) collective-permute-start(bf16[4,2,16,16,128]{4,3,2,1,0:T(8,128)(2,1)S(1)} %get-tuple-element.18), channel_id=1, source_target_pairs={{8,0},{16,8},{24,16},{32,24},{40,32},{48,40},{56,48},{64,56},{72,6... | collective-permute-start | bytes 1572872 | tf_op jit(solution)/shard_map/ppermute | solution.py:18
  12.2 6.7 %copy-start = (bf16[3,4,4,16,16,128]{5,4,3,2,1,0:T(8,128)(2,1)S(1)}, bf16[3,4,4,16,16,128]{5,4,3,2,1,0:T(8,128)(2,1)}, u32[]{:S(2)}) copy-start(bf16[3,4,4,16,16,128]{5,4,3,2,1,0:T(8,128)(2,1)} %refs_2_.11) | copy-start | bytes 9437188
  14.4 14.2 %collective-permute-start.2 = (bf16[4,2,16,16,128]{4,3,2,1,0:T(8,128)(2,1)S(1)}, bf16[4,2,16,16,128]{4,3,2,1,0:T(8,128)(2,1)S(1)}, u32[]{:S(2)}, u32[]{:S(2)}) collective-permute-start(bf16[4,2,16,16,128]{4,3,2,1,0:T(8,128)(2,1)S(1)} %get-tuple-element.22), channel_id=1, source_target_pairs={{8,0},{16,8},{24,16},{32,24},{40,32},{48,40},{56,48},{64,56},{72,6... | collective-permute-start | bytes 1572872 | tf_op jit(solution)/shard_map/ppermute | solution.py:18
  21.2 14.1 %collective-permute-start.1 = (bf16[4,2,16,16,128]{4,3,2,1,0:T(8,128)(2,1)S(1)}, bf16[4,2,16,16,128]{4,3,2,1,0:T(8,128)(2,1)S(1)}, u32[]{:S(2)}, u32[]{:S(2)}) collective-permute-start(bf16[4,2,16,16,128]{4,3,2,1,0:T(8,128)(2,1)S(1)} %get-tuple-element.21), channel_id=1, source_target_pairs={{8,0},{16,8},{24,16},{32,24},{40,32},{48,40},{56,48},{64,56},{72,6... | collective-permute-start | bytes 1572872 | tf_op jit(solution)/shard_map/ppermute | solution.py:18
  30.9 14.7 %collective-permute-start.4 = (bf16[4,2,16,16,128]{4,3,2,1,0:T(8,128)(2,1)S(1)}, bf16[4,2,16,16,128]{4,3,2,1,0:T(8,128)(2,1)S(1)}, u32[]{:S(2)}, u32[]{:S(2)}) collective-permute-start(bf16[4,2,16,16,128]{4,3,2,1,0:T(8,128)(2,1)S(1)} %get-tuple-element.26), channel_id=1, source_target_pairs={{8,0},{16,8},{24,16},{32,24},{40,32},{48,40},{56,48},{64,56},{72,6... | collective-permute-start | bytes 1572872 | tf_op jit(solution)/shard_map/ppermute | solution.py:18
  38.2 14.4 %collective-permute-start.3 = (bf16[4,2,16,16,128]{4,3,2,1,0:T(8,128)(2,1)}, bf16[4,2,16,16,128]{4,3,2,1,0:T(8,128)(2,1)}, u32[]{:S(2)}, u32[]{:S(2)}) collective-permute-start(bf16[4,2,16,16,128]{4,3,2,1,0:T(8,128)(2,1)} %get-tuple-element.25), channel_id=1, source_target_pairs={{8,0},{16,8},{24,16},{32,24},{40,32},{48,40},{56,48},{64,56},{72,6... | collective-permute-start | bytes 1572872 | tf_op jit(solution)/shard_map/ppermute | solution.py:18
  48.9 1.0 %copy-start.4 = (f32[2,128,1152]{2,1,0:T(8,128)}, f32[2,128,1152]{2,1,0:T(8,128)S(1)}, u32[]{:S(2)}) copy-start(f32[2,128,1152]{2,1,0:T(8,128)S(1)} %get-tuple-element.28.refs_3_) | copy-start | bytes 3538948
  49.9 9.4 %collective-permute-start.5 = (bf16[4,2,16,16,128]{4,3,2,1,0:T(8,128)(2,1)}, bf16[4,2,16,16,128]{4,3,2,1,0:T(8,128)(2,1)}, u32[]{:S(2)}, u32[]{:S(2)}) collective-permute-start(bf16[4,2,16,16,128]{4,3,2,1,0:T(8,128)(2,1)} %get-tuple-element.30), channel_id=1, source_target_pairs={{8,0},{16,8},{24,16},{32,24},{40,32},{48,40},{56,48},{64,56},{72,6... | collective-permute-start | bytes 1572872 | tf_op jit(solution)/shard_map/ppermute | solution.py:18
  52.7 1.1 %copy-start.3 = (bf16[1,2,1152,128]{3,2,1,0:T(8,128)(2,1)S(1)}, bf16[1,2,1152,128]{3,2,1,0:T(8,128)(2,1)}, u32[]{:S(2)}) copy-start(bf16[1,2,1152,128]{3,2,1,0:T(8,128)(2,1)} %refs_1_.15) | copy-start | bytes 1769476
  53.7 1.3 %copy-start.5 = (f32[2,128,1152]{2,1,0:T(8,128)S(1)}, f32[2,128,1152]{2,1,0:T(8,128)}, u32[]{:S(2)}) copy-start(f32[2,128,1152]{2,1,0:T(8,128)} %copy-done.4) | copy-start | bytes 3538948
  58.4 4.3 %copy-start.6 = (bf16[4,2,16,16,128]{4,3,2,1,0:T(8,128)(2,1)}, bf16[4,2,16,16,128]{4,3,2,1,0:T(8,128)(2,1)S(1)}, u32[]{:S(2)}) copy-start(bf16[4,2,16,16,128]{4,3,2,1,0:T(8,128)(2,1)S(1)} %get-tuple-element.29) | copy-start | bytes 1572868
  63.5 13.6 %copy-start.7 = (bf16[4,2,16,16,128]{4,3,2,1,0:T(8,128)(2,1)S(1)}, bf16[4,2,16,16,128]{4,3,2,1,0:T(8,128)(2,1)}, u32[]{:S(2)}) copy-start(bf16[4,2,16,16,128]{4,3,2,1,0:T(8,128)(2,1)} %copy-done.6) | copy-start | bytes 1572868
  63.5 13.6 %copy-start.9 = (bf16[4,2,16,16,128]{4,3,2,1,0:T(8,128)(2,1)S(1)}, bf16[4,2,16,16,128]{4,3,2,1,0:T(8,128)(2,1)}, u32[]{:S(2)}) copy-start(bf16[4,2,16,16,128]{4,3,2,1,0:T(8,128)(2,1)} %copy-done.8) | copy-start | bytes 1572868
  64.6 17.5 %copy-start.12 = (f32[1,2,144,128]{3,2,1,0:T(8,128)S(1)}, f32[1,2,144,128]{3,2,1,0:T(8,128)}, u32[]{:S(2)}) copy-start(f32[1,2,144,128]{3,2,1,0:T(8,128)} %param.7) | copy-start | bytes 442372
  64.6 11.9 %collective-permute-start.10 = (bf16[2,144,128]{2,1,0:T(8,128)(2,1)S(1)}, bf16[2,144,128]{2,1,0:T(8,128)(2,1)S(1)}, u32[]{:S(2)}, u32[]{:S(2)}) collective-permute-start(bf16[2,144,128]{2,1,0:T(8,128)(2,1)S(1)} %get-tuple-element.36), channel_id=1, source_target_pairs={{0,5},{1,4},{2,7},{3,6},{4,1},{5,0},{6,3},{7,2},{8,13},{9,12},{10,... | collective-permute-start | bytes 221192 | tf_op jit(solution)/shard_map/ppermute | solution.py:226
  68.1 8.8 %collective-permute-start.11 = (bf16[2,144,128]{2,1,0:T(8,128)(2,1)S(1)}, bf16[2,144,128]{2,1,0:T(8,128)(2,1)S(1)}, u32[]{:S(2)}, u32[]{:S(2)}) collective-permute-start(bf16[2,144,128]{2,1,0:T(8,128)(2,1)S(1)} %get-tuple-element.35), channel_id=1, source_target_pairs={{0,6},{1,7},{2,4},{3,5},{4,2},{5,3},{6,0},{7,1},{8,14},{9,15},{10,... | collective-permute-start | bytes 221192 | tf_op jit(solution)/shard_map/ppermute | solution.py:226
  69.8 8.4 %collective-permute-start.12 = (bf16[2,144,128]{2,1,0:T(8,128)(2,1)S(1)}, bf16[2,144,128]{2,1,0:T(8,128)(2,1)S(1)}, u32[]{:S(2)}, u32[]{:S(2)}) collective-permute-start(bf16[2,144,128]{2,1,0:T(8,128)(2,1)S(1)} %get-tuple-element.40), channel_id=1, source_target_pairs={{0,7},{1,6},{2,5},{3,4},{4,3},{5,2},{6,1},{7,0},{8,15},{9,14},{10,... | collective-permute-start | bytes 221192 | tf_op jit(solution)/shard_map/ppermute | solution.py:226
  72.3 5.9 %collective-permute-start.6 = (bf16[2,144,128]{2,1,0:T(8,128)(2,1)S(1)}, bf16[2,144,128]{2,1,0:T(8,128)(2,1)S(1)}, u32[]{:S(2)}, u32[]{:S(2)}) collective-permute-start(bf16[2,144,128]{2,1,0:T(8,128)(2,1)S(1)} %get-tuple-element.34), channel_id=1, source_target_pairs={{0,1},{1,0},{2,3},{3,2},{4,5},{5,4},{6,7},{7,6},{8,9},{9,8},{10,11... | collective-permute-start | bytes 221192 | tf_op jit(solution)/shard_map/ppermute | solution.py:226
  72.5 7.0 %collective-permute-start.7 = (bf16[2,144,128]{2,1,0:T(8,128)(2,1)S(1)}, bf16[2,144,128]{2,1,0:T(8,128)(2,1)S(1)}, u32[]{:S(2)}, u32[]{:S(2)}) collective-permute-start(bf16[2,144,128]{2,1,0:T(8,128)(2,1)S(1)} %get-tuple-element.39), channel_id=1, source_target_pairs={{0,2},{1,3},{2,0},{3,1},{4,6},{5,7},{6,4},{7,5},{8,10},{9,11},{10,... | collective-permute-start | bytes 221192 | tf_op jit(solution)/shard_map/ppermute | solution.py:226
  76.5 5.6 %collective-permute-start.8 = (bf16[2,144,128]{2,1,0:T(8,128)(2,1)S(1)}, bf16[2,144,128]{2,1,0:T(8,128)(2,1)S(1)}, u32[]{:S(2)}, u32[]{:S(2)}) collective-permute-start(bf16[2,144,128]{2,1,0:T(8,128)(2,1)S(1)} %get-tuple-element.38), channel_id=1, source_target_pairs={{0,3},{1,2},{2,1},{3,0},{4,7},{5,6},{6,5},{7,4},{8,11},{9,10},{10,... | collective-permute-start | bytes 221192 | tf_op jit(solution)/shard_map/ppermute | solution.py:226
  77.0 5.1 %collective-permute-start.9 = (bf16[2,144,128]{2,1,0:T(8,128)(2,1)S(1)}, bf16[2,144,128]{2,1,0:T(8,128)(2,1)S(1)}, u32[]{:S(2)}, u32[]{:S(2)}) collective-permute-start(bf16[2,144,128]{2,1,0:T(8,128)(2,1)S(1)} %get-tuple-element.37), channel_id=1, source_target_pairs={{0,4},{1,5},{2,6},{3,7},{4,0},{5,1},{6,2},{7,3},{8,12},{9,13},{10,... | collective-permute-start | bytes 221192 | tf_op jit(solution)/shard_map/ppermute | solution.py:226
  (2 other events, 1.8 us)

commit v2 on v1

v2 whole, which is shorter than its diff:
```python
import functools

import jax
import jax.numpy as jnp
from jax import lax
from jax.experimental import pallas as pl
from jax.experimental.pallas import tpu as pltpu
from jax.sharding import PartitionSpec as P

TICKS = 4
TAPS = 3
CHUNKS = ((0, 2), (2, 2))
GRANT = 16 << 20
F32, BF16 = jnp.float32, jnp.bfloat16


def passed_along(value, tick):
    count, replicas = lax.axis_size("segment"), lax.axis_size("dp")
    half, swap = count // 2, replicas // 2
    crossing = {half} | ({half + 1} if tick < TICKS - 2 else set()) | ({half - 1} if tick == 1 else set())
    pairs = [
        (s * replicas + d, (s - 1) * replicas + (d ^ swap if s in crossing else d))
        for s in range(1, count)
        for d in range(replicas)
    ]
    return lax.ppermute(value, ("segment", "dp"), pairs)


def tap(w, a, b):
    chans = w.shape[1]
    first = (TAPS * a + b) * chans
    return w[first : first + chans, :]


def sides(value, wid):
    rows = value.shape[0]
    col = lax.broadcasted_iota(jnp.int32, value.shape, 0) % wid
    before = jnp.where(col == 0, 0.0, pltpu.roll(value, 1, 0))
    after = jnp.where(col == wid - 1, 0.0, pltpu.roll(value, rows - 1, 0))
    return before, after


def windows(pad, count, hgt):
    return pad[:, count : count + hgt].reshape(-1, pad.shape[-1])


def conv(pad_ref, w, wid):
    hgt, chans = pad_ref.shape[1] - 2, pad_ref.shape[-1]
    field = pad_ref[...]
    lhs = jnp.concatenate([windows(field, a, hgt) for a in range(TAPS)], axis=1)
    rhs = jnp.concatenate(
        [jnp.concatenate([tap(w, a, b) for b in range(TAPS)], axis=1) for a in range(TAPS)], axis=0
    )
    out = jnp.dot(lhs, rhs, preferred_element_type=F32)
    left, mid, right = (out[:, b * chans : (b + 1) * chans] for b in range(TAPS))
    return sides(left, wid)[0] + mid + sides(right, wid)[1]


def conv_back(pads_ref, w):
    hgt = pads_ref.shape[2] - 2
    lhs = jnp.concatenate(
        [windows(pads_ref[b], a, hgt) for a in range(TAPS) for b in range(TAPS)], axis=1
    )
    rhs = jnp.concatenate(
        [tap(w, TAPS - 1 - a, TAPS - 1 - b) for a in range(TAPS) for b in range(TAPS)], axis=1
    )
    return lax.dot_general(lhs, rhs, (((1,), (1,)), ((), ())), preferred_element_type=F32)


def grad_of(field, pads_ref):
    hgt = pads_ref.shape[2] - 2
    cols = jnp.concatenate(
        [
            windows(pads_ref[TAPS - 1 - b], TAPS - 1 - a, hgt)
            for a in range(TAPS)
            for b in range(TAPS)
        ],
        axis=1,
    )
    return lax.dot_general(field, cols, (((0,), (0,)), ((), ())), preferred_element_type=F32)


def put_field(pad_ref, value):
    frames, tall, wid, chans = pad_ref.shape
    pad_ref[:, 1 : tall - 1] = value.reshape(frames, tall - 2, wid, chans)


def put_slope(pads_ref, slope, wid):
    before, after = sides(slope, wid)
    put_field(pads_ref.at[0], before.astype(BF16))
    put_field(pads_ref.at[1], slope.astype(BF16))
    put_field(pads_ref.at[2], after.astype(BF16))


def clear_edges(pads_ref):
    tall = pads_ref.shape[-3]
    lead = pads_ref.shape[:-3]
    zero = jnp.zeros(lead + (1,) + pads_ref.shape[-2:], BF16)
    at = (slice(None),) * len(lead)
    pads_ref[at + (slice(0, 1),)] = zero
    pads_ref[at + (slice(tall - 1, tall),)] = zero


def slopes(act):
    sig = jax.nn.sigmoid(act)
    return act * sig, sig * (1.0 + act * (1.0 - sig))


def fetched(src, dst, sem):
    copy = pltpu.make_async_copy(src, dst, sem)
    copy.start()
    return copy


def frame_kernel(tick, i, *refs):
    first, frames = CHUNKS[i]
    refs = list(refs)
    src_ref, w_ref = refs[:2]
    del refs[:2]
    if tick:
        fresh_ref = refs.pop(0)
    out_ref, kept_ref = refs[:2]
    del refs[:2]
    hgt, wid, chans = out_ref.shape[2:]
    last = tick == TICKS - 1 and i == len(CHUNKS) - 1
    opening = tick == 0 and i == 0
    if opening:
        whole_ref, wout_ref, xpad, xpad2, zpads, zpads2, sems = refs
        at = pl.ds(first, frames)
        near = [
            fetched(src_ref.at[0, n, at], whole_ref.at[n, at], sems.at[n]) for n in (0, 1, 3, 2)
        ]
        wg = fetched(w_ref.at[0, 1], wout_ref.at[1], sems.at[4])
        wf = fetched(w_ref.at[0, 0], wout_ref.at[0], sems.at[5])
        later = pl.ds(first + frames, src_ref.shape[2] - frames)
        rest = fetched(src_ref.at[0, :, later], whole_ref.at[:, later], sems.at[6])
    else:
        xpad, xpad2, zpads, zpads2 = refs[:4]
    if tick:
        fbuf, sem = refs[4:]
        is_last = lax.axis_index("segment") == lax.axis_size("segment") - 1

        @pl.when(is_last)
        def _():
            fetched(fresh_ref.at[tick - 1, :, pl.ds(first, frames)], fbuf, sem).wait()

        def part(n):
            return jnp.where(is_last, fbuf[n], src_ref[n]).reshape(-1, chans)
    else:
        held = whole_ref if opening else src_ref

        def part(n):
            return held[n, first : first + frames].reshape(-1, chans)

    for pad in (xpad, xpad2, zpads, zpads2):
        clear_edges(pad)
    shape = (frames, hgt, wid, chans)
    if opening:
        near[0].wait()
        wg.wait()
        w_ref = wout_ref
    w_g = w_ref[1]
    y_one = part(0)
    kept_ref[0] = y_one
    put_field(xpad, y_one)
    act, slope = slopes(conv(xpad, w_g, wid))
    if opening:
        for copy in near[1:]:
            copy.wait()
    x_two = (part(1).astype(F32) - act).astype(BF16)
    put_field(xpad2, x_two)
    out_ref[1] = x_two.reshape(shape)
    put_slope(zpads, part(3).astype(F32) * slope, wid)
    kept_ref[1] = windows(zpads[1], 1, hgt)
    dx_one = (part(2).astype(F32) + conv_back(zpads, w_g)).astype(BF16)
    out_ref[2] = dx_one.reshape(shape)

    if opening:
        wf.wait()
    w_f = w_ref[0]
    act, slope = slopes(conv(xpad2, w_f, wid))
    out_ref[0] = (y_one.astype(F32) - act).astype(BF16).reshape(shape)
    if last:
        kept_ref[2] = (dx_one.astype(F32) * slope).astype(BF16)
        out_ref[3] = part(3).reshape(shape)
    else:
        put_slope(zpads2, dx_one.astype(F32) * slope, wid)
        kept_ref[2] = windows(zpads2[1], 1, hgt)
        dx_two = part(3).astype(F32) + conv_back(zpads2, w_f)
        out_ref[3] = dx_two.astype(BF16).reshape(shape)
    if opening:
        rest.wait()


VMEM_SPEC = pl.BlockSpec(memory_space=pltpu.VMEM)
HBM_SPEC = pl.BlockSpec(memory_space=pltpu.HBM)


def in_hbm(value):
    return pltpu.with_memory_space_constraint(value, pltpu.HBM)


def pads(frames, tall, wid, chans, lead=()):
    return pltpu.VMEM(lead + (frames, tall, wid, chans), BF16)


def frame_step(tick, i, source, weights, fresh):
    frames = CHUNKS[i][1]
    hgt, wid, chans = source.shape[-3:]
    rows = weights.shape[-2]
    opening = tick == 0 and i == 0
    cells = frames * hgt * wid
    args, specs = [source, weights], [HBM_SPEC if opening else VMEM_SPEC] * 2
    outs = [
        jax.ShapeDtypeStruct((4, frames, hgt, wid, chans), BF16),
        jax.ShapeDtypeStruct((3, cells, chans), BF16),
    ]
    if opening:
        args = [in_hbm(source), in_hbm(weights)]
        outs.append(jax.ShapeDtypeStruct(source.shape[1:], BF16))
        outs.append(jax.ShapeDtypeStruct(weights.shape[1:], BF16))
    if tick:
        args.append(in_hbm(fresh))
        specs.append(HBM_SPEC)
    tall = hgt + 2
    scratch = [pads(frames, tall, wid, chans)] * 2 + [pads(frames, tall, wid, chans, (TAPS,))] * 2
    if opening:
        scratch.append(pltpu.SemaphoreType.DMA((7,)))
    if tick:
        scratch += [pads(frames, hgt, wid, chans, (4,)), pltpu.SemaphoreType.DMA]
    return pl.pallas_call(
        functools.partial(frame_kernel, tick, i),
        out_shape=outs,
        in_specs=specs,
        out_specs=[VMEM_SPEC] * len(outs),
        scratch_shapes=scratch,
        compiler_params=pltpu.CompilerParams(vmem_limit_bytes=GRANT),
        cost_estimate=pl.CostEstimate(
            flops=8 * cells * rows * chans, bytes_accessed=10 * cells * chans * 2, transcendentals=0
        ),
        name=f"frame_{tick}_{i}",
    )(*args)


def grads_kernel(count, begin, last, *refs):
    refs = list(refs)
    outs, kepts = refs[:count], refs[count : 2 * count]
    del refs[: 2 * count]
    acc_ref = None if begin else refs.pop(0)
    zpads = refs.pop()
    full_ref = refs.pop() if last else None
    frames, tall, wid, chans = zpads.shape[2:]
    clear_edges(zpads)
    sums = []
    for branch in range(2):
        fields = []
        begun = 0
        for out_ref, kept_ref in zip(outs, kepts):
            some = out_ref.shape[1]
            slope = kept_ref[2 - branch].astype(F32)
            put_slope_at = zpads.at[branch, :, pl.ds(begun, some)]
            put_slope(put_slope_at, slope, wid)
            fields.append(kept_ref[0] if branch else out_ref[1].reshape(-1, chans))
            begun += some
        field = fields[0] if count == 1 else jnp.concatenate(fields, axis=0)
        total = grad_of(field, zpads.at[branch])
        if not begin:
            total = total + acc_ref[branch]
        sums.append(total)
    if not last:
        refs[0][0] = sums[0]
        refs[0][1] = sums[1]
        return
    for b in range(TAPS * TAPS):
        for branch in range(2):
            full_ref[branch, pl.ds(b * chans, chans)] = sums[branch][:, b * chans : (b + 1) * chans]
    me = lax.axis_index("dp")
    rows = refs[0].shape[1]
    for k, ref in enumerate(refs):
        begins = pl.multiple_of((me ^ k) * rows, 16)
        ref[...] = full_ref[:, pl.ds(begins, rows)].astype(ref.dtype)


def grads_step(outs, kepts, acc, rows, last, name):
    frames, hgt, wid, chans = outs[0].shape[1:]
    frames = sum(out.shape[1] for out in outs)
    begin = acc is None
    args = [*outs, *kepts] + ([] if begin else [acc])
    scratch = [pads(frames, hgt + 2, wid, chans, (2, TAPS))]
    if last:
        replicas = lax.axis_size("dp")
        part = (2, rows // replicas, chans)
        shapes = [jax.ShapeDtypeStruct(part, BF16 if k else F32) for k in range(replicas)]
        scratch.insert(0, pltpu.VMEM((2, rows, chans), F32))
    else:
        shapes = [jax.ShapeDtypeStruct((2, chans, rows), F32)]
    cells = frames * hgt * wid
    return pl.pallas_call(
        functools.partial(grads_kernel, len(outs), begin, last),
        out_shape=shapes,
        in_specs=[VMEM_SPEC] * len(args),
        out_specs=[VMEM_SPEC] * len(shapes),
        scratch_shapes=scratch,
        compiler_params=pltpu.CompilerParams(vmem_limit_bytes=GRANT),
        cost_estimate=pl.CostEstimate(
            flops=4 * cells * rows * chans, bytes_accessed=4 * rows * chans * 4, transcendentals=0
        ),
        name=name,
    )(*args)


def finish_kernel(count, *refs):
    outs, kept_ref, w_ref = refs[:count], refs[count], refs[count + 1]
    whole_ref, zpads, sems = refs[count + 2 :]
    copies = [
        fetched(outs[i], whole_ref.at[0, :, pl.ds(*CHUNKS[i])], sems.at[i])
        for i in range(count - 1)
    ]
    end = outs[-1]
    shape, wid, chans = end.shape[1:], end.shape[3], end.shape[4]
    at = pl.ds(*CHUNKS[-1])
    copies.append(fetched(end.at[:3], whole_ref.at[0, :3, at], sems.at[count - 1]))
    clear_edges(zpads)
    put_slope(zpads, kept_ref[2].astype(F32), wid)
    dx_two = end[3].reshape(-1, chans).astype(F32) + conv_back(zpads, w_ref[0])
    zpads[0, :, 1 : shape[1] + 1] = dx_two.astype(BF16).reshape(shape)
    copies.append(
        fetched(zpads.at[0, :, pl.ds(1, shape[1])], whole_ref.at[0, 3, at], sems.at[count])
    )
    for copy in copies:
        copy.wait()


def finish(outs, kept, weights, frames):
    hgt, wid, chans = outs[-1].shape[2:]
    args = [*outs, kept, weights]
    return pl.pallas_call(
        functools.partial(finish_kernel, len(outs)),
        out_shape=jax.ShapeDtypeStruct((1, 4, frames, hgt, wid, chans), BF16),
        in_specs=[VMEM_SPEC] * len(args),
        out_specs=HBM_SPEC,
        scratch_shapes=[
            pads(CHUNKS[-1][1], hgt + 2, wid, chans, (TAPS,)),
            pltpu.SemaphoreType.DMA((len(outs) + 1,)),
        ],
        compiler_params=pltpu.CompilerParams(vmem_limit_bytes=GRANT),
        cost_estimate=pl.CostEstimate(flops=1 << 27, bytes_accessed=1 << 20, transcendentals=0),
        name="finish",
    )(*args)


def momentum_kernel(scale, mom_ref, *refs):
    out_ref = refs[-1]
    total = refs[0][...]
    for ref in refs[1:-1]:
        total = total + ref[...].astype(F32)
    out_ref[0] = 0.9 * mom_ref[0] + total * scale


def shards(incoming, fresh, weights, momentum):
    replicas = lax.axis_size("dp")
    frames = incoming.shape[2]
    rows = weights.shape[2]
    count = len(CHUNKS)
    source, wts = incoming, weights
    states = [None] * count
    acc = None
    for tick in range(TICKS):
        outs, kepts = [], []
        for i in range(count):
            source = states[i] if tick else (whole if i else incoming)
            got = frame_step(tick, i, source, wts, fresh)
            outs.append(got[0])
            kepts.append(got[1])
            if tick == 0 and i == 0:
                whole, wts = got[2:]
            if tick < TICKS - 1:
                states[i] = passed_along(got[0], tick)
        if tick < TICKS - 1:
            (acc,) = grads_step(outs, kepts, acc, rows, False, f"grads_{tick}")
    if count > 1:
        (acc,) = grads_step(outs[:-1], kepts[:-1], acc, rows, False, "grads_late")
    pieces = grads_step(outs[-1:], kepts[-1:], acc, rows, True, "grads_last")
    terms = [pieces[0]] + [
        lax.ppermute(pieces[k], "dp", [(d, d ^ k) for d in range(replicas)])
        for k in range(1, replicas)
    ]
    outgoing = finish(outs, kepts[-1], wts, frames)
    new_momentum = pl.pallas_call(
        functools.partial(momentum_kernel, 1.0 / (TICKS * frames * replicas)),
        out_shape=jax.ShapeDtypeStruct(momentum.shape, F32),
        in_specs=[VMEM_SPEC] * (1 + replicas),
        out_specs=VMEM_SPEC,
        compiler_params=pltpu.CompilerParams(vmem_limit_bytes=GRANT),
        name="momentum",
    )(momentum, *terms)
    return (outgoing, new_momentum)


def solution(mesh):
    return jax.shard_map(
        shards,
        mesh=mesh,
        in_specs=(
            P("segment", None, "dp", None, None, None),
            P(None, None, "dp", None, None, None),
            P("segment", None, None, None),
            P("segment", None, "dp", None),
        ),
        out_specs=(P("segment", None, "dp", None, None, None), P("segment", None, "dp", None)),
        check_vma=False,
    )
```

time: 84.2 us -> 75.6 us (0.90)
  local copies, waits for them, and re-layouts: 7.56 us -> 0.01 us
  Pallas kernels: 21.9 us -> 25.3 us
  other arithmetic: 2.73 us -> 0 us
  starting transfers between devices: 42.6 us -> 41.7 us
    unnamed x26 -> x2, local copies, waits for them, and re-layouts: 7.49 us -> 0.01 us
    pallas_call x8 -> x15, Pallas kernels: 21.9 us -> 25.3 us  [the longest x8 19.2 us: frame_step(): pl.pallas_call(functools.partial(frame_kernel, tick, i), out_shape=outs,...]
    broadcast_in_dim x2 -> x0, other arithmetic: 2.73 us -> none  [shards(): return (jnp.concatenate(outs, axis=1)[None], new_momentum[None])]
    ppermute x13, starting transfers between devices: 42.6 us -> 41.7 us  [the longest x6 28.3 us: passed_along(): return lax.ppermute(value, ('segment', 'dp'), pairs)]
  transfers between devices with their start and end apart: 13 -> 13, of which waited for: 6 -> 5; matrix products, arithmetic and copies ran while one was open for 1% -> 0% of each run, Pallas kernels for 20% -> 25%
where the time goes in v2:
time: 75.6 us; the launch traced here: 75.1 us
  starting transfers between devices  41.7 us (55%)
  Pallas kernels  25.3 us (33%)
  waiting for transfers between devices  7.22 us (10%)
  between operations  0.83 us (1%)
    ppermute x6, starting transfers between devices, passed_along(): return lax.ppermute(value, ('segment', 'dp'), pairs)  28.3 us
    pallas_call x8, Pallas kernels, frame_step(): pl.pallas_call(functools.partial(frame_kernel, tick, i), out_shape=outs,...  19.2 us
    ppermute x7, starting transfers between devices, shards(): lax.ppermute(pieces[k], 'dp', [(d, d ^ k) for d in range(replicas)])  13.4 us
    pallas_call x5, Pallas kernels, grads_step(): pl.pallas_call(functools.partial(grads_kernel, len(outs), begin, last), o...  4.25 us
    ppermute x7, waiting for transfers between devices, shards(): lax.ppermute(pieces[k], 'dp', [(d, d ^ k) for d in range(replicas)])  3.76 us
    ppermute x6, waiting for transfers between devices, passed_along(): return lax.ppermute(value, ('segment', 'dp'), pairs)  3.46 us
  transfers between devices with their start and end apart: 13, of which 5 were waited for; matrix products, arithmetic and copies ran while one was open for 0% of the time, Pallas kernels for 25%

profile of v2, /device:TPU:16, one launch (start us, length us, event | category | flops | bytes accessed | tf_op | source)
XLA Modules:
  0.0 75.1 jit_solution(17228243430331263402)
XLA Ops:
  0.6 4.0 %frame_0_0.1 = (bf16[4,2,16,16,128]{4,3,2,1,0:T(8,128)(2,1)S(1)}, bf16[3,512,128]{2,1,0:T(8,128)(2,1)S(1)}, bf16[4,4,16,16,128]{4,3,2,1,0:T(8,128)(2,1)S(1)}, bf16[2,1152,128]{2,1,0:T(8,128)(2,1)S(1)}) custom-call(bf16[1,4,4,16,16,128]{5,4,3,2,1,0:T(8,128)(2,1)} %refs_0_.1, bf16[1,2,1152,128]{3,2,1,0:T(8,128)(2,1)} %refs_1_.1), custom_call_target="tpu_custom_call" | custom-call | flops 603979776 | bytes 1310720 | tf_op jit(solution)/shard_map/frame_0_0/pallas_call | solution.py:231
  4.6 7.1 %collective-permute-start = (bf16[4,2,16,16,128]{4,3,2,1,0:T(8,128)(2,1)S(1)}, bf16[4,2,16,16,128]{4,3,2,1,0:T(8,128)(2,1)S(1)}, u32[]{:S(2)}, u32[]{:S(2)}) collective-permute-start(bf16[4,2,16,16,128]{4,3,2,1,0:T(8,128)(2,1)S(1)} %get-tuple-element.28.refs_0_), channel_id=1, source_target_pairs={{8,0},{9,1},{10,2},{11,3},{12,4},{13,5},{14,6},{15,7},{16,8},{17,9... | collective-permute-start | bytes 1572872 | tf_op jit(solution)/shard_map/ppermute | solution.py:26
  11.7 2.3 %frame_0_1.1 = (bf16[4,2,16,16,128]{4,3,2,1,0:T(8,128)(2,1)S(1)}, bf16[3,512,128]{2,1,0:T(8,128)(2,1)S(1)}) custom-call(bf16[4,4,16,16,128]{4,3,2,1,0:T(8,128)(2,1)S(1)} %get-tuple-element.33.refs_0_, bf16[2,1152,128]{2,1,0:T(8,128)(2,1)S(1)} %get-tuple-element.29.refs_1_.refs_3_), custom_call_target="tpu_custom_call" | custom-call | flops 603979776 | bytes 1310720 | tf_op jit(solution)/shard_map/frame_0_1/pallas_call | solution.py:231
  14.0 2.6 %collective-permute-start.3 = (bf16[4,2,16,16,128]{4,3,2,1,0:T(8,128)(2,1)S(1)}, bf16[4,2,16,16,128]{4,3,2,1,0:T(8,128)(2,1)S(1)}, u32[]{:S(2)}, u32[]{:S(2)}) collective-permute-start(bf16[4,2,16,16,128]{4,3,2,1,0:T(8,128)(2,1)S(1)} %get-tuple-element.34.refs_1_), channel_id=1, source_target_pairs={{8,0},{9,1},{10,2},{11,3},{12,4},{13,5},{14,6},{15,7},{16,8},{17,9... | collective-permute-start | bytes 1572872 | tf_op jit(solution)/shard_map/ppermute | solution.py:26
  16.6 1.8 %collective-permute-done.refs_0_ = bf16[4,2,16,16,128]{4,3,2,1,0:T(8,128)(2,1)S(1)} collective-permute-done((bf16[4,2,16,16,128]{4,3,2,1,0:T(8,128)(2,1)S(1)}, bf16[4,2,16,16,128]{4,3,2,1,0:T(8,128)(2,1)S(1)}, u32[]{:S(2)}, u32[]{:S(2)}) %collective-permute-start) | collective-permute-done | bytes 524320 | tf_op jit(solution)/shard_map/ppermute | solution.py:26
  18.4 2.3 %frame_1_0.1 = (bf16[4,2,16,16,128]{4,3,2,1,0:T(8,128)(2,1)S(1)}, bf16[3,512,128]{2,1,0:T(8,128)(2,1)S(1)}) custom-call(bf16[4,2,16,16,128]{4,3,2,1,0:T(8,128)(2,1)S(1)} %collective-permute-done.refs_0_, bf16[2,1152,128]{2,1,0:T(8,128)(2,1)S(1)} %get-tuple-element.29.refs_1_.refs_3_, bf16[3,4,4,16,16,128]{5,4,3,2,1,0:T(8,128)(2,1)} %refs_2_.11), custom_call_target="tpu_custom_call" | custom-call | flops 603979776 | bytes 1310720 | tf_op jit(solution)/shard_map/frame_1_0/pallas_call | solution.py:231
  20.7 5.9 %collective-permute-start.1 = (bf16[4,2,16,16,128]{4,3,2,1,0:T(8,128)(2,1)S(1)}, bf16[4,2,16,16,128]{4,3,2,1,0:T(8,128)(2,1)S(1)}, u32[]{:S(2)}, u32[]{:S(2)}) collective-permute-start(bf16[4,2,16,16,128]{4,3,2,1,0:T(8,128)(2,1)S(1)} %get-tuple-element.30.refs_0_), channel_id=1, source_target_pairs={{8,0},{9,1},{10,2},{11,3},{12,4},{13,5},{14,6},{15,7},{16,8},{17,9... | collective-permute-start | bytes 1572872 | tf_op jit(solution)/shard_map/ppermute | solution.py:26
  26.7 2.3 %frame_1_1.1 = (bf16[4,2,16,16,128]{4,3,2,1,0:T(8,128)(2,1)S(1)}, bf16[3,512,128]{2,1,0:T(8,128)(2,1)S(1)}) custom-call(bf16[4,2,16,16,128]{4,3,2,1,0:T(8,128)(2,1)S(1)} %collective-permute-done.3.refs_0_, bf16[2,1152,128]{2,1,0:T(8,128)(2,1)S(1)} %get-tuple-element.29.refs_1_.refs_3_, bf16[3,4,4,16,16,128]{5,4,3,2,1,0:T(8,128)(2,1)} %refs_2_.11), custom_call_target="tpu_custom_call" | custom-call | flops 603979776 | bytes 1310720 | tf_op jit(solution)/shard_map/frame_1_1/pallas_call | solution.py:231
  29.0 3.3 %collective-permute-start.4 = (bf16[4,2,16,16,128]{4,3,2,1,0:T(8,128)(2,1)S(1)}, bf16[4,2,16,16,128]{4,3,2,1,0:T(8,128)(2,1)S(1)}, u32[]{:S(2)}, u32[]{:S(2)}) collective-permute-start(bf16[4,2,16,16,128]{4,3,2,1,0:T(8,128)(2,1)S(1)} %get-tuple-element.35.refs_1_), channel_id=1, source_target_pairs={{8,0},{9,1},{10,2},{11,3},{12,4},{13,5},{14,6},{15,7},{16,8},{17,9... | collective-permute-start | bytes 1572872 | tf_op jit(solution)/shard_map/ppermute | solution.py:26
  32.3 1.1 %collective-permute-done.1.refs_0_ = bf16[4,2,16,16,128]{4,3,2,1,0:T(8,128)(2,1)S(1)} collective-permute-done((bf16[4,2,16,16,128]{4,3,2,1,0:T(8,128)(2,1)S(1)}, bf16[4,2,16,16,128]{4,3,2,1,0:T(8,128)(2,1)S(1)}, u32[]{:S(2)}, u32[]{:S(2)}) %collective-permute-start.1) | collective-permute-done | bytes 524320 | tf_op jit(solution)/shard_map/ppermute | solution.py:26
  33.3 2.3 %frame_2_0.1 = (bf16[4,2,16,16,128]{4,3,2,1,0:T(8,128)(2,1)S(1)}, bf16[3,512,128]{2,1,0:T(8,128)(2,1)S(1)}) custom-call(bf16[4,2,16,16,128]{4,3,2,1,0:T(8,128)(2,1)S(1)} %collective-permute-done.1.refs_0_, bf16[2,1152,128]{2,1,0:T(8,128)(2,1)S(1)} %get-tuple-element.29.refs_1_.refs_3_, bf16[3,4,4,16,16,128]{5,4,3,2,1,0:T(8,128)(2,1)} %refs_2_.11), custom_call_target="tpu_custom_call" | custom-call | flops 603979776 | bytes 1310720 | tf_op jit(solution)/shard_map/frame_2_0/pallas_call | solution.py:231
  35.6 5.9 %collective-permute-start.2 = (bf16[4,2,16,16,128]{4,3,2,1,0:T(8,128)(2,1)S(1)}, bf16[4,2,16,16,128]{4,3,2,1,0:T(8,128)(2,1)S(1)}, u32[]{:S(2)}, u32[]{:S(2)}) collective-permute-start(bf16[4,2,16,16,128]{4,3,2,1,0:T(8,128)(2,1)S(1)} %get-tuple-element.31.refs_0_), channel_id=1, source_target_pairs={{8,0},{9,1},{10,2},{11,3},{12,4},{13,5},{14,6},{15,7},{16,8},{17,9... | collective-permute-start | bytes 1572872 | tf_op jit(solution)/shard_map/ppermute | solution.py:26
  41.6 2.3 %frame_2_1.1 = (bf16[4,2,16,16,128]{4,3,2,1,0:T(8,128)(2,1)S(1)}, bf16[3,512,128]{2,1,0:T(8,128)(2,1)S(1)}) custom-call(bf16[4,2,16,16,128]{4,3,2,1,0:T(8,128)(2,1)S(1)} %collective-permute-done.4.refs_0_, bf16[2,1152,128]{2,1,0:T(8,128)(2,1)S(1)} %get-tuple-element.29.refs_1_.refs_3_, bf16[3,4,4,16,16,128]{5,4,3,2,1,0:T(8,128)(2,1)} %refs_2_.11), custom_call_target="tpu_custom_call" | custom-call | flops 603979776 | bytes 1310720 | tf_op jit(solution)/shard_map/frame_2_1/pallas_call | solution.py:231
  43.9 3.5 %collective-permute-start.5 = (bf16[4,2,16,16,128]{4,3,2,1,0:T(8,128)(2,1)S(1)}, bf16[4,2,16,16,128]{4,3,2,1,0:T(8,128)(2,1)S(1)}, u32[]{:S(2)}, u32[]{:S(2)}) collective-permute-start(bf16[4,2,16,16,128]{4,3,2,1,0:T(8,128)(2,1)S(1)} %get-tuple-element.36.refs_1_), channel_id=1, source_target_pairs={{8,0},{9,1},{10,2},{11,3},{12,4},{13,5},{14,6},{15,7},{16,8},{17,9... | collective-permute-start | bytes 1572872 | tf_op jit(solution)/shard_map/ppermute | solution.py:26
  48.3 1.0 %grads_1.1.refs_4_ = f32[2,128,1152]{2,1,0:T(8,128)S(1)} custom-call(bf16[4,2,16,16,128]{4,3,2,1,0:T(8,128)(2,1)S(1)} %get-tuple-element.30.refs_0_, bf16[4,2,16,16,128]{4,3,2,1,0:T(8,128)(2,1)S(1)} %get-tuple-element.35.refs_1_, bf16[3,512,128]{2,1,0:T(8,128)(2,1)S(1)} %get-tuple-element.42.refs_2_, bf16[3,512,128]{2,1,0:T(8,128)(2,1)S(1)} %get-tuple-element.43.refs_3_, ...), custom_call_target="tpu_custom_call" | custom-call | flops 603979776 | bytes 2359296 | tf_op jit(solution)/shard_map/grads_1/pallas_call | solution.py:298
  50.4 2.3 %frame_3_0.1 = (bf16[4,2,16,16,128]{4,3,2,1,0:T(8,128)(2,1)S(1)}, bf16[3,512,128]{2,1,0:T(8,128)(2,1)S(1)}) custom-call(bf16[4,2,16,16,128]{4,3,2,1,0:T(8,128)(2,1)S(1)} %collective-permute-done.2.refs_0_, bf16[2,1152,128]{2,1,0:T(8,128)(2,1)S(1)} %get-tuple-element.29.refs_1_.refs_3_, bf16[3,4,4,16,16,128]{5,4,3,2,1,0:T(8,128)(2,1)} %refs_2_.11), custom_call_target="tpu_custom_call" | custom-call | flops 603979776 | bytes 1310720 | tf_op jit(solution)/shard_map/frame_3_0/pallas_call | solution.py:231
  53.9 1.4 %frame_3_1.1 = (bf16[4,2,16,16,128]{4,3,2,1,0:T(8,128)(2,1)S(1)}, bf16[3,512,128]{2,1,0:T(8,128)(2,1)S(1)}) custom-call(bf16[4,2,16,16,128]{4,3,2,1,0:T(8,128)(2,1)S(1)} %collective-permute-done.5.refs_0_, bf16[2,1152,128]{2,1,0:T(8,128)(2,1)S(1)} %get-tuple-element.29.refs_1_.refs_3_, bf16[3,4,4,16,16,128]{5,4,3,2,1,0:T(8,128)(2,1)} %refs_2_.11), custom_call_target="tpu_custom_call" | custom-call | flops 603979776 | bytes 1310720 | tf_op jit(solution)/shard_map/frame_3_1/pallas_call | solution.py:231
  56.0 4.5 %collective-permute-start.10 = (bf16[2,144,128]{2,1,0:T(8,128)(2,1)S(1)}, bf16[2,144,128]{2,1,0:T(8,128)(2,1)S(1)}, u32[]{:S(2)}, u32[]{:S(2)}) collective-permute-start(bf16[2,144,128]{2,1,0:T(8,128)(2,1)S(1)} %get-tuple-element.51), channel_id=1, source_target_pairs={{0,5},{1,4},{2,7},{3,6},{4,1},{5,0},{6,3},{7,2},{8,13},{9,12},{10,... | collective-permute-start | bytes 221192 | tf_op jit(solution)/shard_map/ppermute | solution.py:385
  60.5 1.6 %collective-permute-start.11 = (bf16[2,144,128]{2,1,0:T(8,128)(2,1)S(1)}, bf16[2,144,128]{2,1,0:T(8,128)(2,1)S(1)}, u32[]{:S(2)}, u32[]{:S(2)}) collective-permute-start(bf16[2,144,128]{2,1,0:T(8,128)(2,1)S(1)} %get-tuple-element.52), channel_id=1, source_target_pairs={{0,6},{1,7},{2,4},{3,5},{4,2},{5,3},{6,0},{7,1},{8,14},{9,15},{10,... | collective-permute-start | bytes 221192 | tf_op jit(solution)/shard_map/ppermute | solution.py:385
  62.1 2.5 %collective-permute-start.12 = (bf16[2,144,128]{2,1,0:T(8,128)(2,1)S(1)}, bf16[2,144,128]{2,1,0:T(8,128)(2,1)S(1)}, u32[]{:S(2)}, u32[]{:S(2)}) collective-permute-start(bf16[2,144,128]{2,1,0:T(8,128)(2,1)S(1)} %get-tuple-element.53), channel_id=1, source_target_pairs={{0,7},{1,6},{2,5},{3,4},{4,3},{5,2},{6,1},{7,0},{8,15},{9,14},{10,... | collective-permute-start | bytes 221192 | tf_op jit(solution)/shard_map/ppermute | solution.py:385
  64.8 3.9 %collective-permute-start.7 = (bf16[2,144,128]{2,1,0:T(8,128)(2,1)S(1)}, bf16[2,144,128]{2,1,0:T(8,128)(2,1)S(1)}, u32[]{:S(2)}, u32[]{:S(2)}) collective-permute-start(bf16[2,144,128]{2,1,0:T(8,128)(2,1)S(1)} %get-tuple-element.48), channel_id=1, source_target_pairs={{0,2},{1,3},{2,0},{3,1},{4,6},{5,7},{6,4},{7,5},{8,10},{9,11},{10,... | collective-permute-start | bytes 221192 | tf_op jit(solution)/shard_map/ppermute | solution.py:385
  69.4 1.2 %finish.1 = bf16[1,4,4,16,16,128]{5,4,3,2,1,0:T(8,128)(2,1)} custom-call(bf16[4,2,16,16,128]{4,3,2,1,0:T(8,128)(2,1)S(1)} %get-tuple-element.32.refs_0_, bf16[4,2,16,16,128]{4,3,2,1,0:T(8,128)(2,1)S(1)} %get-tuple-element.37.refs_1_.refs_0_, bf16[3,512,128]{2,1,0:T(8,128)(2,1)S(1)} %get-tuple-element.38.refs_2_.refs_1_, ...), custom_call_target="tpu_custom_call" | custom-call | flops 134217728 | bytes 1048576 | tf_op jit(solution)/shard_map/finish/pallas_call | solution.py:337
  70.6 1.3 %collective-permute-done.7.refs_2_ = bf16[2,144,128]{2,1,0:T(8,128)(2,1)S(1)} collective-permute-done((bf16[2,144,128]{2,1,0:T(8,128)(2,1)S(1)}, bf16[2,144,128]{2,1,0:T(8,128)(2,1)S(1)}, u32[]{:S(2)}, u32[]{:S(2)}) %collective-permute-start.7) | collective-permute-done | bytes 73760 | tf_op jit(solution)/shard_map/ppermute | solution.py:385
  71.9 2.5 %collective-permute-done.8.refs_3_ = bf16[2,144,128]{2,1,0:T(8,128)(2,1)S(1)} collective-permute-done((bf16[2,144,128]{2,1,0:T(8,128)(2,1)S(1)}, bf16[2,144,128]{2,1,0:T(8,128)(2,1)S(1)}, u32[]{:S(2)}, u32[]{:S(2)}) %collective-permute-start.8) | collective-permute-done | bytes 73760 | tf_op jit(solution)/shard_map/ppermute | solution.py:385
  (19 shorter events, 5.5 us)
Async XLA Ops:
  4.6 13.8 %collective-permute-start = (bf16[4,2,16,16,128]{4,3,2,1,0:T(8,128)(2,1)S(1)}, bf16[4,2,16,16,128]{4,3,2,1,0:T(8,128)(2,1)S(1)}, u32[]{:S(2)}, u32[]{:S(2)}) collective-permute-start(bf16[4,2,16,16,128]{4,3,2,1,0:T(8,128)(2,1)S(1)} %get-tuple-element.28.refs_0_), channel_id=1, source_target_pairs={{8,0},{9,1},{10,2},{11,3},{12,4},{13,5},{14,6},{15,7},{16,8},{17,9... | collective-permute-start | bytes 1572872 | tf_op jit(solution)/shard_map/ppermute | solution.py:26
  14.0 12.6 %collective-permute-start.3 = (bf16[4,2,16,16,128]{4,3,2,1,0:T(8,128)(2,1)S(1)}, bf16[4,2,16,16,128]{4,3,2,1,0:T(8,128)(2,1)S(1)}, u32[]{:S(2)}, u32[]{:S(2)}) collective-permute-start(bf16[4,2,16,16,128]{4,3,2,1,0:T(8,128)(2,1)S(1)} %get-tuple-element.34.refs_1_), channel_id=1, source_target_pairs={{8,0},{9,1},{10,2},{11,3},{12,4},{13,5},{14,6},{15,7},{16,8},{17,9... | collective-permute-start | bytes 1572872 | tf_op jit(solution)/shard_map/ppermute | solution.py:26
  20.7 12.6 %collective-permute-start.1 = (bf16[4,2,16,16,128]{4,3,2,1,0:T(8,128)(2,1)S(1)}, bf16[4,2,16,16,128]{4,3,2,1,0:T(8,128)(2,1)S(1)}, u32[]{:S(2)}, u32[]{:S(2)}) collective-permute-start(bf16[4,2,16,16,128]{4,3,2,1,0:T(8,128)(2,1)S(1)} %get-tuple-element.30.refs_0_), channel_id=1, source_target_pairs={{8,0},{9,1},{10,2},{11,3},{12,4},{13,5},{14,6},{15,7},{16,8},{17,9... | collective-permute-start | bytes 1572872 | tf_op jit(solution)/shard_map/ppermute | solution.py:26
  29.0 12.6 %collective-permute-start.4 = (bf16[4,2,16,16,128]{4,3,2,1,0:T(8,128)(2,1)S(1)}, bf16[4,2,16,16,128]{4,3,2,1,0:T(8,128)(2,1)S(1)}, u32[]{:S(2)}, u32[]{:S(2)}) collective-permute-start(bf16[4,2,16,16,128]{4,3,2,1,0:T(8,128)(2,1)S(1)} %get-tuple-element.35.refs_1_), channel_id=1, source_target_pairs={{8,0},{9,1},{10,2},{11,3},{12,4},{13,5},{14,6},{15,7},{16,8},{17,9... | collective-permute-start | bytes 1572872 | tf_op jit(solution)/shard_map/ppermute | solution.py:26
  35.6 14.7 %collective-permute-start.2 = (bf16[4,2,16,16,128]{4,3,2,1,0:T(8,128)(2,1)S(1)}, bf16[4,2,16,16,128]{4,3,2,1,0:T(8,128)(2,1)S(1)}, u32[]{:S(2)}, u32[]{:S(2)}) collective-permute-start(bf16[4,2,16,16,128]{4,3,2,1,0:T(8,128)(2,1)S(1)} %get-tuple-element.31.refs_0_), channel_id=1, source_target_pairs={{8,0},{9,1},{10,2},{11,3},{12,4},{13,5},{14,6},{15,7},{16,8},{17,9... | collective-permute-start | bytes 1572872 | tf_op jit(solution)/shard_map/ppermute | solution.py:26
  43.9 10.0 %collective-permute-start.5 = (bf16[4,2,16,16,128]{4,3,2,1,0:T(8,128)(2,1)S(1)}, bf16[4,2,16,16,128]{4,3,2,1,0:T(8,128)(2,1)S(1)}, u32[]{:S(2)}, u32[]{:S(2)}) collective-permute-start(bf16[4,2,16,16,128]{4,3,2,1,0:T(8,128)(2,1)S(1)} %get-tuple-element.36.refs_1_), channel_id=1, source_target_pairs={{8,0},{9,1},{10,2},{11,3},{12,4},{13,5},{14,6},{15,7},{16,8},{17,9... | collective-permute-start | bytes 1572872 | tf_op jit(solution)/shard_map/ppermute | solution.py:26
  56.0 12.8 %collective-permute-start.10 = (bf16[2,144,128]{2,1,0:T(8,128)(2,1)S(1)}, bf16[2,144,128]{2,1,0:T(8,128)(2,1)S(1)}, u32[]{:S(2)}, u32[]{:S(2)}) collective-permute-start(bf16[2,144,128]{2,1,0:T(8,128)(2,1)S(1)} %get-tuple-element.51), channel_id=1, source_target_pairs={{0,5},{1,4},{2,7},{3,6},{4,1},{5,0},{6,3},{7,2},{8,13},{9,12},{10,... | collective-permute-start | bytes 221192 | tf_op jit(solution)/shard_map/ppermute | solution.py:385
  60.5 8.8 %collective-permute-start.11 = (bf16[2,144,128]{2,1,0:T(8,128)(2,1)S(1)}, bf16[2,144,128]{2,1,0:T(8,128)(2,1)S(1)}, u32[]{:S(2)}, u32[]{:S(2)}) collective-permute-start(bf16[2,144,128]{2,1,0:T(8,128)(2,1)S(1)} %get-tuple-element.52), channel_id=1, source_target_pairs={{0,6},{1,7},{2,4},{3,5},{4,2},{5,3},{6,0},{7,1},{8,14},{9,15},{10,... | collective-permute-start | bytes 221192 | tf_op jit(solution)/shard_map/ppermute | solution.py:385
  62.1 8.5 %collective-permute-start.12 = (bf16[2,144,128]{2,1,0:T(8,128)(2,1)S(1)}, bf16[2,144,128]{2,1,0:T(8,128)(2,1)S(1)}, u32[]{:S(2)}, u32[]{:S(2)}) collective-permute-start(bf16[2,144,128]{2,1,0:T(8,128)(2,1)S(1)} %get-tuple-element.53), channel_id=1, source_target_pairs={{0,7},{1,6},{2,5},{3,4},{4,3},{5,2},{6,1},{7,0},{8,15},{9,14},{10,... | collective-permute-start | bytes 221192 | tf_op jit(solution)/shard_map/ppermute | solution.py:385
  64.6 6.0 %collective-permute-start.6 = (bf16[2,144,128]{2,1,0:T(8,128)(2,1)S(1)}, bf16[2,144,128]{2,1,0:T(8,128)(2,1)S(1)}, u32[]{:S(2)}, u32[]{:S(2)}) collective-permute-start(bf16[2,144,128]{2,1,0:T(8,128)(2,1)S(1)} %get-tuple-element.47), channel_id=1, source_target_pairs={{0,1},{1,0},{2,3},{3,2},{4,5},{5,4},{6,7},{7,6},{8,9},{9,8},{10,11... | collective-permute-start | bytes 221192 | tf_op jit(solution)/shard_map/ppermute | solution.py:385
  64.8 7.1 %collective-permute-start.7 = (bf16[2,144,128]{2,1,0:T(8,128)(2,1)S(1)}, bf16[2,144,128]{2,1,0:T(8,128)(2,1)S(1)}, u32[]{:S(2)}, u32[]{:S(2)}) collective-permute-start(bf16[2,144,128]{2,1,0:T(8,128)(2,1)S(1)} %get-tuple-element.48), channel_id=1, source_target_pairs={{0,2},{1,3},{2,0},{3,1},{4,6},{5,7},{6,4},{7,5},{8,10},{9,11},{10,... | collective-permute-start | bytes 221192 | tf_op jit(solution)/shard_map/ppermute | solution.py:385
  68.8 5.6 %collective-permute-start.8 = (bf16[2,144,128]{2,1,0:T(8,128)(2,1)S(1)}, bf16[2,144,128]{2,1,0:T(8,128)(2,1)S(1)}, u32[]{:S(2)}, u32[]{:S(2)}) collective-permute-start(bf16[2,144,128]{2,1,0:T(8,128)(2,1)S(1)} %get-tuple-element.49), channel_id=1, source_target_pairs={{0,3},{1,2},{2,1},{3,0},{4,7},{5,6},{6,5},{7,4},{8,11},{9,10},{10,... | collective-permute-start | bytes 221192 | tf_op jit(solution)/shard_map/ppermute | solution.py:385
  69.3 5.1 %copy-start = (f32[1,2,144,128]{3,2,1,0:T(8,128)S(1)}, f32[1,2,144,128]{3,2,1,0:T(8,128)}, u32[]{:S(2)}) copy-start(f32[1,2,144,128]{3,2,1,0:T(8,128)} %mom_ref.1) | copy-start | bytes 442372
  69.3 5.1 %collective-permute-start.9 = (bf16[2,144,128]{2,1,0:T(8,128)(2,1)S(1)}, bf16[2,144,128]{2,1,0:T(8,128)(2,1)S(1)}, u32[]{:S(2)}, u32[]{:S(2)}) collective-permute-start(bf16[2,144,128]{2,1,0:T(8,128)(2,1)S(1)} %get-tuple-element.50), channel_id=1, source_target_pairs={{0,4},{1,5},{2,6},{3,7},{4,0},{5,1},{6,2},{7,3},{8,12},{9,13},{10,... | collective-permute-start | bytes 221192 | tf_op jit(solution)/shard_map/ppermute | solution.py:385

commit v3 on v1

v3 whole, which is shorter than its diff:
```python
import functools

import jax
import jax.numpy as jnp
from jax import lax
from jax.experimental import pallas as pl
from jax.experimental.pallas import tpu as pltpu
from jax.sharding import PartitionSpec as P


TICKS = 4
TAPS = 3
CHUNKS = ((0, 2), (2, 2))
GRANT = 16 << 20
ORDER = (6, 5, 7, 4, 2, 3, 1)
F32, BF16 = jnp.float32, jnp.bfloat16


def passed_along(value, slot):
    count, replicas = lax.axis_size("segment"), lax.axis_size("dp")
    half, swap, per = count // 2, replicas // 2, len(CHUNKS)

    def pairs(sections, tick):
        crossing = {half} | ({half + 1} if tick < TICKS - 2 else set())
        crossing |= {half - 1} if tick == 1 else set()
        return [
            (s * replicas + d, (s - 1) * replicas + (d ^ swap if s in crossing else d))
            for s in sections
            for d in range(replicas)
        ]

    sent = per * (TICKS - 1)
    near, over = [], None
    if slot < sent:
        near += pairs(range(half + 1, count), slot // per)
        over = lax.ppermute(value, ("segment", "dp"), pairs([half], slot // per))
    if 0 < slot <= sent:
        near += pairs(range(1, half), (slot - 1) // per)
    return lax.ppermute(value, ("segment", "dp"), near), over


def tap(w, a, b):
    chans = w.shape[1]
    first = (TAPS * a + b) * chans
    return w[first : first + chans, :]


def sides(value, wid):
    half = wid // 2
    pair = value.reshape(-1, 2, half, value.shape[-1])
    low, high = pair[:, 0], pair[:, 1]
    at = lax.broadcasted_iota(jnp.int32, low.shape, 1)
    moved = [pltpu.roll(part, 1, 1) for part in (low, high)]
    before = [jnp.where(at == 0, 0.0, moved[0]), jnp.where(at == 0, moved[0], moved[1])]
    moved = [pltpu.roll(part, half - 1, 1) for part in (low, high)]
    after = [
        jnp.where(at == half - 1, moved[1], moved[0]),
        jnp.where(at == half - 1, 0.0, moved[1]),
    ]
    return tuple(jnp.stack(parts, axis=1).reshape(value.shape) for parts in (before, after))


def windows(pad, count, hgt):
    return pad[:, count : count + hgt].reshape(-1, pad.shape[-1])


def conv(pad_ref, w, wid):
    hgt, chans = pad_ref.shape[1] - 2, pad_ref.shape[-1]
    field = pad_ref[...]
    lhs = jnp.concatenate([windows(field, a, hgt) for a in range(TAPS)], axis=1)
    rhs = jnp.concatenate(
        [jnp.concatenate([tap(w, a, b) for b in range(TAPS)], axis=1) for a in range(TAPS)], axis=0
    )
    out = jnp.dot(lhs, rhs, preferred_element_type=F32)
    left, mid, right = (out[:, b * chans : (b + 1) * chans] for b in range(TAPS))
    return sides(left, wid)[0] + mid + sides(right, wid)[1]


def conv_back(pads_ref, w):
    hgt = pads_ref.shape[2] - 2
    lhs = jnp.concatenate(
        [windows(pads_ref[b], a, hgt) for a in range(TAPS) for b in range(TAPS)], axis=1
    )
    rhs = jnp.concatenate(
        [tap(w, TAPS - 1 - a, TAPS - 1 - b) for a in range(TAPS) for b in range(TAPS)], axis=1
    )
    return lax.dot_general(lhs, rhs, (((1,), (1,)), ((), ())), preferred_element_type=F32)


def grad_of(field, pads_ref):
    hgt = pads_ref.shape[2] - 2
    cols = jnp.concatenate(
        [
            windows(pads_ref[TAPS - 1 - b], TAPS - 1 - a, hgt)
            for a in range(TAPS)
            for b in range(TAPS)
        ],
        axis=1,
    )
    return lax.dot_general(field, cols, (((0,), (0,)), ((), ())), preferred_element_type=F32)


def put_field(pad_ref, value):
    frames, tall, wid, chans = pad_ref.shape
    pad_ref[:, 1 : tall - 1] = value.reshape(frames, tall - 2, wid, chans)


def put_slope(pads_ref, slope, wid):
    before, after = sides(slope, wid)
    put_field(pads_ref.at[0], before.astype(BF16))
    put_field(pads_ref.at[1], slope.astype(BF16))
    put_field(pads_ref.at[2], after.astype(BF16))


def clear_edges(pads_ref):
    tall = pads_ref.shape[-3]
    lead = pads_ref.shape[:-3]
    zero = jnp.zeros(lead + (1,) + pads_ref.shape[-2:], BF16)
    at = (slice(None),) * len(lead)
    pads_ref[at + (slice(0, 1),)] = zero
    pads_ref[at + (slice(tall - 1, tall),)] = zero


def slopes(act):
    sig = jax.nn.sigmoid(act)
    out = act * sig
    return out, sig + (out - out * sig)


def fetched(src, dst, sem):
    copy = pltpu.make_async_copy(src, dst, sem)
    copy.start()
    return copy


def places():
    me = lax.axis_index("segment")
    half = lax.axis_size("segment") // 2
    return me < half, me == half - 1, me == lax.axis_size("segment") - 1


def frame_kernel(slot, *refs):
    per, frames = len(CHUNKS), CHUNKS[0][1]
    refs = list(refs)
    opening, last = slot == 0, slot == TICKS * per
    late, joint, newest = places()
    if opening:
        src_ref, w_in = refs[:2]
        out_ref, sum_ref, whole_ref, w_ref, xpad, xpad2, zpads, zpads2, sems = refs[2:]
    else:
        w_ref, acc_ref = refs[:2]
        del refs[:2]
        whole_ref = refs.pop(0) if slot <= per else None
        near_ref = refs.pop(0) if slot >= per else None
        over_ref = refs.pop(0) if slot > per else None
        fresh_ref = refs.pop(0) if per <= slot < TICKS * per else None
        out_ref = refs.pop(0)
        if last:
            kept_ref, full_ref = refs.pop(0), refs.pop()
            pieces = [refs.pop(0) for _ in range(lax.axis_size("dp"))]
        else:
            sum_ref = refs.pop(0)
        xpad, xpad2, zpads, zpads2 = refs[:4]
        if fresh_ref is not None:
            fbuf, sem = refs[4:]

            @pl.when(newest)
            def _():
                at = pl.ds(frames * (slot % per), frames)
                fetched(fresh_ref.at[slot // per - 1, :, at], fbuf, sem).wait()

    hgt, wid, chans = out_ref.shape[2:]
    shape = (frames, hgt, wid, chans)
    if opening:
        at = pl.ds(0, frames)
        first = [
            fetched(src_ref.at[0, n, at], whole_ref.at[n, at], sems.at[n]) for n in (0, 1, 3, 2)
        ]
        wg = fetched(w_in.at[0, 1], w_ref.at[1], sems.at[4])
        wf = fetched(w_in.at[0, 0], w_ref.at[0], sems.at[5])
        later = pl.ds(frames, src_ref.shape[2] - frames)
        rest = fetched(src_ref.at[0, :, later], whole_ref.at[:, later], sems.at[6])

    def part(n):
        if opening:
            value = whole_ref[n, :frames]
        elif slot < per:
            at = pl.multiple_of(frames * (slot - late.astype(jnp.int32)), frames)
            value = whole_ref[n, pl.ds(at, frames)]
        else:
            value = near_ref[n]
            if fresh_ref is not None:
                value = jnp.where(newest, fbuf[n], value)
            if slot == per:
                value = jnp.where(late, whole_ref[n, frames * (per - 1) :], value)
            else:
                value = jnp.where(joint, over_ref[n], value)
        return value.reshape(-1, chans)

    def work():
        for pad in (xpad, xpad2, zpads, zpads2):
            clear_edges(pad)
        if opening:
            first[0].wait()
            wg.wait()
        w_g = w_ref[1]
        y_one = part(0)
        put_field(xpad, y_one)
        act, slope = slopes(conv(xpad, w_g, wid))
        if opening:
            for copy in first[1:]:
                copy.wait()
        x_two = (part(1).astype(F32) - act).astype(BF16)
        put_field(xpad2, x_two)
        out_ref[1] = x_two.reshape(shape)
        put_slope(zpads, part(3).astype(F32) * slope, wid)
        dx_one = (part(2).astype(F32) + conv_back(zpads, w_g)).astype(BF16)
        out_ref[2] = dx_one.reshape(shape)

        if opening:
            wf.wait()
        w_f = w_ref[0]
        act = conv(xpad2, w_f, wid)
        sum_g = grad_of(y_one, zpads)
        if not opening:
            sum_g = sum_g + acc_ref[1]
        if not last:
            sum_ref[1] = sum_g
        act, slope = slopes(act)
        out_ref[0] = (y_one.astype(F32) - act).astype(BF16).reshape(shape)
        put_slope(zpads2, dx_one.astype(F32) * slope, wid)
        sum_f = grad_of(x_two, zpads2)
        if not opening:
            sum_f = sum_f + acc_ref[0]
        if last:
            kept_ref[...] = windows(zpads2[1], 1, hgt)
            out_ref[3] = part(3).reshape(shape)
            spread(full_ref, sum_f, sum_g)
        else:
            sum_ref[0] = sum_f
            dx_two = part(3).astype(F32) + conv_back(zpads2, w_f)
            out_ref[3] = dx_two.astype(BF16).reshape(shape)

    def spread(full_ref, sum_f, sum_g):
        for b in range(TAPS * TAPS):
            at = slice(b * chans, (b + 1) * chans)
            full_ref[0, at] = sum_f[:, at]
            full_ref[1, at] = sum_g[:, at]

    if opening:

        @pl.when(late)
        def _():
            sum_ref[...] = jnp.zeros_like(sum_ref)
            for copy in (*first, wg, wf):
                copy.wait()

        pl.when(jnp.logical_not(late))(work)
        rest.wait()
    elif last:
        pl.when(late)(work)

        @pl.when(jnp.logical_not(late))
        def _():
            spread(full_ref, acc_ref[0], acc_ref[1])

        me = lax.axis_index("dp")
        rows = pieces[0].shape[1]
        for k, ref in enumerate(pieces):
            begins = pl.multiple_of((me ^ k) * rows, 16)
            ref[...] = full_ref[:, pl.ds(begins, rows)].astype(ref.dtype)
    else:
        work()


VMEM_SPEC = pl.BlockSpec(memory_space=pltpu.VMEM)
HBM_SPEC = pl.BlockSpec(memory_space=pltpu.HBM)


def in_hbm(value):
    return pltpu.with_memory_space_constraint(value, pltpu.HBM)


def pads(frames, tall, wid, chans, lead=()):
    return pltpu.VMEM(lead + (frames, tall, wid, chans), BF16)


def frame_step(slot, incoming, fresh, weights, acc, whole, near, over):
    per, frames = len(CHUNKS), CHUNKS[0][1]
    hgt, wid, chans = incoming.shape[-3:]
    rows = weights.shape[-2]
    opening, last = slot == 0, slot == TICKS * per
    cells = frames * hgt * wid
    outs = [jax.ShapeDtypeStruct((4, frames, hgt, wid, chans), BF16)]
    tall = hgt + 2
    scratch = [pads(frames, tall, wid, chans)] * 2 + [pads(frames, tall, wid, chans, (TAPS,))] * 2
    if last:
        replicas = lax.axis_size("dp")
        outs.append(jax.ShapeDtypeStruct((cells, chans), BF16))
        outs += [
            jax.ShapeDtypeStruct((2, rows // replicas, chans), BF16 if k else F32)
            for k in range(replicas)
        ]
    else:
        outs.append(jax.ShapeDtypeStruct((2, chans, rows), F32))
    if opening:
        args = [in_hbm(incoming), in_hbm(weights)]
        specs = [HBM_SPEC] * 2
        outs.append(jax.ShapeDtypeStruct(incoming.shape[1:], BF16))
        outs.append(jax.ShapeDtypeStruct(weights.shape[1:], BF16))
        scratch.append(pltpu.SemaphoreType.DMA((7,)))
    else:
        args = [weights, acc]
        args += [whole] if slot <= per else []
        args += [near] if slot >= per else []
        args += [over] if slot > per else []
        specs = [VMEM_SPEC] * len(args)
        if per <= slot < TICKS * per:
            args.append(in_hbm(fresh))
            specs.append(HBM_SPEC)
            scratch += [pads(frames, hgt, wid, chans, (4,)), pltpu.SemaphoreType.DMA]
        if last:
            scratch.append(pltpu.VMEM((2, rows, chans), F32))
    return pl.pallas_call(
        functools.partial(frame_kernel, slot),
        out_shape=outs,
        in_specs=specs,
        out_specs=[VMEM_SPEC] * len(outs),
        scratch_shapes=scratch,
        compiler_params=pltpu.CompilerParams(vmem_limit_bytes=GRANT),
        cost_estimate=pl.CostEstimate(
            flops=12 * cells * rows * chans, bytes_accessed=10 * cells * chans * 2, transcendentals=0
        ),
    )(*args)


def finish_kernel(early_ref, mid_ref, end_ref, kept_ref, w_ref, whole_ref, zpads, sems):
    late, _, _ = places()
    _, hgt, wid, chans = end_ref.shape[1:]
    firsts = [pl.ds(*chunk) for chunk in CHUNKS]

    @pl.when(jnp.logical_not(late))
    def _():
        one = fetched(early_ref, whole_ref.at[0, :, firsts[0]], sems.at[0])
        two = fetched(mid_ref, whole_ref.at[0, :, firsts[1]], sems.at[1])
        one.wait()
        two.wait()

    @pl.when(late)
    def _():
        one = fetched(mid_ref, whole_ref.at[0, :, firsts[0]], sems.at[0])
        two = fetched(end_ref.at[:3], whole_ref.at[0, :3, firsts[1]], sems.at[1])
        clear_edges(zpads)
        put_slope(zpads, kept_ref[...].astype(F32), wid)
        dx_two = end_ref[3].reshape(-1, chans).astype(F32) + conv_back(zpads, w_ref[0])
        put_field(zpads.at[0], dx_two.astype(BF16))
        three = fetched(
            zpads.at[0, :, pl.ds(1, hgt)], whole_ref.at[0, 3, firsts[1]], sems.at[2]
        )
        one.wait()
        two.wait()
        three.wait()


def finish(early, mid, end, kept, weights, frames):
    hgt, wid, chans = end.shape[2:]
    args = [early, mid, end, kept, weights]
    return pl.pallas_call(
        finish_kernel,
        out_shape=jax.ShapeDtypeStruct((1, 4, frames, hgt, wid, chans), BF16),
        in_specs=[VMEM_SPEC] * len(args),
        out_specs=HBM_SPEC,
        scratch_shapes=[
            pads(end.shape[1], hgt + 2, wid, chans, (TAPS,)),
            pltpu.SemaphoreType.DMA((3,)),
        ],
        compiler_params=pltpu.CompilerParams(vmem_limit_bytes=GRANT),
        cost_estimate=pl.CostEstimate(flops=1 << 27, bytes_accessed=1 << 20, transcendentals=0),
        name="finish",
    )(*args)


def momentum_kernel(scale, mom_ref, *refs):
    out_ref = refs[-1]
    total = refs[0][...]
    for ref in refs[1:-1]:
        total = total + ref[...].astype(F32)
    out_ref[0] = 0.9 * mom_ref[0] + total * scale


def shards(incoming, fresh, weights, momentum):
    replicas = lax.axis_size("dp")
    frames = incoming.shape[2]
    per = len(CHUNKS)
    whole = acc = None
    wts = weights
    outs, nears, overs = [], [], []
    for slot in range(TICKS * per + 1):
        near = nears[slot - per] if slot >= per else None
        over = overs[slot - per - 1] if slot > per else None
        got = frame_step(slot, incoming, fresh, wts, acc, whole, near, over)
        outs.append(got[0])
        acc = got[1]
        if slot == 0:
            whole, wts = got[2:]
        if slot <= per * (TICKS - 1):
            near, over = passed_along(got[0], slot)
            nears.append(near)
            overs.append(over)
    kept, *pieces = got[1:]
    terms = [pieces[0]] + [
        lax.ppermute(pieces[k], "dp", [(d, d ^ k) for d in range(replicas)]) for k in ORDER
    ]
    outgoing = finish(*outs[-3:], kept, wts, frames)
    new_momentum = pl.pallas_call(
        functools.partial(momentum_kernel, 1.0 / (TICKS * frames * replicas)),
        out_shape=jax.ShapeDtypeStruct(momentum.shape, F32),
        in_specs=[VMEM_SPEC] * (1 + replicas),
        out_specs=VMEM_SPEC,
        compiler_params=pltpu.CompilerParams(vmem_limit_bytes=GRANT),
        name="momentum",
    )(momentum, *terms)
    return (outgoing, new_momentum)


def solution(mesh):
    return jax.shard_map(
        shards,
        mesh=mesh,
        in_specs=(
            P("segment", None, "dp", None, None, None),
            P(None, None, "dp", None, None, None),
            P("segment", None, None, None),
            P("segment", None, "dp", None),
        ),
        out_specs=(P("segment", None, "dp", None, None, None), P("segment", None, "dp", None)),
        check_vma=False,
    )
```

time: 84.2 us -> 73.1 us (0.87)
  local copies, waits for them, and re-layouts: 7.56 us -> 0.01 us
  other arithmetic: 2.73 us -> 0 us
  waiting for transfers between devices: 8.02 us -> 6.06 us
  Pallas kernels: 21.9 us -> 23 us
    unnamed x26 -> x2, local copies, waits for them, and re-layouts: 7.49 us -> 0.01 us
    broadcast_in_dim x2 -> x0, other arithmetic: 2.73 us -> none  [shards(): return (jnp.concatenate(outs, axis=1)[None], new_momentum[None])]
    ppermute x13 -> x20, waiting for transfers between devices: 8.02 us -> 6.06 us  [the longest x7 2.84 us: shards(): lax.ppermute(pieces[k], 'dp', [(d, d ^ k) for d in range(replicas)])]
    pallas_call x8 -> x11, Pallas kernels: 21.9 us -> 23 us  [the longest x9 21.2 us: frame_step(): pl.pallas_call(functools.partial(frame_kernel, slot), out_shape=outs, in_...]
    ppermute x13 -> x20, starting transfers between devices: 42.6 us -> 41.9 us  [the longest x6 21.2 us: passed_along(): over = lax.ppermute(value, ('segment', 'dp'), pairs([half], slot // per))]
  transfers between devices with their start and end apart: 13 -> 20, of which waited for: 6 -> 6; matrix products, arithmetic and copies ran while one was open for 1% -> 0% of each run, Pallas kernels for 20% -> 25%
where the time goes in v3:
time: 73.1 us; the launch traced here: 71.9 us
  starting transfers between devices  41.9 us (57%)
  Pallas kernels  23 us (31%)
  waiting for transfers between devices  6.06 us (8%)
  between operations  0.9 us (1%)
    pallas_call x9, Pallas kernels, frame_step(): pl.pallas_call(functools.partial(frame_kernel, slot), out_shape=outs, in_...  21.2 us
    ppermute x6, starting transfers between devices, passed_along(): over = lax.ppermute(value, ('segment', 'dp'), pairs([half], slot // per))  21.2 us
    ppermute x7, starting transfers between devices, shards(): lax.ppermute(pieces[k], 'dp', [(d, d ^ k) for d in range(replicas)])  12.2 us
    ppermute x7, starting transfers between devices, passed_along(): return (lax.ppermute(value, ('segment', 'dp'), near), over)  8.45 us
    ppermute x7, waiting for transfers between devices, shards(): lax.ppermute(pieces[k], 'dp', [(d, d ^ k) for d in range(replicas)])  2.84 us
    ppermute x6, waiting for transfers between devices, passed_along(): over = lax.ppermute(value, ('segment', 'dp'), pairs([half], slot // per))  2.24 us
  transfers between devices with their start and end apart: 20, of which 6 were waited for; matrix products, arithmetic and copies ran while one was open for 0% of the time, Pallas kernels for 25%

profile of v3, /device:TPU:16, one launch (start us, length us, event | category | flops | bytes accessed | tf_op | source)
XLA Modules:
  0.0 71.9 jit_solution(13012526363347530579)
XLA Ops:
  0.6 4.3 %shard_map.59 = (bf16[4,2,16,16,128]{4,3,2,1,0:T(8,128)(2,1)S(1)}, f32[2,128,1152]{2,1,0:T(8,128)S(1)}, bf16[4,4,16,16,128]{4,3,2,1,0:T(8,128)(2,1)S(1)}, bf16[2,1152,128]{2,1,0:T(8,128)(2,1)S(1)}) custom-call(bf16[1,4,4,16,16,128]{5,4,3,2,1,0:T(8,128)(2,1)} %refs_0_.1, bf16[1,2,1152,128]{3,2,1,0:T(8,128)(2,1)} %refs_1_.1), custom_call_target="tpu_custom_call" | custom-call | flops 905969664 | bytes 1310720 | tf_op jit(solution)/shard_map/pallas_call | solution.py:324
  4.9 1.3 %collective-permute-start = (bf16[4,2,16,16,128]{4,3,2,1,0:T(8,128)(2,1)S(1)}, bf16[4,2,16,16,128]{4,3,2,1,0:T(8,128)(2,1)S(1)}, u32[]{:S(2)}, u32[]{:S(2)}) collective-permute-start(bf16[4,2,16,16,128]{4,3,2,1,0:T(8,128)(2,1)S(1)} %get-tuple-element.34), channel_id=1, source_target_pairs={{136,132},{137,133},{138,134},{139,135},{140,128},{141,129},{142,1... | collective-permute-start | bytes 1572872 | tf_op jit(solution)/shard_map/ppermute | solution.py:39
  6.2 2.4 %shard_map.60 = (bf16[4,2,16,16,128]{4,3,2,1,0:T(8,128)(2,1)S(1)}, f32[2,128,1152]{2,1,0:T(8,128)S(1)}) custom-call(bf16[2,1152,128]{2,1,0:T(8,128)(2,1)S(1)} %get-tuple-element.30.refs_0_.w_ref, f32[2,128,1152]{2,1,0:T(8,128)S(1)} %get-tuple-element.31.refs_1_, bf16[4,4,16,16,128]{4,3,2,1,0:T(8,128)(2,1)S(1)} %get-tuple-element.32.refs_2_), custom_call_target="tpu_custom_call" | custom-call | flops 905969664 | bytes 1310720 | tf_op jit(solution)/shard_map/pallas_call | solution.py:324
  8.6 1.3 %collective-permute-start.1 = (bf16[4,2,16,16,128]{4,3,2,1,0:T(8,128)(2,1)S(1)}, bf16[4,2,16,16,128]{4,3,2,1,0:T(8,128)(2,1)S(1)}, u32[]{:S(2)}, u32[]{:S(2)}) collective-permute-start(bf16[4,2,16,16,128]{4,3,2,1,0:T(8,128)(2,1)S(1)} %get-tuple-element.36), channel_id=1, source_target_pairs={{136,132},{137,133},{138,134},{139,135},{140,128},{141,129},{142,1... | collective-permute-start | bytes 1572872 | tf_op jit(solution)/shard_map/ppermute | solution.py:39
  9.9 5.1 %collective-permute-start.2 = (bf16[4,2,16,16,128]{4,3,2,1,0:T(8,128)(2,1)S(1)}, bf16[4,2,16,16,128]{4,3,2,1,0:T(8,128)(2,1)S(1)}, u32[]{:S(2)}, u32[]{:S(2)}) collective-permute-start(bf16[4,2,16,16,128]{4,3,2,1,0:T(8,128)(2,1)S(1)} %get-tuple-element.34), channel_id=1, source_target_pairs={{128,124},{129,125},{130,126},{131,127},{132,120},{133,121},{134,1... | collective-permute-start | bytes 1572872 | tf_op jit(solution)/shard_map/ppermute | solution.py:36
  15.0 1.3 %collective-permute-start.4 = (bf16[4,2,16,16,128]{4,3,2,1,0:T(8,128)(2,1)S(1)}, bf16[4,2,16,16,128]{4,3,2,1,0:T(8,128)(2,1)S(1)}, u32[]{:S(2)}, u32[]{:S(2)}) collective-permute-start(bf16[4,2,16,16,128]{4,3,2,1,0:T(8,128)(2,1)S(1)} %get-tuple-element.36), channel_id=1, source_target_pairs={{128,124},{129,125},{130,126},{131,127},{132,120},{133,121},{134,1... | collective-permute-start | bytes 1572872 | tf_op jit(solution)/shard_map/ppermute | solution.py:36
  16.3 2.4 %shard_map.61 = (bf16[4,2,16,16,128]{4,3,2,1,0:T(8,128)(2,1)S(1)}, f32[2,128,1152]{2,1,0:T(8,128)S(1)}) custom-call(bf16[2,1152,128]{2,1,0:T(8,128)(2,1)S(1)} %get-tuple-element.30.refs_0_.w_ref, f32[2,128,1152]{2,1,0:T(8,128)S(1)} %get-tuple-element.33.refs_1_, bf16[4,4,16,16,128]{4,3,2,1,0:T(8,128)(2,1)S(1)} %get-tuple-element.32.refs_2_, ...), custom_call_target="tpu_custom_call" | custom-call | flops 905969664 | bytes 1310720 | tf_op jit(solution)/shard_map/pallas_call | solution.py:324
  18.8 1.3 %collective-permute-start.3 = (bf16[4,2,16,16,128]{4,3,2,1,0:T(8,128)(2,1)S(1)}, bf16[4,2,16,16,128]{4,3,2,1,0:T(8,128)(2,1)S(1)}, u32[]{:S(2)}, u32[]{:S(2)}) collective-permute-start(bf16[4,2,16,16,128]{4,3,2,1,0:T(8,128)(2,1)S(1)} %get-tuple-element.38), channel_id=1, source_target_pairs={{136,132},{137,133},{138,134},{139,135},{140,128},{141,129},{142,1... | collective-permute-start | bytes 1572872 | tf_op jit(solution)/shard_map/ppermute | solution.py:39
  21.6 2.4 %shard_map.62 = (bf16[4,2,16,16,128]{4,3,2,1,0:T(8,128)(2,1)S(1)}, f32[2,128,1152]{2,1,0:T(8,128)S(1)}) custom-call(bf16[2,1152,128]{2,1,0:T(8,128)(2,1)S(1)} %get-tuple-element.30.refs_0_.w_ref, f32[2,128,1152]{2,1,0:T(8,128)S(1)} %get-tuple-element.35.refs_1_, bf16[4,2,16,16,128]{4,3,2,1,0:T(8,128)(2,1)S(1)} %collective-permute-done.1.refs_2_, ...), custom_call_target="tpu_custom_call" | custom-call | flops 905969664 | bytes 1310720 | tf_op jit(solution)/shard_map/pallas_call | solution.py:324
  25.4 6.0 %collective-permute-start.6 = (bf16[4,2,16,16,128]{4,3,2,1,0:T(8,128)(2,1)S(1)}, bf16[4,2,16,16,128]{4,3,2,1,0:T(8,128)(2,1)S(1)}, u32[]{:S(2)}, u32[]{:S(2)}) collective-permute-start(bf16[4,2,16,16,128]{4,3,2,1,0:T(8,128)(2,1)S(1)} %get-tuple-element.38), channel_id=1, source_target_pairs={{128,124},{129,125},{130,126},{131,127},{132,120},{133,121},{134,1... | collective-permute-start | bytes 1572872 | tf_op jit(solution)/shard_map/ppermute | solution.py:36
  31.3 1.3 %collective-permute-start.8 = (bf16[4,2,16,16,128]{4,3,2,1,0:T(8,128)(2,1)S(1)}, bf16[4,2,16,16,128]{4,3,2,1,0:T(8,128)(2,1)S(1)}, u32[]{:S(2)}, u32[]{:S(2)}) collective-permute-start(bf16[4,2,16,16,128]{4,3,2,1,0:T(8,128)(2,1)S(1)} %get-tuple-element.40), channel_id=1, source_target_pairs={{128,124},{129,125},{130,126},{131,127},{132,120},{133,121},{134,1... | collective-permute-start | bytes 1572872 | tf_op jit(solution)/shard_map/ppermute | solution.py:36
  32.7 2.4 %shard_map.63 = (bf16[4,2,16,16,128]{4,3,2,1,0:T(8,128)(2,1)S(1)}, f32[2,128,1152]{2,1,0:T(8,128)S(1)}) custom-call(bf16[2,1152,128]{2,1,0:T(8,128)(2,1)S(1)} %get-tuple-element.30.refs_0_.w_ref, f32[2,128,1152]{2,1,0:T(8,128)S(1)} %get-tuple-element.37.refs_1_, bf16[4,2,16,16,128]{4,3,2,1,0:T(8,128)(2,1)S(1)} %collective-permute-done.3.refs_2_, ...), custom_call_target="tpu_custom_call" | custom-call | flops 905969664 | bytes 1310720 | tf_op jit(solution)/shard_map/pallas_call | solution.py:324
  35.1 1.3 %collective-permute-start.7 = (bf16[4,2,16,16,128]{4,3,2,1,0:T(8,128)(2,1)S(1)}, bf16[4,2,16,16,128]{4,3,2,1,0:T(8,128)(2,1)S(1)}, u32[]{:S(2)}, u32[]{:S(2)}) collective-permute-start(bf16[4,2,16,16,128]{4,3,2,1,0:T(8,128)(2,1)S(1)} %get-tuple-element.42), channel_id=1, source_target_pairs={{136,128},{137,129},{138,130},{139,131},{140,132},{141,133},{142,1... | collective-permute-start | bytes 1572872 | tf_op jit(solution)/shard_map/ppermute | solution.py:39
  36.4 1.5 %collective-permute-start.10 = (bf16[4,2,16,16,128]{4,3,2,1,0:T(8,128)(2,1)S(1)}, bf16[4,2,16,16,128]{4,3,2,1,0:T(8,128)(2,1)S(1)}, u32[]{:S(2)}, u32[]{:S(2)}) collective-permute-start(bf16[4,2,16,16,128]{4,3,2,1,0:T(8,128)(2,1)S(1)} %get-tuple-element.42), channel_id=1, source_target_pairs={{128,124},{129,125},{130,126},{131,127},{132,120},{133,121},{134,1... | collective-permute-start | bytes 1572872 | tf_op jit(solution)/shard_map/ppermute | solution.py:36
  38.0 2.4 %shard_map.64 = (bf16[4,2,16,16,128]{4,3,2,1,0:T(8,128)(2,1)S(1)}, f32[2,128,1152]{2,1,0:T(8,128)S(1)}) custom-call(bf16[2,1152,128]{2,1,0:T(8,128)(2,1)S(1)} %get-tuple-element.30.refs_0_.w_ref, f32[2,128,1152]{2,1,0:T(8,128)S(1)} %get-tuple-element.39.refs_1_, bf16[4,2,16,16,128]{4,3,2,1,0:T(8,128)(2,1)S(1)} %collective-permute-done.5.refs_2_, ...), custom_call_target="tpu_custom_call" | custom-call | flops 905969664 | bytes 1310720 | tf_op jit(solution)/shard_map/pallas_call | solution.py:324
  40.4 1.3 %collective-permute-start.9 = (bf16[4,2,16,16,128]{4,3,2,1,0:T(8,128)(2,1)S(1)}, bf16[4,2,16,16,128]{4,3,2,1,0:T(8,128)(2,1)S(1)}, u32[]{:S(2)}, u32[]{:S(2)}) collective-permute-start(bf16[4,2,16,16,128]{4,3,2,1,0:T(8,128)(2,1)S(1)} %get-tuple-element.45), channel_id=1, source_target_pairs={{136,128},{137,129},{138,130},{139,131},{140,132},{141,133},{142,1... | collective-permute-start | bytes 1572872 | tf_op jit(solution)/shard_map/ppermute | solution.py:39
  41.7 6.0 %collective-permute-start.12 = (bf16[4,2,16,16,128]{4,3,2,1,0:T(8,128)(2,1)S(1)}, bf16[4,2,16,16,128]{4,3,2,1,0:T(8,128)(2,1)S(1)}, u32[]{:S(2)}, u32[]{:S(2)}) collective-permute-start(bf16[4,2,16,16,128]{4,3,2,1,0:T(8,128)(2,1)S(1)} %get-tuple-element.45), channel_id=1, source_target_pairs={{128,124},{129,125},{130,126},{131,127},{132,120},{133,121},{134,1... | collective-permute-start | bytes 1572872 | tf_op jit(solution)/shard_map/ppermute | solution.py:36
  47.7 2.4 %shard_map.65 = (bf16[4,2,16,16,128]{4,3,2,1,0:T(8,128)(2,1)S(1)}, f32[2,128,1152]{2,1,0:T(8,128)S(1)}) custom-call(bf16[2,1152,128]{2,1,0:T(8,128)(2,1)S(1)} %get-tuple-element.30.refs_0_.w_ref, f32[2,128,1152]{2,1,0:T(8,128)S(1)} %get-tuple-element.41.refs_1_, bf16[4,2,16,16,128]{4,3,2,1,0:T(8,128)(2,1)S(1)} %collective-permute-done.7.refs_2_, ...), custom_call_target="tpu_custom_call" | custom-call | flops 905969664 | bytes 1310720 | tf_op jit(solution)/shard_map/pallas_call | solution.py:324
  50.9 2.4 %shard_map.66 = (bf16[4,2,16,16,128]{4,3,2,1,0:T(8,128)(2,1)S(1)}, f32[2,128,1152]{2,1,0:T(8,128)S(1)}) custom-call(bf16[2,1152,128]{2,1,0:T(8,128)(2,1)S(1)} %get-tuple-element.30.refs_0_.w_ref, f32[2,128,1152]{2,1,0:T(8,128)S(1)} %get-tuple-element.44.refs_1_, bf16[4,2,16,16,128]{4,3,2,1,0:T(8,128)(2,1)S(1)} %collective-permute-done.9.refs_2_, ...), custom_call_target="tpu_custom_call" | custom-call | flops 905969664 | bytes 1310720 | tf_op jit(solution)/shard_map/pallas_call | solution.py:324
  53.3 1.6 %collective-permute-done.12.refs_3_ = bf16[4,2,16,16,128]{4,3,2,1,0:T(8,128)(2,1)S(1)} collective-permute-done((bf16[4,2,16,16,128]{4,3,2,1,0:T(8,128)(2,1)S(1)}, bf16[4,2,16,16,128]{4,3,2,1,0:T(8,128)(2,1)S(1)}, u32[]{:S(2)}, u32[]{:S(2)}) %collective-permute-start.12) | collective-permute-done | bytes 524320 | tf_op jit(solution)/shard_map/ppermute | solution.py:36
  55.0 5.5 %collective-permute-start.13 = (bf16[2,144,128]{2,1,0:T(8,128)(2,1)S(1)}, bf16[2,144,128]{2,1,0:T(8,128)(2,1)S(1)}, u32[]{:S(2)}, u32[]{:S(2)}) collective-permute-start(bf16[2,144,128]{2,1,0:T(8,128)(2,1)S(1)} %get-tuple-element.51), channel_id=1, source_target_pairs={{0,6},{1,7},{2,4},{3,5},{4,2},{5,3},{6,0},{7,1},{8,14},{9,15},{10,... | collective-permute-start | bytes 221192 | tf_op jit(solution)/shard_map/ppermute | solution.py:412
  60.5 2.0 %collective-permute-start.15 = (bf16[2,144,128]{2,1,0:T(8,128)(2,1)S(1)}, bf16[2,144,128]{2,1,0:T(8,128)(2,1)S(1)}, u32[]{:S(2)}, u32[]{:S(2)}) collective-permute-start(bf16[2,144,128]{2,1,0:T(8,128)(2,1)S(1)} %get-tuple-element.53), channel_id=1, source_target_pairs={{0,7},{1,6},{2,5},{3,4},{4,3},{5,2},{6,1},{7,0},{8,15},{9,14},{10,... | collective-permute-start | bytes 221192 | tf_op jit(solution)/shard_map/ppermute | solution.py:412
  63.1 2.4 %collective-permute-start.17 = (bf16[2,144,128]{2,1,0:T(8,128)(2,1)S(1)}, bf16[2,144,128]{2,1,0:T(8,128)(2,1)S(1)}, u32[]{:S(2)}, u32[]{:S(2)}) collective-permute-start(bf16[2,144,128]{2,1,0:T(8,128)(2,1)S(1)} %get-tuple-element.55), channel_id=1, source_target_pairs={{0,2},{1,3},{2,0},{3,1},{4,6},{5,7},{6,4},{7,5},{8,10},{9,11},{10,... | collective-permute-start | bytes 221192 | tf_op jit(solution)/shard_map/ppermute | solution.py:412
  69.3 1.8 %collective-permute-done.18.refs_6_ = bf16[2,144,128]{2,1,0:T(8,128)(2,1)S(1)} collective-permute-done((bf16[2,144,128]{2,1,0:T(8,128)(2,1)S(1)}, bf16[2,144,128]{2,1,0:T(8,128)(2,1)S(1)}, u32[]{:S(2)}, u32[]{:S(2)}) %collective-permute-start.18) | collective-permute-done | bytes 73760 | tf_op jit(solution)/shard_map/ppermute | solution.py:412
  (29 shorter events, 8.9 us)
Async XLA Ops:
  4.9 11.4 %collective-permute-start = (bf16[4,2,16,16,128]{4,3,2,1,0:T(8,128)(2,1)S(1)}, bf16[4,2,16,16,128]{4,3,2,1,0:T(8,128)(2,1)S(1)}, u32[]{:S(2)}, u32[]{:S(2)}) collective-permute-start(bf16[4,2,16,16,128]{4,3,2,1,0:T(8,128)(2,1)S(1)} %get-tuple-element.34), channel_id=1, source_target_pairs={{136,132},{137,133},{138,134},{139,135},{140,128},{141,129},{142,1... | collective-permute-start | bytes 1572872 | tf_op jit(solution)/shard_map/ppermute | solution.py:39
  8.6 12.5 %collective-permute-start.1 = (bf16[4,2,16,16,128]{4,3,2,1,0:T(8,128)(2,1)S(1)}, bf16[4,2,16,16,128]{4,3,2,1,0:T(8,128)(2,1)S(1)}, u32[]{:S(2)}, u32[]{:S(2)}) collective-permute-start(bf16[4,2,16,16,128]{4,3,2,1,0:T(8,128)(2,1)S(1)} %get-tuple-element.36), channel_id=1, source_target_pairs={{136,132},{137,133},{138,134},{139,135},{140,128},{141,129},{142,1... | collective-permute-start | bytes 1572872 | tf_op jit(solution)/shard_map/ppermute | solution.py:39
  9.9 11.8 %collective-permute-start.2 = (bf16[4,2,16,16,128]{4,3,2,1,0:T(8,128)(2,1)S(1)}, bf16[4,2,16,16,128]{4,3,2,1,0:T(8,128)(2,1)S(1)}, u32[]{:S(2)}, u32[]{:S(2)}) collective-permute-start(bf16[4,2,16,16,128]{4,3,2,1,0:T(8,128)(2,1)S(1)} %get-tuple-element.34), channel_id=1, source_target_pairs={{128,124},{129,125},{130,126},{131,127},{132,120},{133,121},{134,1... | collective-permute-start | bytes 1572872 | tf_op jit(solution)/shard_map/ppermute | solution.py:36
  15.0 17.7 %collective-permute-start.4 = (bf16[4,2,16,16,128]{4,3,2,1,0:T(8,128)(2,1)S(1)}, bf16[4,2,16,16,128]{4,3,2,1,0:T(8,128)(2,1)S(1)}, u32[]{:S(2)}, u32[]{:S(2)}) collective-permute-start(bf16[4,2,16,16,128]{4,3,2,1,0:T(8,128)(2,1)S(1)} %get-tuple-element.36), channel_id=1, source_target_pairs={{128,124},{129,125},{130,126},{131,127},{132,120},{133,121},{134,1... | collective-permute-start | bytes 1572872 | tf_op jit(solution)/shard_map/ppermute | solution.py:36
  18.8 13.9 %collective-permute-start.3 = (bf16[4,2,16,16,128]{4,3,2,1,0:T(8,128)(2,1)S(1)}, bf16[4,2,16,16,128]{4,3,2,1,0:T(8,128)(2,1)S(1)}, u32[]{:S(2)}, u32[]{:S(2)}) collective-permute-start(bf16[4,2,16,16,128]{4,3,2,1,0:T(8,128)(2,1)S(1)} %get-tuple-element.38), channel_id=1, source_target_pairs={{136,132},{137,133},{138,134},{139,135},{140,128},{141,129},{142,1... | collective-permute-start | bytes 1572872 | tf_op jit(solution)/shard_map/ppermute | solution.py:39
  24.1 13.9 %collective-permute-start.5 = (bf16[4,2,16,16,128]{4,3,2,1,0:T(8,128)(2,1)S(1)}, bf16[4,2,16,16,128]{4,3,2,1,0:T(8,128)(2,1)S(1)}, u32[]{:S(2)}, u32[]{:S(2)}) collective-permute-start(bf16[4,2,16,16,128]{4,3,2,1,0:T(8,128)(2,1)S(1)} %get-tuple-element.40), channel_id=1, source_target_pairs={{136,132},{137,133},{138,134},{139,135},{140,128},{141,129},{142,1... | collective-permute-start | bytes 1572872 | tf_op jit(solution)/shard_map/ppermute | solution.py:39
  25.4 12.6 %collective-permute-start.6 = (bf16[4,2,16,16,128]{4,3,2,1,0:T(8,128)(2,1)S(1)}, bf16[4,2,16,16,128]{4,3,2,1,0:T(8,128)(2,1)S(1)}, u32[]{:S(2)}, u32[]{:S(2)}) collective-permute-start(bf16[4,2,16,16,128]{4,3,2,1,0:T(8,128)(2,1)S(1)} %get-tuple-element.38), channel_id=1, source_target_pairs={{128,124},{129,125},{130,126},{131,127},{132,120},{133,121},{134,1... | collective-permute-start | bytes 1572872 | tf_op jit(solution)/shard_map/ppermute | solution.py:36
  31.3 16.4 %collective-permute-start.8 = (bf16[4,2,16,16,128]{4,3,2,1,0:T(8,128)(2,1)S(1)}, bf16[4,2,16,16,128]{4,3,2,1,0:T(8,128)(2,1)S(1)}, u32[]{:S(2)}, u32[]{:S(2)}) collective-permute-start(bf16[4,2,16,16,128]{4,3,2,1,0:T(8,128)(2,1)S(1)} %get-tuple-element.40), channel_id=1, source_target_pairs={{128,124},{129,125},{130,126},{131,127},{132,120},{133,121},{134,1... | collective-permute-start | bytes 1572872 | tf_op jit(solution)/shard_map/ppermute | solution.py:36
  35.1 12.6 %collective-permute-start.7 = (bf16[4,2,16,16,128]{4,3,2,1,0:T(8,128)(2,1)S(1)}, bf16[4,2,16,16,128]{4,3,2,1,0:T(8,128)(2,1)S(1)}, u32[]{:S(2)}, u32[]{:S(2)}) collective-permute-start(bf16[4,2,16,16,128]{4,3,2,1,0:T(8,128)(2,1)S(1)} %get-tuple-element.42), channel_id=1, source_target_pairs={{136,128},{137,129},{138,130},{139,131},{140,132},{141,133},{142,1... | collective-permute-start | bytes 1572872 | tf_op jit(solution)/shard_map/ppermute | solution.py:39
  36.4 14.4 %collective-permute-start.10 = (bf16[4,2,16,16,128]{4,3,2,1,0:T(8,128)(2,1)S(1)}, bf16[4,2,16,16,128]{4,3,2,1,0:T(8,128)(2,1)S(1)}, u32[]{:S(2)}, u32[]{:S(2)}) collective-permute-start(bf16[4,2,16,16,128]{4,3,2,1,0:T(8,128)(2,1)S(1)} %get-tuple-element.42), channel_id=1, source_target_pairs={{128,124},{129,125},{130,126},{131,127},{132,120},{133,121},{134,1... | collective-permute-start | bytes 1572872 | tf_op jit(solution)/shard_map/ppermute | solution.py:36
  40.4 10.4 %collective-permute-start.9 = (bf16[4,2,16,16,128]{4,3,2,1,0:T(8,128)(2,1)S(1)}, bf16[4,2,16,16,128]{4,3,2,1,0:T(8,128)(2,1)S(1)}, u32[]{:S(2)}, u32[]{:S(2)}) collective-permute-start(bf16[4,2,16,16,128]{4,3,2,1,0:T(8,128)(2,1)S(1)} %get-tuple-element.45), channel_id=1, source_target_pairs={{136,128},{137,129},{138,130},{139,131},{140,132},{141,133},{142,1... | collective-permute-start | bytes 1572872 | tf_op jit(solution)/shard_map/ppermute | solution.py:39
  41.7 13.1 %collective-permute-start.12 = (bf16[4,2,16,16,128]{4,3,2,1,0:T(8,128)(2,1)S(1)}, bf16[4,2,16,16,128]{4,3,2,1,0:T(8,128)(2,1)S(1)}, u32[]{:S(2)}, u32[]{:S(2)}) collective-permute-start(bf16[4,2,16,16,128]{4,3,2,1,0:T(8,128)(2,1)S(1)} %get-tuple-element.45), channel_id=1, source_target_pairs={{128,124},{129,125},{130,126},{131,127},{132,120},{133,121},{134,1... | collective-permute-start | bytes 1572872 | tf_op jit(solution)/shard_map/ppermute | solution.py:36
  50.1 4.7 %collective-permute-start.11 = (bf16[4,2,16,16,128]{4,3,2,1,0:T(8,128)(2,1)S(1)}, bf16[4,2,16,16,128]{4,3,2,1,0:T(8,128)(2,1)S(1)}, u32[]{:S(2)}, u32[]{:S(2)}) collective-permute-start(bf16[4,2,16,16,128]{4,3,2,1,0:T(8,128)(2,1)S(1)} %get-tuple-element.43.early_ref), channel_id=1, source_target_pairs={{8,0},{9,1},{10,2},{11,3},{12,4},{13,5},{14,6},{15,7},{16,8},{17,9... | collective-permute-start | bytes 1572872 | tf_op jit(solution)/shard_map/ppermute | solution.py:39
  55.0 10.5 %collective-permute-start.13 = (bf16[2,144,128]{2,1,0:T(8,128)(2,1)S(1)}, bf16[2,144,128]{2,1,0:T(8,128)(2,1)S(1)}, u32[]{:S(2)}, u32[]{:S(2)}) collective-permute-start(bf16[2,144,128]{2,1,0:T(8,128)(2,1)S(1)} %get-tuple-element.51), channel_id=1, source_target_pairs={{0,6},{1,7},{2,4},{3,5},{4,2},{5,3},{6,0},{7,1},{8,14},{9,15},{10,... | collective-permute-start | bytes 221192 | tf_op jit(solution)/shard_map/ppermute | solution.py:412
  60.5 6.2 %collective-permute-start.14 = (bf16[2,144,128]{2,1,0:T(8,128)(2,1)S(1)}, bf16[2,144,128]{2,1,0:T(8,128)(2,1)S(1)}, u32[]{:S(2)}, u32[]{:S(2)}) collective-permute-start(bf16[2,144,128]{2,1,0:T(8,128)(2,1)S(1)} %get-tuple-element.52), channel_id=1, source_target_pairs={{0,5},{1,4},{2,7},{3,6},{4,1},{5,0},{6,3},{7,2},{8,13},{9,12},{10,... | collective-permute-start | bytes 221192 | tf_op jit(solution)/shard_map/ppermute | solution.py:412
  60.5 7.7 %collective-permute-start.15 = (bf16[2,144,128]{2,1,0:T(8,128)(2,1)S(1)}, bf16[2,144,128]{2,1,0:T(8,128)(2,1)S(1)}, u32[]{:S(2)}, u32[]{:S(2)}) collective-permute-start(bf16[2,144,128]{2,1,0:T(8,128)(2,1)S(1)} %get-tuple-element.53), channel_id=1, source_target_pairs={{0,7},{1,6},{2,5},{3,4},{4,3},{5,2},{6,1},{7,0},{8,15},{9,14},{10,... | collective-permute-start | bytes 221192 | tf_op jit(solution)/shard_map/ppermute | solution.py:412
  62.5 5.8 %collective-permute-start.16 = (bf16[2,144,128]{2,1,0:T(8,128)(2,1)S(1)}, bf16[2,144,128]{2,1,0:T(8,128)(2,1)S(1)}, u32[]{:S(2)}, u32[]{:S(2)}) collective-permute-start(bf16[2,144,128]{2,1,0:T(8,128)(2,1)S(1)} %get-tuple-element.54), channel_id=1, source_target_pairs={{0,4},{1,5},{2,6},{3,7},{4,0},{5,1},{6,2},{7,3},{8,12},{9,13},{10,... | collective-permute-start | bytes 221192 | tf_op jit(solution)/shard_map/ppermute | solution.py:412
  63.1 6.1 %collective-permute-start.17 = (bf16[2,144,128]{2,1,0:T(8,128)(2,1)S(1)}, bf16[2,144,128]{2,1,0:T(8,128)(2,1)S(1)}, u32[]{:S(2)}, u32[]{:S(2)}) collective-permute-start(bf16[2,144,128]{2,1,0:T(8,128)(2,1)S(1)} %get-tuple-element.55), channel_id=1, source_target_pairs={{0,2},{1,3},{2,0},{3,1},{4,6},{5,7},{6,4},{7,5},{8,10},{9,11},{10,... | collective-permute-start | bytes 221192 | tf_op jit(solution)/shard_map/ppermute | solution.py:412
  65.5 5.6 %collective-permute-start.18 = (bf16[2,144,128]{2,1,0:T(8,128)(2,1)S(1)}, bf16[2,144,128]{2,1,0:T(8,128)(2,1)S(1)}, u32[]{:S(2)}, u32[]{:S(2)}) collective-permute-start(bf16[2,144,128]{2,1,0:T(8,128)(2,1)S(1)} %get-tuple-element.56), channel_id=1, source_target_pairs={{0,3},{1,2},{2,1},{3,0},{4,7},{5,6},{6,5},{7,4},{8,11},{9,10},{10,... | collective-permute-start | bytes 221192 | tf_op jit(solution)/shard_map/ppermute | solution.py:412
  66.7 4.4 %collective-permute-start.19 = (bf16[2,144,128]{2,1,0:T(8,128)(2,1)S(1)}, bf16[2,144,128]{2,1,0:T(8,128)(2,1)S(1)}, u32[]{:S(2)}, u32[]{:S(2)}) collective-permute-start(bf16[2,144,128]{2,1,0:T(8,128)(2,1)S(1)} %get-tuple-element.57), channel_id=1, source_target_pairs={{0,1},{1,0},{2,3},{3,2},{4,5},{5,4},{6,7},{7,6},{8,9},{9,8},{10,11... | collective-permute-start | bytes 221192 | tf_op jit(solution)/shard_map/ppermute | solution.py:412
  67.2 3.9 %copy-start = (f32[1,2,144,128]{3,2,1,0:T(8,128)S(1)}, f32[1,2,144,128]{3,2,1,0:T(8,128)}, u32[]{:S(2)}) copy-start(f32[1,2,144,128]{3,2,1,0:T(8,128)} %mom_ref.1) | copy-start | bytes 442372

commit v4 on v3

--- a/solution.py
+++ b/solution.py
@@ -146,10 +146,10 @@
     late, joint, newest = places()
     if opening:
         src_ref, w_in = refs[:2]
-        out_ref, sum_ref, whole_ref, w_ref, xpad, xpad2, zpads, zpads2, sems = refs[2:]
+        out_ref, ys_ref, zpads, zpads2, whole_ref, w_ref, xpad, xpad2, sems = refs[2:]
     else:
-        w_ref, acc_ref = refs[:2]
-        del refs[:2]
+        w_ref = refs.pop(0)
+        acc_ref = refs.pop(0) if last else None
         whole_ref = refs.pop(0) if slot <= per else None
         near_ref = refs.pop(0) if slot >= per else None
         over_ref = refs.pop(0) if slot > per else None
@@ -158,11 +158,13 @@
         if last:
             kept_ref, full_ref = refs.pop(0), refs.pop()
             pieces = [refs.pop(0) for _ in range(lax.axis_size("dp"))]
+            zpads, zpads2 = refs.pop(), refs.pop()
         else:
-            sum_ref = refs.pop(0)
-        xpad, xpad2, zpads, zpads2 = refs[:4]
+            ys_ref, zpads, zpads2 = refs[:3]
+            del refs[:3]
+        xpad, xpad2 = refs[:2]
         if fresh_ref is not None:
-            fbuf, sem = refs[4:]
+            fbuf, sem = refs[2:]
 
             @pl.when(newest)
             def _():
@@ -170,7 +172,7 @@
                 fetched(fresh_ref.at[slot // per - 1, :, at], fbuf, sem).wait()
 
     hgt, wid, chans = out_ref.shape[2:]
-    shape = (frames, hgt, wid, chans)
+    shape = (hgt, wid, chans)
     if opening:
         at = pl.ds(0, frames)
         first = [
@@ -181,65 +183,73 @@
         later = pl.ds(frames, src_ref.shape[2] - frames)
         rest = fetched(src_ref.at[0, :, later], whole_ref.at[:, later], sems.at[6])
 
-    def part(n):
+    def part(n, f):
         if opening:
-            value = whole_ref[n, :frames]
+            value = whole_ref[n, f]
         elif slot < per:
-            at = pl.multiple_of(frames * (slot - late.astype(jnp.int32)), frames)
-            value = whole_ref[n, pl.ds(at, frames)]
+            value = whole_ref[n, frames * (slot - late.astype(jnp.int32)) + f]
         else:
-            value = near_ref[n]
+            value = near_ref[n, f]
             if fresh_ref is not None:
-                value = jnp.where(newest, fbuf[n], value)
+                value = jnp.where(newest, fbuf[n, f], value)
             if slot == per:
-                value = jnp.where(late, whole_ref[n, frames * (per - 1) :], value)
+                value = jnp.where(late, whole_ref[n, frames * (per - 1) + f], value)
             else:
-                value = jnp.where(joint, over_ref[n], value)
+                value = jnp.where(joint, over_ref[n, f], value)
         return value.reshape(-1, chans)
 
     def work():
+        each = range(frames)
         for pad in (xpad, xpad2, zpads, zpads2):
             clear_edges(pad)
         if opening:
             first[0].wait()
             wg.wait()
         w_g = w_ref[1]
-        y_one = part(0)
-        put_field(xpad, y_one)
-        act, slope = slopes(conv(xpad, w_g, wid))
+        y_one = [part(0, f) for f in each]
+        for f in each:
+            put_field(one(xpad, f), y_one[f])
+            if not last:
+                ys_ref[pl.ds(f * hgt * wid, hgt * wid)] = y_one[f]
+        acts = [conv(one(xpad, f), w_g, wid) for f in each]
         if opening:
             for copy in first[1:]:
                 copy.wait()
-        x_two = (part(1).astype(F32) - act).astype(BF16)
-        put_field(xpad2, x_two)
-        out_ref[1] = x_two.reshape(shape)
-        put_slope(zpads, part(3).astype(F32) * slope, wid)
-        dx_one = (part(2).astype(F32) + conv_back(zpads, w_g)).astype(BF16)
-        out_ref[2] = dx_one.reshape(shape)
-
+        x_two = []
+        for f in each:
+            act, slope = slopes(acts[f])
+            x_two.append((part(1, f).astype(F32) - act).astype(BF16))
+            put_field(one(xpad2, f), x_two[f])
+            out_ref[1, f] = x_two[f].reshape(shape)
+            put_slope(zpads.at[:, pl.ds(f, 1)], part(3, f).astype(F32) * slope, wid)
         if opening:
             wf.wait()
         w_f = w_ref[0]
-        act = conv(xpad2, w_f, wid)
-        sum_g = grad_of(y_one, zpads)
-        if not opening:
-            sum_g = sum_g + acc_ref[1]
+        dx_one, acts = [], []
+        for f in each:
+            back = conv_back(zpads.at[:, pl.ds(f, 1)], w_g)
+            acts.append(conv(one(xpad2, f), w_f, wid))
+            dx_one.append((part(2, f).astype(F32) + back).astype(BF16))
+            out_ref[2, f] = dx_one[f].reshape(shape)
+        if last:
+            sum_g = acc_ref[1] + grad_of(jnp.concatenate(y_one, axis=0), zpads)
+        for f in each:
+            act, slope = slopes(acts[f])
+            out_ref[0, f] = (y_one[f].astype(F32) - act).astype(BF16).reshape(shape)
+            put_slope(zpads2.at[:, pl.ds(f, 1)], dx_one[f].astype(F32) * slope, wid)
         if not last:
-            sum_ref[1] = sum_g
-        act, slope = slopes(act)
-        out_ref[0] = (y_one.astype(F32) - act).astype(BF16).reshape(shape)
-        put_slope(zpads2, dx_one.astype(F32) * slope, wid)
-        sum_f = grad_of(x_two, zpads2)
-        if not opening:
-            sum_f = sum_f + acc_ref[0]
+            for f in each:
+                dx_two = part(3, f).astype(F32) + conv_back(zpads2.at[:, pl.ds(f, 1)], w_f)
+                out_ref[3, f] = dx_two.astype(BF16).reshape(shape)
         if last:
+            sum_f = acc_ref[0] + grad_of(jnp.concatenate(x_two, axis=0), zpads2)
             kept_ref[...] = windows(zpads2[1], 1, hgt)
-            out_ref[3] = part(3).reshape(shape)
+            for f in each:
+                out_ref[3, f] = part(3, f).reshape(shape)
             spread(full_ref, sum_f, sum_g)
-        else:
-            sum_ref[0] = sum_f
-            dx_two = part(3).astype(F32) + conv_back(zpads2, w_f)
-            out_ref[3] = dx_two.astype(BF16).reshape(shape)
+
+    def one(pad, f):
+        return pad.at[pl.ds(f, 1)]
 
     def spread(full_ref, sum_f, sum_g):
         for b in range(TAPS * TAPS):
@@ -251,7 +261,6 @@
 
         @pl.when(late)
         def _():
-            sum_ref[...] = jnp.zeros_like(sum_ref)
             for copy in (*first, wg, wf):
                 copy.wait()
 
@@ -293,7 +302,7 @@
     cells = frames * hgt * wid
     outs = [jax.ShapeDtypeStruct((4, frames, hgt, wid, chans), BF16)]
     tall = hgt + 2
-    scratch = [pads(frames, tall, wid, chans)] * 2 + [pads(frames, tall, wid, chans, (TAPS,))] * 2
+    scratch = [pads(frames, tall, wid, chans)] * 2
     if last:
         replicas = lax.axis_size("dp")
         outs.append(jax.ShapeDtypeStruct((cells, chans), BF16))
@@ -302,7 +311,8 @@
             for k in range(replicas)
         ]
     else:
-        outs.append(jax.ShapeDtypeStruct((2, chans, rows), F32))
+        outs.append(jax.ShapeDtypeStruct((cells, chans), BF16))
+        outs += [jax.ShapeDtypeStruct((TAPS, frames, tall, wid, chans), BF16)] * 2
     if opening:
         args = [in_hbm(incoming), in_hbm(weights)]
         specs = [HBM_SPEC] * 2
@@ -310,7 +320,7 @@
         outs.append(jax.ShapeDtypeStruct(weights.shape[1:], BF16))
         scratch.append(pltpu.SemaphoreType.DMA((7,)))
     else:
-        args = [weights, acc]
+        args = [weights] + ([acc] if last else [])
         args += [whole] if slot <= per else []
         args += [near] if slot >= per else []
         args += [over] if slot > per else []
@@ -321,6 +331,9 @@
             scratch += [pads(frames, hgt, wid, chans, (4,)), pltpu.SemaphoreType.DMA]
         if last:
             scratch.append(pltpu.VMEM((2, rows, chans), F32))
+            scratch += [pads(frames, tall, wid, chans, (TAPS,))] * 2
+            full = scratch.pop(-3)
+            scratch.append(full)
     return pl.pallas_call(
         functools.partial(frame_kernel, slot),
         out_shape=outs,
@@ -329,7 +342,45 @@
         scratch_shapes=scratch,
         compiler_params=pltpu.CompilerParams(vmem_limit_bytes=GRANT),
         cost_estimate=pl.CostEstimate(
-            flops=12 * cells * rows * chans, bytes_accessed=10 * cells * chans * 2, transcendentals=0
+            flops=8 * cells * rows * chans, bytes_accessed=10 * cells * chans * 2, transcendentals=0
+        ),
+    )(*args)
+
+
+def grads_kernel(begin, *refs):
+    out_ref, ys_ref, zpads, zpads2 = refs[:4]
+    sum_ref = refs[-1]
+    late, _, _ = places()
+
+    def work():
+        sum_f = grad_of(out_ref[1].reshape(ys_ref.shape), zpads2)
+        sum_g = grad_of(ys_ref[...], zpads)
+        sum_ref[0] = sum_f if begin else refs[4][0] + sum_f
+        sum_ref[1] = sum_g if begin else refs[4][1] + sum_g
+
+    if not begin:
+        work()
+        return
+
+    @pl.when(late)
+    def _():
+        sum_ref[...] = jnp.zeros_like(sum_ref)
+
+    pl.when(jnp.logical_not(late))(work)
+
+
+def grads_step(got, acc, rows):
+    begin = acc is None
+    cells, chans = got[1].shape
+    args = list(got[:4]) + ([] if begin else [acc])
+    return pl.pallas_call(
+        functools.partial(grads_kernel, begin),
+        out_shape=jax.ShapeDtypeStruct((2, chans, rows), F32),
+        in_specs=[VMEM_SPEC] * len(args),
+        out_specs=VMEM_SPEC,
+        compiler_params=pltpu.CompilerParams(vmem_limit_bytes=GRANT),
+        cost_estimate=pl.CostEstimate(
+            flops=4 * cells * rows * chans, bytes_accessed=4 * rows * chans * 4, transcendentals=0
         ),
     )(*args)
 
@@ -400,13 +451,14 @@
         over = overs[slot - per - 1] if slot > per else None
         got = frame_step(slot, incoming, fresh, wts, acc, whole, near, over)
         outs.append(got[0])
-        acc = got[1]
         if slot == 0:
-            whole, wts = got[2:]
+            whole, wts = got[4:]
         if slot <= per * (TICKS - 1):
             near, over = passed_along(got[0], slot)
             nears.append(near)
             overs.append(over)
+        if slot < TICKS * per:
+            acc = grads_step(got, acc, weights.shape[2])
     kept, *pieces = got[1:]
     terms = [pieces[0]] + [
         lax.ppermute(pieces[k], "dp", [(d, d ^ k) for d in range(replicas)]) for k in ORDER

time: 73.1 us -> 76 us (1.040)
  waiting for transfers between devices: 6.06 us -> 10.6 us
  Pallas kernels: 23 us -> 19.8 us
  starting transfers between devices: 41.9 us -> 43.4 us
    pallas_call x9, Pallas kernels: 21.2 us -> 13.5 us  [frame_step(): pl.pallas_call(functools.partial(frame_kernel, slot), out_shape=outs, in_...]
    pallas_call x0 -> x8, Pallas kernels: none -> 4.57 us  [grads_step(): pl.pallas_call(functools.partial(grads_kernel, begin), out_shape=jax.Shap...]
    ppermute x6, waiting for transfers between devices: 2.24 us -> 6.04 us  [passed_along(): over = lax.ppermute(value, ('segment', 'dp'), pairs([half], slot // per))]
    ppermute x6, starting transfers between devices: 21.2 us -> 22.3 us  [passed_along(): over = lax.ppermute(value, ('segment', 'dp'), pairs([half], slot // per))]
  transfers between devices with their start and end apart: 20 -> 20, of which waited for: 6 -> 6; matrix products, arithmetic and copies ran while one was open for 0% -> 0% of each run, Pallas kernels for 25% -> 21%
where the time goes in v4:
time: 76 us; the launch traced here: 74.7 us
  starting transfers between devices  43.4 us (57%)
  Pallas kernels  19.8 us (26%)
  waiting for transfers between devices  10.6 us (14%)
  between operations  0.93 us (1%)
    ppermute x6, starting transfers between devices, passed_along(): over = lax.ppermute(value, ('segment', 'dp'), pairs([half], slot // per))  22.3 us
    pallas_call x9, Pallas kernels, frame_step(): pl.pallas_call(functools.partial(frame_kernel, slot), out_shape=outs, in_...  13.5 us
    ppermute x7, starting transfers between devices, shards(): lax.ppermute(pieces[k], 'dp', [(d, d ^ k) for d in range(replicas)])  12.6 us
    ppermute x7, starting transfers between devices, passed_along(): return (lax.ppermute(value, ('segment', 'dp'), near), over)  8.45 us
    ppermute x6, waiting for transfers between devices, passed_along(): over = lax.ppermute(value, ('segment', 'dp'), pairs([half], slot // per))  6.04 us
    pallas_call x8, Pallas kernels, grads_step(): pl.pallas_call(functools.partial(grads_kernel, begin), out_shape=jax.Shap...  4.57 us
    ppermute x7, waiting for transfers between devices, shards(): lax.ppermute(pieces[k], 'dp', [(d, d ^ k) for d in range(replicas)])  2.93 us
    ppermute x7, waiting for transfers between devices, passed_along(): return (lax.ppermute(value, ('segment', 'dp'), near), over)  1.6 us
  transfers between devices with their start and end apart: 20, of which 6 were waited for; matrix products, arithmetic and copies ran while one was open for 0% of the time, Pallas kernels for 21%

profile of v4, /device:TPU:16, one launch (start us, length us, event | category | flops | bytes accessed | tf_op | source)
XLA Modules:
  0.0 74.7 jit_solution(10729765687125326728)
XLA Ops:
  0.6 3.0 %shard_map.59 = (bf16[4,2,16,16,128]{4,3,2,1,0:T(8,128)(2,1)S(1)}, bf16[512,128]{1,0:T(8,128)(2,1)S(1)}, bf16[3,2,18,16,128]{4,3,2,1,0:T(8,128)(2,1)S(1)}, bf16[...) custom-call(bf16[1,4,4,16,16,128]{5,4,3,2,1,0:T(8,128)(2,1)} %refs_0, ...), custom_call_target="tpu_custom_call" | custom-call | flops 603979776 | bytes 1310720 | tf_op jit(solution)/shard_map/pallas_call | solution.py:337
  3.7 1.3 %collective-permute-start = (bf16[4,2,16,16,128]{4,3,2,1,0:T(8,128)(2,1)S(1)}, bf16[4,2,16,16,128]{4,3,2,1,0:T(8,128)(2,1)S(1)}, u32[]{:S(2)}, u32[]{:S(2)}) collective-permute-start(bf16[4,2,16,16,128]{4,3,2,1,0:T(8,128)(2,1)S(1)} %get-tuple-element.48.refs_0_), channel_id=1, source_target_pairs={{136,132},{137,133},{138,134},{139,135},{140,128},{141,129},{142,1... | collective-permute-start | bytes 1572872 | tf_op jit(solution)/shard_map/ppermute | solution.py:39
  5.0 1.4 %shard_map.61 = (bf16[4,2,16,16,128]{4,3,2,1,0:T(8,128)(2,1)S(1)}, bf16[512,128]{1,0:T(8,128)(2,1)S(1)}, bf16[3,2,18,16,128]{4,3,2,1,0:T(8,128)(2,1)S(1)}, bf16[3,2,18,16,128]{4,3,2,1,0:T(8,128)(2,1)S(1)}) custom-call(bf16[2,1152,128]{2,1,0:T(8,128)(2,1)S(1)} %get-tuple-element.46.refs_0_.w_ref, bf16[4,4,16,16,128]{4,3,2,1,0:T(8,128)(2,1)S(1)} %get-tuple-element.47.refs_1_), custom_call_target="tpu_custom_call" | custom-call | flops 603979776 | bytes 1310720 | tf_op jit(solution)/shard_map/pallas_call | solution.py:337
  6.4 1.3 %collective-permute-start.4 = (bf16[4,2,16,16,128]{4,3,2,1,0:T(8,128)(2,1)S(1)}, bf16[4,2,16,16,128]{4,3,2,1,0:T(8,128)(2,1)S(1)}, u32[]{:S(2)}, u32[]{:S(2)}) collective-permute-start(bf16[4,2,16,16,128]{4,3,2,1,0:T(8,128)(2,1)S(1)} %get-tuple-element.50.refs_0_), channel_id=1, source_target_pairs={{136,132},{137,133},{138,134},{139,135},{140,128},{141,129},{142,1... | collective-permute-start | bytes 1572872 | tf_op jit(solution)/shard_map/ppermute | solution.py:39
  7.7 6.4 %collective-permute-start.5 = (bf16[4,2,16,16,128]{4,3,2,1,0:T(8,128)(2,1)S(1)}, bf16[4,2,16,16,128]{4,3,2,1,0:T(8,128)(2,1)S(1)}, u32[]{:S(2)}, u32[]{:S(2)}) collective-permute-start(bf16[4,2,16,16,128]{4,3,2,1,0:T(8,128)(2,1)S(1)} %get-tuple-element.48.refs_0_), channel_id=1, source_target_pairs={{128,124},{129,125},{130,126},{131,127},{132,120},{133,121},{134,1... | collective-permute-start | bytes 1572872 | tf_op jit(solution)/shard_map/ppermute | solution.py:36
  14.1 1.3 %collective-permute-start.2 = (bf16[4,2,16,16,128]{4,3,2,1,0:T(8,128)(2,1)S(1)}, bf16[4,2,16,16,128]{4,3,2,1,0:T(8,128)(2,1)S(1)}, u32[]{:S(2)}, u32[]{:S(2)}) collective-permute-start(bf16[4,2,16,16,128]{4,3,2,1,0:T(8,128)(2,1)S(1)} %get-tuple-element.50.refs_0_), channel_id=1, source_target_pairs={{128,124},{129,125},{130,126},{131,127},{132,120},{133,121},{134,1... | collective-permute-start | bytes 1572872 | tf_op jit(solution)/shard_map/ppermute | solution.py:36
  15.4 1.5 %shard_map.60 = (bf16[4,2,16,16,128]{4,3,2,1,0:T(8,128)(2,1)S(1)}, bf16[512,128]{1,0:T(8,128)(2,1)S(1)}, bf16[3,2,18,16,128]{4,3,2,1,0:T(8,128)(2,1)S(1)}, bf16[3,2,18,16,128]{4,3,2,1,0:T(8,128)(2,1)S(1)}) custom-call(bf16[2,1152,128]{2,1,0:T(8,128)(2,1)S(1)} %get-tuple-element.46.refs_0_.w_ref, bf16[4,4,16,16,128]{4,3,2,1,0:T(8,128)(2,1)S(1)} %get-tuple-element.47.refs_1_, ...), custom_call_target="tpu_custom_call" | custom-call | flops 603979776 | bytes 1310720 | tf_op jit(solution)/shard_map/pallas_call | solution.py:337
  16.9 1.3 %collective-permute-start.1 = (bf16[4,2,16,16,128]{4,3,2,1,0:T(8,128)(2,1)S(1)}, bf16[4,2,16,16,128]{4,3,2,1,0:T(8,128)(2,1)S(1)}, u32[]{:S(2)}, u32[]{:S(2)}) collective-permute-start(bf16[4,2,16,16,128]{4,3,2,1,0:T(8,128)(2,1)S(1)} %get-tuple-element.49.refs_0_), channel_id=1, source_target_pairs={{136,132},{137,133},{138,134},{139,135},{140,128},{141,129},{142,1... | collective-permute-start | bytes 1572872 | tf_op jit(solution)/shard_map/ppermute | solution.py:39
  18.2 1.6 %collective-permute-done.4.refs_1_ = bf16[4,2,16,16,128]{4,3,2,1,0:T(8,128)(2,1)S(1)} collective-permute-done((bf16[4,2,16,16,128]{4,3,2,1,0:T(8,128)(2,1)S(1)}, bf16[4,2,16,16,128]{4,3,2,1,0:T(8,128)(2,1)S(1)}, u32[]{:S(2)}, u32[]{:S(2)}) %collective-permute-start.4) | collective-permute-done | bytes 524320 | tf_op jit(solution)/shard_map/ppermute | solution.py:39
  20.7 1.5 %shard_map.63 = (bf16[4,2,16,16,128]{4,3,2,1,0:T(8,128)(2,1)S(1)}, bf16[512,128]{1,0:T(8,128)(2,1)S(1)}, bf16[3,2,18,16,128]{4,3,2,1,0:T(8,128)(2,1)S(1)}, bf16[3,2,18,16,128]{4,3,2,1,0:T(8,128)(2,1)S(1)}) custom-call(bf16[2,1152,128]{2,1,0:T(8,128)(2,1)S(1)} %get-tuple-element.46.refs_0_.w_ref, ...), custom_call_target="tpu_custom_call" | custom-call | flops 603979776 | bytes 1310720 | tf_op jit(solution)/shard_map/pallas_call | solution.py:337
  23.5 6.0 %collective-permute-start.8 = (bf16[4,2,16,16,128]{4,3,2,1,0:T(8,128)(2,1)S(1)}, bf16[4,2,16,16,128]{4,3,2,1,0:T(8,128)(2,1)S(1)}, u32[]{:S(2)}, u32[]{:S(2)}) collective-permute-start(bf16[4,2,16,16,128]{4,3,2,1,0:T(8,128)(2,1)S(1)} %get-tuple-element.49.refs_0_), channel_id=1, source_target_pairs={{128,124},{129,125},{130,126},{131,127},{132,120},{133,121},{134,1... | collective-permute-start | bytes 1572872 | tf_op jit(solution)/shard_map/ppermute | solution.py:36
  29.5 1.3 %collective-permute-start.6 = (bf16[4,2,16,16,128]{4,3,2,1,0:T(8,128)(2,1)S(1)}, bf16[4,2,16,16,128]{4,3,2,1,0:T(8,128)(2,1)S(1)}, u32[]{:S(2)}, u32[]{:S(2)}) collective-permute-start(bf16[4,2,16,16,128]{4,3,2,1,0:T(8,128)(2,1)S(1)} %get-tuple-element.52.refs_0_), channel_id=1, source_target_pairs={{128,124},{129,125},{130,126},{131,127},{132,120},{133,121},{134,1... | collective-permute-start | bytes 1572872 | tf_op jit(solution)/shard_map/ppermute | solution.py:36
  30.8 1.5 %shard_map.62 = (bf16[4,2,16,16,128]{4,3,2,1,0:T(8,128)(2,1)S(1)}, bf16[512,128]{1,0:T(8,128)(2,1)S(1)}, bf16[3,2,18,16,128]{4,3,2,1,0:T(8,128)(2,1)S(1)}, bf16[3,2,18,16,128]{4,3,2,1,0:T(8,128)(2,1)S(1)}) custom-call(bf16[2,1152,128]{2,1,0:T(8,128)(2,1)S(1)} %get-tuple-element.46.refs_0_.w_ref, ...), custom_call_target="tpu_custom_call" | custom-call | flops 603979776 | bytes 1310720 | tf_op jit(solution)/shard_map/pallas_call | solution.py:337
  33.6 2.5 %collective-permute-done.8.refs_2_ = bf16[4,2,16,16,128]{4,3,2,1,0:T(8,128)(2,1)S(1)} collective-permute-done((bf16[4,2,16,16,128]{4,3,2,1,0:T(8,128)(2,1)S(1)}, bf16[4,2,16,16,128]{4,3,2,1,0:T(8,128)(2,1)S(1)}, u32[]{:S(2)}, u32[]{:S(2)}) %collective-permute-start.8) | collective-permute-done | bytes 524320 | tf_op jit(solution)/shard_map/ppermute | solution.py:36
  36.1 1.5 %shard_map.65 = (bf16[4,2,16,16,128]{4,3,2,1,0:T(8,128)(2,1)S(1)}, bf16[512,128]{1,0:T(8,128)(2,1)S(1)}, bf16[3,2,18,16,128]{4,3,2,1,0:T(8,128)(2,1)S(1)}, bf16[3,2,18,16,128]{4,3,2,1,0:T(8,128)(2,1)S(1)}) custom-call(bf16[2,1152,128]{2,1,0:T(8,128)(2,1)S(1)} %get-tuple-element.46.refs_0_.w_ref, ...), custom_call_target="tpu_custom_call" | custom-call | flops 603979776 | bytes 1310720 | tf_op jit(solution)/shard_map/pallas_call | solution.py:337
  38.9 6.0 %collective-permute-start.10 = (bf16[4,2,16,16,128]{4,3,2,1,0:T(8,128)(2,1)S(1)}, bf16[4,2,16,16,128]{4,3,2,1,0:T(8,128)(2,1)S(1)}, u32[]{:S(2)}, u32[]{:S(2)}) collective-permute-start(bf16[4,2,16,16,128]{4,3,2,1,0:T(8,128)(2,1)S(1)} %get-tuple-element.51.refs_0_), channel_id=1, source_target_pairs={{128,124},{129,125},{130,126},{131,127},{132,120},{133,121},{134,1... | collective-permute-start | bytes 1572872 | tf_op jit(solution)/shard_map/ppermute | solution.py:36
  44.9 1.3 %collective-permute-start.12 = (bf16[4,2,16,16,128]{4,3,2,1,0:T(8,128)(2,1)S(1)}, bf16[4,2,16,16,128]{4,3,2,1,0:T(8,128)(2,1)S(1)}, u32[]{:S(2)}, u32[]{:S(2)}) collective-permute-start(bf16[4,2,16,16,128]{4,3,2,1,0:T(8,128)(2,1)S(1)} %get-tuple-element.54.refs_0_), channel_id=1, source_target_pairs={{128,124},{129,125},{130,126},{131,127},{132,120},{133,121},{134,1... | collective-permute-start | bytes 1572872 | tf_op jit(solution)/shard_map/ppermute | solution.py:36
  46.3 1.5 %shard_map.64 = (bf16[4,2,16,16,128]{4,3,2,1,0:T(8,128)(2,1)S(1)}, bf16[512,128]{1,0:T(8,128)(2,1)S(1)}, bf16[3,2,18,16,128]{4,3,2,1,0:T(8,128)(2,1)S(1)}, bf16[3,2,18,16,128]{4,3,2,1,0:T(8,128)(2,1)S(1)}) custom-call(bf16[2,1152,128]{2,1,0:T(8,128)(2,1)S(1)} %get-tuple-element.46.refs_0_.w_ref, ...), custom_call_target="tpu_custom_call" | custom-call | flops 603979776 | bytes 1310720 | tf_op jit(solution)/shard_map/pallas_call | solution.py:337
  52.5 1.5 %shard_map.66 = (bf16[4,2,16,16,128]{4,3,2,1,0:T(8,128)(2,1)S(1)}, bf16[512,128]{1,0:T(8,128)(2,1)S(1)}, bf16[3,2,18,16,128]{4,3,2,1,0:T(8,128)(2,1)S(1)}, bf16[3,2,18,16,128]{4,3,2,1,0:T(8,128)(2,1)S(1)}) custom-call(bf16[2,1152,128]{2,1,0:T(8,128)(2,1)S(1)} %get-tuple-element.46.refs_0_.w_ref, ...), custom_call_target="tpu_custom_call" | custom-call | flops 603979776 | bytes 1310720 | tf_op jit(solution)/shard_map/pallas_call | solution.py:337
  54.6 2.6 %collective-permute-done.12.refs_3_ = bf16[4,2,16,16,128]{4,3,2,1,0:T(8,128)(2,1)S(1)} collective-permute-done((bf16[4,2,16,16,128]{4,3,2,1,0:T(8,128)(2,1)S(1)}, bf16[4,2,16,16,128]{4,3,2,1,0:T(8,128)(2,1)S(1)}, u32[]{:S(2)}, u32[]{:S(2)}) %collective-permute-start.12) | collective-permute-done | bytes 524320 | tf_op jit(solution)/shard_map/ppermute | solution.py:36
  57.3 6.0 %collective-permute-start.13 = (bf16[2,144,128]{2,1,0:T(8,128)(2,1)S(1)}, bf16[2,144,128]{2,1,0:T(8,128)(2,1)S(1)}, u32[]{:S(2)}, u32[]{:S(2)}) collective-permute-start(bf16[2,144,128]{2,1,0:T(8,128)(2,1)S(1)} %get-tuple-element.83), channel_id=1, source_target_pairs={{0,6},{1,7},{2,4},{3,5},{4,2},{5,3},{6,0},{7,1},{8,14},{9,15},{10,... | collective-permute-start | bytes 221192 | tf_op jit(solution)/shard_map/ppermute | solution.py:464
  63.3 2.0 %collective-permute-start.15 = (bf16[2,144,128]{2,1,0:T(8,128)(2,1)S(1)}, bf16[2,144,128]{2,1,0:T(8,128)(2,1)S(1)}, u32[]{:S(2)}, u32[]{:S(2)}) collective-permute-start(bf16[2,144,128]{2,1,0:T(8,128)(2,1)S(1)} %get-tuple-element.85), channel_id=1, source_target_pairs={{0,7},{1,6},{2,5},{3,4},{4,3},{5,2},{6,1},{7,0},{8,15},{9,14},{10,... | collective-permute-start | bytes 221192 | tf_op jit(solution)/shard_map/ppermute | solution.py:464
  65.9 2.4 %collective-permute-start.17 = (bf16[2,144,128]{2,1,0:T(8,128)(2,1)S(1)}, bf16[2,144,128]{2,1,0:T(8,128)(2,1)S(1)}, u32[]{:S(2)}, u32[]{:S(2)}) collective-permute-start(bf16[2,144,128]{2,1,0:T(8,128)(2,1)S(1)} %get-tuple-element.87), channel_id=1, source_target_pairs={{0,2},{1,3},{2,0},{3,1},{4,6},{5,7},{6,4},{7,5},{8,10},{9,11},{10,... | collective-permute-start | bytes 221192 | tf_op jit(solution)/shard_map/ppermute | solution.py:464
  71.8 2.1 %collective-permute-done.18.refs_6_ = bf16[2,144,128]{2,1,0:T(8,128)(2,1)S(1)} collective-permute-done((bf16[2,144,128]{2,1,0:T(8,128)(2,1)S(1)}, bf16[2,144,128]{2,1,0:T(8,128)(2,1)S(1)}, u32[]{:S(2)}, u32[]{:S(2)}) %collective-permute-start.18) | collective-permute-done | bytes 73760 | tf_op jit(solution)/shard_map/ppermute | solution.py:464
  (37 shorter events, 15.1 us)
Async XLA Ops:
  3.7 11.7 %collective-permute-start = (bf16[4,2,16,16,128]{4,3,2,1,0:T(8,128)(2,1)S(1)}, bf16[4,2,16,16,128]{4,3,2,1,0:T(8,128)(2,1)S(1)}, u32[]{:S(2)}, u32[]{:S(2)}) collective-permute-start(bf16[4,2,16,16,128]{4,3,2,1,0:T(8,128)(2,1)S(1)} %get-tuple-element.48.refs_0_), channel_id=1, source_target_pairs={{136,132},{137,133},{138,134},{139,135},{140,128},{141,129},{142,1... | collective-permute-start | bytes 1572872 | tf_op jit(solution)/shard_map/ppermute | solution.py:39
  6.4 13.4 %collective-permute-start.4 = (bf16[4,2,16,16,128]{4,3,2,1,0:T(8,128)(2,1)S(1)}, bf16[4,2,16,16,128]{4,3,2,1,0:T(8,128)(2,1)S(1)}, u32[]{:S(2)}, u32[]{:S(2)}) collective-permute-start(bf16[4,2,16,16,128]{4,3,2,1,0:T(8,128)(2,1)S(1)} %get-tuple-element.50.refs_0_), channel_id=1, source_target_pairs={{136,132},{137,133},{138,134},{139,135},{140,128},{141,129},{142,1... | collective-permute-start | bytes 1572872 | tf_op jit(solution)/shard_map/ppermute | solution.py:39
  7.7 13.0 %collective-permute-start.5 = (bf16[4,2,16,16,128]{4,3,2,1,0:T(8,128)(2,1)S(1)}, bf16[4,2,16,16,128]{4,3,2,1,0:T(8,128)(2,1)S(1)}, u32[]{:S(2)}, u32[]{:S(2)}) collective-permute-start(bf16[4,2,16,16,128]{4,3,2,1,0:T(8,128)(2,1)S(1)} %get-tuple-element.48.refs_0_), channel_id=1, source_target_pairs={{128,124},{129,125},{130,126},{131,127},{132,120},{133,121},{134,1... | collective-permute-start | bytes 1572872 | tf_op jit(solution)/shard_map/ppermute | solution.py:36
  14.1 16.7 %collective-permute-start.2 = (bf16[4,2,16,16,128]{4,3,2,1,0:T(8,128)(2,1)S(1)}, bf16[4,2,16,16,128]{4,3,2,1,0:T(8,128)(2,1)S(1)}, u32[]{:S(2)}, u32[]{:S(2)}) collective-permute-start(bf16[4,2,16,16,128]{4,3,2,1,0:T(8,128)(2,1)S(1)} %get-tuple-element.50.refs_0_), channel_id=1, source_target_pairs={{128,124},{129,125},{130,126},{131,127},{132,120},{133,121},{134,1... | collective-permute-start | bytes 1572872 | tf_op jit(solution)/shard_map/ppermute | solution.py:36
  16.9 13.9 %collective-permute-start.1 = (bf16[4,2,16,16,128]{4,3,2,1,0:T(8,128)(2,1)S(1)}, bf16[4,2,16,16,128]{4,3,2,1,0:T(8,128)(2,1)S(1)}, u32[]{:S(2)}, u32[]{:S(2)}) collective-permute-start(bf16[4,2,16,16,128]{4,3,2,1,0:T(8,128)(2,1)S(1)} %get-tuple-element.49.refs_0_), channel_id=1, source_target_pairs={{136,132},{137,133},{138,134},{139,135},{140,128},{141,129},{142,1... | collective-permute-start | bytes 1572872 | tf_op jit(solution)/shard_map/ppermute | solution.py:39
  22.2 11.4 %collective-permute-start.7 = (bf16[4,2,16,16,128]{4,3,2,1,0:T(8,128)(2,1)S(1)}, bf16[4,2,16,16,128]{4,3,2,1,0:T(8,128)(2,1)S(1)}, u32[]{:S(2)}, u32[]{:S(2)}) collective-permute-start(bf16[4,2,16,16,128]{4,3,2,1,0:T(8,128)(2,1)S(1)} %get-tuple-element.52.refs_0_), channel_id=1, source_target_pairs={{136,132},{137,133},{138,134},{139,135},{140,128},{141,129},{142,1... | collective-permute-start | bytes 1572872 | tf_op jit(solution)/shard_map/ppermute | solution.py:39
  23.5 12.6 %collective-permute-start.8 = (bf16[4,2,16,16,128]{4,3,2,1,0:T(8,128)(2,1)S(1)}, bf16[4,2,16,16,128]{4,3,2,1,0:T(8,128)(2,1)S(1)}, u32[]{:S(2)}, u32[]{:S(2)}) collective-permute-start(bf16[4,2,16,16,128]{4,3,2,1,0:T(8,128)(2,1)S(1)} %get-tuple-element.49.refs_0_), channel_id=1, source_target_pairs={{128,124},{129,125},{130,126},{131,127},{132,120},{133,121},{134,1... | collective-permute-start | bytes 1572872 | tf_op jit(solution)/shard_map/ppermute | solution.py:36
  29.5 16.8 %collective-permute-start.6 = (bf16[4,2,16,16,128]{4,3,2,1,0:T(8,128)(2,1)S(1)}, bf16[4,2,16,16,128]{4,3,2,1,0:T(8,128)(2,1)S(1)}, u32[]{:S(2)}, u32[]{:S(2)}) collective-permute-start(bf16[4,2,16,16,128]{4,3,2,1,0:T(8,128)(2,1)S(1)} %get-tuple-element.52.refs_0_), channel_id=1, source_target_pairs={{128,124},{129,125},{130,126},{131,127},{132,120},{133,121},{134,1... | collective-permute-start | bytes 1572872 | tf_op jit(solution)/shard_map/ppermute | solution.py:36
  32.3 13.9 %collective-permute-start.3 = (bf16[4,2,16,16,128]{4,3,2,1,0:T(8,128)(2,1)S(1)}, bf16[4,2,16,16,128]{4,3,2,1,0:T(8,128)(2,1)S(1)}, u32[]{:S(2)}, u32[]{:S(2)}) collective-permute-start(bf16[4,2,16,16,128]{4,3,2,1,0:T(8,128)(2,1)S(1)} %get-tuple-element.51.refs_0_), channel_id=1, source_target_pairs={{136,128},{137,129},{138,130},{139,131},{140,132},{141,133},{142,1... | collective-permute-start | bytes 1572872 | tf_op jit(solution)/shard_map/ppermute | solution.py:39
  37.6 14.9 %collective-permute-start.9 = (bf16[4,2,16,16,128]{4,3,2,1,0:T(8,128)(2,1)S(1)}, bf16[4,2,16,16,128]{4,3,2,1,0:T(8,128)(2,1)S(1)}, u32[]{:S(2)}, u32[]{:S(2)}) collective-permute-start(bf16[4,2,16,16,128]{4,3,2,1,0:T(8,128)(2,1)S(1)} %get-tuple-element.54.refs_0_), channel_id=1, source_target_pairs={{136,128},{137,129},{138,130},{139,131},{140,132},{141,133},{142,1... | collective-permute-start | bytes 1572872 | tf_op jit(solution)/shard_map/ppermute | solution.py:39
  38.9 13.6 %collective-permute-start.10 = (bf16[4,2,16,16,128]{4,3,2,1,0:T(8,128)(2,1)S(1)}, bf16[4,2,16,16,128]{4,3,2,1,0:T(8,128)(2,1)S(1)}, u32[]{:S(2)}, u32[]{:S(2)}) collective-permute-start(bf16[4,2,16,16,128]{4,3,2,1,0:T(8,128)(2,1)S(1)} %get-tuple-element.51.refs_0_), channel_id=1, source_target_pairs={{128,124},{129,125},{130,126},{131,127},{132,120},{133,121},{134,1... | collective-permute-start | bytes 1572872 | tf_op jit(solution)/shard_map/ppermute | solution.py:36
  44.9 12.3 %collective-permute-start.12 = (bf16[4,2,16,16,128]{4,3,2,1,0:T(8,128)(2,1)S(1)}, bf16[4,2,16,16,128]{4,3,2,1,0:T(8,128)(2,1)S(1)}, u32[]{:S(2)}, u32[]{:S(2)}) collective-permute-start(bf16[4,2,16,16,128]{4,3,2,1,0:T(8,128)(2,1)S(1)} %get-tuple-element.54.refs_0_), channel_id=1, source_target_pairs={{128,124},{129,125},{130,126},{131,127},{132,120},{133,121},{134,1... | collective-permute-start | bytes 1572872 | tf_op jit(solution)/shard_map/ppermute | solution.py:36
  47.7 9.4 %collective-permute-start.11 = (bf16[4,2,16,16,128]{4,3,2,1,0:T(8,128)(2,1)S(1)}, bf16[4,2,16,16,128]{4,3,2,1,0:T(8,128)(2,1)S(1)}, u32[]{:S(2)}, u32[]{:S(2)}) collective-permute-start(bf16[4,2,16,16,128]{4,3,2,1,0:T(8,128)(2,1)S(1)} %get-tuple-element.53.refs_0_.early_ref), channel_id=1, source_target_pairs={{8,0},{9,1},{10,2},{11,3},{12,4},{13,5},{14,6},{15,7},{16,8},{17,9... | collective-permute-start | bytes 1572872 | tf_op jit(solution)/shard_map/ppermute | solution.py:39
  57.3 11.0 %collective-permute-start.13 = (bf16[2,144,128]{2,1,0:T(8,128)(2,1)S(1)}, bf16[2,144,128]{2,1,0:T(8,128)(2,1)S(1)}, u32[]{:S(2)}, u32[]{:S(2)}) collective-permute-start(bf16[2,144,128]{2,1,0:T(8,128)(2,1)S(1)} %get-tuple-element.83), channel_id=1, source_target_pairs={{0,6},{1,7},{2,4},{3,5},{4,2},{5,3},{6,0},{7,1},{8,14},{9,15},{10,... | collective-permute-start | bytes 221192 | tf_op jit(solution)/shard_map/ppermute | solution.py:464
  63.3 6.2 %collective-permute-start.14 = (bf16[2,144,128]{2,1,0:T(8,128)(2,1)S(1)}, bf16[2,144,128]{2,1,0:T(8,128)(2,1)S(1)}, u32[]{:S(2)}, u32[]{:S(2)}) collective-permute-start(bf16[2,144,128]{2,1,0:T(8,128)(2,1)S(1)} %get-tuple-element.84), channel_id=1, source_target_pairs={{0,5},{1,4},{2,7},{3,6},{4,1},{5,0},{6,3},{7,2},{8,13},{9,12},{10,... | collective-permute-start | bytes 221192 | tf_op jit(solution)/shard_map/ppermute | solution.py:464
  63.3 7.6 %collective-permute-start.15 = (bf16[2,144,128]{2,1,0:T(8,128)(2,1)S(1)}, bf16[2,144,128]{2,1,0:T(8,128)(2,1)S(1)}, u32[]{:S(2)}, u32[]{:S(2)}) collective-permute-start(bf16[2,144,128]{2,1,0:T(8,128)(2,1)S(1)} %get-tuple-element.85), channel_id=1, source_target_pairs={{0,7},{1,6},{2,5},{3,4},{4,3},{5,2},{6,1},{7,0},{8,15},{9,14},{10,... | collective-permute-start | bytes 221192 | tf_op jit(solution)/shard_map/ppermute | solution.py:464
  65.3 5.7 %collective-permute-start.16 = (bf16[2,144,128]{2,1,0:T(8,128)(2,1)S(1)}, bf16[2,144,128]{2,1,0:T(8,128)(2,1)S(1)}, u32[]{:S(2)}, u32[]{:S(2)}) collective-permute-start(bf16[2,144,128]{2,1,0:T(8,128)(2,1)S(1)} %get-tuple-element.86), channel_id=1, source_target_pairs={{0,4},{1,5},{2,6},{3,7},{4,0},{5,1},{6,2},{7,3},{8,12},{9,13},{10,... | collective-permute-start | bytes 221192 | tf_op jit(solution)/shard_map/ppermute | solution.py:464
  65.9 5.9 %collective-permute-start.17 = (bf16[2,144,128]{2,1,0:T(8,128)(2,1)S(1)}, bf16[2,144,128]{2,1,0:T(8,128)(2,1)S(1)}, u32[]{:S(2)}, u32[]{:S(2)}) collective-permute-start(bf16[2,144,128]{2,1,0:T(8,128)(2,1)S(1)} %get-tuple-element.87), channel_id=1, source_target_pairs={{0,2},{1,3},{2,0},{3,1},{4,6},{5,7},{6,4},{7,5},{8,10},{9,11},{10,... | collective-permute-start | bytes 221192 | tf_op jit(solution)/shard_map/ppermute | solution.py:464
  68.3 5.6 %collective-permute-start.18 = (bf16[2,144,128]{2,1,0:T(8,128)(2,1)S(1)}, bf16[2,144,128]{2,1,0:T(8,128)(2,1)S(1)}, u32[]{:S(2)}, u32[]{:S(2)}) collective-permute-start(bf16[2,144,128]{2,1,0:T(8,128)(2,1)S(1)} %get-tuple-element.88), channel_id=1, source_target_pairs={{0,3},{1,2},{2,1},{3,0},{4,7},{5,6},{6,5},{7,4},{8,11},{9,10},{10,... | collective-permute-start | bytes 221192 | tf_op jit(solution)/shard_map/ppermute | solution.py:464
  69.5 4.4 %collective-permute-start.19 = (bf16[2,144,128]{2,1,0:T(8,128)(2,1)S(1)}, bf16[2,144,128]{2,1,0:T(8,128)(2,1)S(1)}, u32[]{:S(2)}, u32[]{:S(2)}) collective-permute-start(bf16[2,144,128]{2,1,0:T(8,128)(2,1)S(1)} %get-tuple-element.89), channel_id=1, source_target_pairs={{0,1},{1,0},{2,3},{3,2},{4,5},{5,4},{6,7},{7,6},{8,9},{9,8},{10,11... | collective-permute-start | bytes 221192 | tf_op jit(solution)/shard_map/ppermute | solution.py:464
  70.0 3.9 %copy-start = (f32[1,2,144,128]{3,2,1,0:T(8,128)S(1)}, f32[1,2,144,128]{3,2,1,0:T(8,128)}, u32[]{:S(2)}) copy-start(f32[1,2,144,128]{3,2,1,0:T(8,128)} %mom_ref.1) | copy-start | bytes 442372
